TPU v7x, 768 devices: a whole 4x8x12 slice. The times are simulated.
768 devices in a mesh: wide: 96 (over z, x, core), grp: 8 (over y).
Axes of the slice: x: 4, y: 8, z: 12, core: 2. Of those that a mesh axis runs over, the one named last changes fastest.
Arguments:
- state: float32 [5, 125, 98304], P(None, None, ('wide', 'grp')), as said below
- metric: float32 [98304], P(('wide', 'grp')), may hold values from 1 to 4
- nbr_elem: int32 [6, 98304], P(None, ('wide', 'grp')), may hold values from 0 to 98303, as said below
- nbr_face: int32 [6, 98304], P(None, ('wide', 'grp')), may hold values from 0 to 5, as said below
- troubled: int32 [36864], P(('wide', 'grp')), may hold values from -1 to 127, as said below
- new_owner: int32 [98304], P(('wide', 'grp')), may hold values from 0 to 767, as said below
Outputs:
- migrated: float32 [5, 125, 147456], P(None, None, ('wide', 'grp'))
Inputs may be any that keep to these rules, and one draw needn't show every extreme that they name: Across face f of element e lies face nbr_face[f, e] of element nbr_elem[f, e], and that face lies across face f of element e again; a face never meets itself. The element across lies on the same device, or on another device of the same grp group, exactly 16 faces with each of them, or on a wide neighbour (same grp index, wide index minus or plus one, wrapping), exactly 32 faces with each of the two. `nbr_face`: see nbr_elem. `troubled`: each device's 48 entries list distinct local element indices first and -1 after them; every draw has devices whose list is full. `new_owner`: each element's new owner is its device or one of its two wide neighbours; at most 32 elements of a device go to each neighbour, and every draw has devices that send 32 to both. `state`: at every node density and pressure lie between 0.4 and 2.5 and each velocity component within -0.9 to 0.9.
All inputs are finite; a program needn't handle non-finite values.
Results may differ from a plain program's by a relative error of at most 0.0001.
Values sent between devices are 32-bit elements; how exact they have to be, the bound alone decides.
No kernel may reach another device: no remote copies, remote signals or barrier semaphores. Data moves between devices by JAX's collectives and lax.ppermute only.
A program may use at most 32 MiB of HBM per device.

v0:
```python
import math

import jax
import jax.numpy as jnp
import numpy as np
from jax import lax
from jax.sharding import PartitionSpec as P

GROUP_FACES = 16
WIDE_FACES = 32
MOVE_CAP = 32


SECTION_STEP = 0.01
LIFT_GAIN = 10.0


def from_behind(value, axis, steps):
    count = lax.axis_size(axis)
    pairs = [(source, (source + steps) % count) for source in range(count)]
    return lax.ppermute(value, axis, pairs)


def gll_tables():
    root = math.sqrt(3.0 / 7.0)
    points = np.array([-1.0, -root, 0.0, root, 1.0])
    weights = np.array([0.1, 49.0 / 90.0, 32.0 / 45.0, 49.0 / 90.0, 0.1])
    bary = np.array(
        [1.0 / np.prod([points[j] - points[k] for k in range(5) if k != j]) for j in range(5)]
    )
    deriv = np.zeros((5, 5))
    for i in range(5):
        for j in range(5):
            if i != j:
                deriv[i, j] = bary[j] / bary[i] / (points[i] - points[j])
        deriv[i, i] = -np.sum(deriv[i])
    ident = np.eye(5)
    diffs = [
        np.kron(np.kron(deriv, ident), ident),
        np.kron(np.kron(ident, deriv), ident),
        np.kron(np.kron(ident, ident), deriv),
    ]
    cell_weights = np.kron(np.kron(weights, weights), weights) / 8.0
    face_table = np.zeros((6, 25), np.int32)
    for a in range(5):
        for b in range(5):
            face_table[0, 5 * a + b] = 5 * a + b
            face_table[1, 5 * a + b] = 100 + 5 * a + b
            face_table[2, 5 * a + b] = 25 * a + b
            face_table[3, 5 * a + b] = 25 * a + 20 + b
            face_table[4, 5 * a + b] = 25 * a + 5 * b
            face_table[5, 5 * a + b] = 25 * a + 5 * b + 4
    return (diffs, cell_weights, face_table)


def pressure_of(u):
    density = u[0]
    return 0.4 * (u[4] - 0.5 * (u[1] * u[1] + u[2] * u[2] + u[3] * u[3]) / density)


def inviscid_flux(u, axis_label):
    density = u[0]
    velocity = u[1 + axis_label] / density
    pressure = pressure_of(u)
    rows = [
        u[1 + axis_label],
        u[1] * velocity,
        u[2] * velocity,
        u[3] * velocity,
        (u[4] + pressure) * velocity,
    ]
    rows[1 + axis_label] = rows[1 + axis_label] + pressure
    return jnp.stack(rows)


def signal_speed(u, axis_label):
    density = u[0]
    return jnp.abs(u[1 + axis_label] / density) + jnp.sqrt(1.4 * pressure_of(u) / density)


def section_update(state, metric, neighbour_traces):
    diffs, cell_weights, face_table = gll_tables()
    volume_term = jnp.zeros_like(state)
    for axis_label in range(3):
        operator_matrix = jnp.asarray(diffs[axis_label], state.dtype)
        volume_term = volume_term + jnp.einsum(
            "lk,bkr->blr",
            operator_matrix,
            inviscid_flux(state, axis_label),
            precision=lax.Precision.HIGHEST,
        )
    change = -metric[None, None, :] * volume_term
    for face in range(6):
        axis_label = face // 2
        sign_value = -1.0 if face % 2 == 0 else 1.0
        inner = state[:, face_table[face], :]
        outer = neighbour_traces[face]
        flux_in = sign_value * inviscid_flux(inner, axis_label)
        flux_out = sign_value * inviscid_flux(outer, axis_label)
        speed = jnp.maximum(signal_speed(inner, axis_label), signal_speed(outer, axis_label))
        common = 0.5 * (flux_in + flux_out) - 0.5 * speed[None] * (outer - inner)
        lift = (LIFT_GAIN * metric)[None, None, :] * (flux_in - common)
        change = change.at[:, face_table[face], :].add(lift)
    return state + SECTION_STEP * change


def cell_mean(values, cell_weights):
    return jnp.sum(values * cell_weights[None, :, None], axis=1)


def weno_combine(own, neighbours, cell_weights):
    own_mean = cell_mean(own, cell_weights)
    candidates = [(own, 0.4)]
    for other in neighbours:
        candidates.append(
            (other - cell_mean(other, cell_weights)[:, None, :] + own_mean[:, None, :], 0.1)
        )
    numer = jnp.zeros_like(own)
    denom = jnp.zeros_like(own_mean)
    for values, linear in candidates:
        spread = values - cell_mean(values, cell_weights)[:, None, :]
        smooth = jnp.sum(cell_weights[None, :, None] * spread * spread, axis=1)
        weight = linear / ((1e-06 + smooth) * (1e-06 + smooth))
        numer = numer + weight[:, None, :] * values
        denom = denom + weight
    return numer / denom[:, None, :]


def group_move(blocks, group_pos, group_size):
    arrived = jnp.zeros_like(blocks)
    for offset in range(1, group_size):
        outgoing = lax.dynamic_index_in_dim(
            blocks, (group_pos + offset) % group_size, 1, keepdims=True
        )
        incoming = from_behind(outgoing, "grp", offset)
        arrived = lax.dynamic_update_slice_in_dim(
            arrived, incoming, (group_pos - offset) % group_size, 1
        )
    return arrived


def wide_pair(to_left, to_right):
    results = []
    for offset, outgoing in ((1, to_right), (-1, to_left)):
        results.append(from_behind(outgoing, "wide", offset))
    from_left = results[0]
    from_right = results[1]
    return (from_left, from_right)


def shards(state, metric, nbr_elem, nbr_face, troubled, new_owner):
    diffs, cell_weights_np, face_table = gll_tables()
    cell_weights = jnp.asarray(cell_weights_np, state.dtype)
    elem_count = state.shape[2]
    slot_count = 6 * elem_count
    group_size = lax.axis_size("grp")
    wide_size = lax.axis_size("wide")
    group_pos = lax.axis_index("grp")
    wide_pos = lax.axis_index("wide")
    own_device = wide_pos * group_size + group_pos
    left_device = (wide_pos - 1) % wide_size * group_size + group_pos
    right_device = (wide_pos + 1) % wide_size * group_size + group_pos
    owner = (nbr_elem // elem_count).reshape(-1)
    partner_local = (nbr_elem % elem_count).reshape(-1)
    partner_slot = (nbr_face * elem_count).reshape(-1) + partner_local
    owner_wide = owner // group_size
    owner_group = owner % group_size
    category = jnp.where(
        owner == own_device,
        group_size + 2,
        jnp.where(
            owner_wide == wide_pos,
            owner_group,
            jnp.where(owner == left_device, group_size, group_size + 1),
        ),
    )
    own_slots = jnp.arange(slot_count, dtype=jnp.int32)
    send_order = jnp.argsort(category * slot_count + partner_slot, stable=True)
    recv_order = jnp.argsort(category * slot_count + own_slots, stable=True)
    group_total = (group_size - 1) * GROUP_FACES
    remote_total = group_total + 2 * WIDE_FACES
    block_ids = jnp.arange(group_size, dtype=jnp.int32)
    block_rows = jnp.minimum(block_ids - (block_ids > group_pos).astype(jnp.int32), group_size - 2)
    send_blocks = send_order[:group_total].reshape(group_size - 1, GROUP_FACES)[block_rows]
    left_send = send_order[group_total : group_total + WIDE_FACES]
    right_send = send_order[group_total + WIDE_FACES : remote_total]
    peer_ids = jnp.arange(group_size - 1, dtype=jnp.int32)
    arrived_rows = peer_ids + (peer_ids >= group_pos).astype(jnp.int32)
    remote_slots = recv_order[:remote_total]
    remote_range = jnp.arange(remote_total, dtype=jnp.int32)

    def carry_remote(source, blocks, to_left, to_right):
        grouped = group_move(source[:, blocks], group_pos, group_size)
        grouped = grouped[:, arrived_rows, :].reshape(source.shape[0], group_total)
        from_left, from_right = wide_pair(source[:, to_left], source[:, to_right])
        return jnp.concatenate([grouped, from_left, from_right], axis=1)

    traces = jnp.transpose(state[:, face_table, :], (0, 2, 1, 3)).reshape(125, slot_count)
    remote_traces = carry_remote(traces, send_blocks, left_send, right_send)
    trace_cols = partner_slot.at[remote_slots].set(slot_count + remote_range)
    neighbour_flat = jnp.concatenate([traces, remote_traces], axis=1)[:, trace_cols]
    neighbour = [
        neighbour_flat[:, face * elem_count : (face + 1) * elem_count].reshape(5, 25, elem_count)
        for face in range(6)
    ]
    sectioned = section_update(state, metric, neighbour)
    polys = sectioned.reshape(625, elem_count)
    remote_polys = carry_remote(
        polys, send_blocks % elem_count, left_send % elem_count, right_send % elem_count
    )
    poly_cols = partner_local.at[remote_slots].set(elem_count + remote_range)
    polynomial_donor = jnp.concatenate([polys, remote_polys], axis=1)
    valid = troubled >= 0
    cells = jnp.where(valid, troubled, 0)
    trouble_count = troubled.shape[0]
    own = sectioned[:, :, cells]
    neighbours = [
        polynomial_donor[:, poly_cols[face * elem_count + cells]].reshape(5, 125, trouble_count)
        for face in range(6)
    ]
    limited_cells = weno_combine(own, neighbours, cell_weights)
    limited = sectioned.at[:, :, jnp.where(valid, cells, elem_count)].set(
        limited_cells, mode="drop"
    )
    elem_ids = jnp.arange(elem_count, dtype=jnp.int32)
    stays = new_owner == own_device
    kept = jnp.where(stays[None, None, :], limited, 0.0)
    flat_state = limited.reshape(625, elem_count)

    def departures(leaving):
        order = jnp.argsort(jnp.where(leaving, elem_ids, elem_count + elem_ids), stable=True)[
            :MOVE_CAP
        ]
        filled = jnp.arange(MOVE_CAP, dtype=jnp.int32) < jnp.sum(leaving.astype(jnp.int32))
        return jnp.where(filled[None, :], flat_state[:, order], 0.0)

    from_left, from_right = wide_pair(
        departures(new_owner == left_device), departures(new_owner == right_device)
    )
    return jnp.concatenate(
        [kept, from_left.reshape(5, 125, MOVE_CAP), from_right.reshape(5, 125, MOVE_CAP)], axis=2
    )


def solution(mesh):
    placed = (
        P(None, None, ("wide", "grp")),
        P(("wide", "grp")),
        P(None, ("wide", "grp")),
        P(None, ("wide", "grp")),
        P(("wide", "grp")),
        P(("wide", "grp")),
    )
    return jax.shard_map(
        shards,
        mesh=mesh,
        in_specs=placed,
        out_specs=P(None, None, ("wide", "grp")),
        check_vma=False,
    )
```

profile of v0, /device:TPU:8, one launch (start us, length us, event | category | flops | bytes accessed | tf_op | source)
XLA Modules:
  0.0 174.1 jit_solution(7462620790918039141)
XLA Ops:
  1.5 4.4 %sort.62 = (s32[768]{0:T(1024)}, s32[768]{0:T(1024)S(1)}) sort(s32[768]{0:T(1024)S(1)} %get-tuple-element.57, s32[768]{0:T(1024)S(1)} %iota.55), dimensions={0}, to_apply=%region_0.1 | sort | flops 7680 | bytes 12288 | tf_op jit(solution)/shard_map/jit(argsort)/sort | solution.py:178
  10.2 3.5 %collective-permute-start = (f32[125,1,16]{0,2,1:T(8,128)S(1)}, f32[125,1,16]{0,2,1:T(8,128)S(1)}, u32[]{:S(2)}, u32[]{:S(2)}) collective-permute-start(f32[125,1,16]{0,2,1:T(8,128)S(1)} %get-tuple-element.123), channel_id=1, source_target_pairs={{0,1},{1,2},{2,3},{3,4},{4,5},{5,6},{6,7},{7,0},{8,9},{9,10},{10,1... | collective-permute-start | bytes 24008 | tf_op jit(solution)/shard_map/ppermute | solution.py:21
  13.7 5.7 %collective-permute-start.1 = (f32[125,1,16]{0,2,1:T(8,128)S(1)}, f32[125,1,16]{0,2,1:T(8,128)S(1)}, u32[]{:S(2)}, u32[]{:S(2)}) collective-permute-start(f32[125,1,16]{0,2,1:T(8,128)S(1)} %get-tuple-element.122), channel_id=1, source_target_pairs={{0,2},{1,3},{2,4},{3,5},{4,6},{5,7},{6,0},{7,1},{8,10},{9,11},{10,... | collective-permute-start | bytes 24008 | tf_op jit(solution)/shard_map/ppermute | solution.py:21
  19.4 2.8 %collective-permute-start.2 = (f32[125,1,16]{0,2,1:T(8,128)S(1)}, f32[125,1,16]{0,2,1:T(8,128)S(1)}, u32[]{:S(2)}, u32[]{:S(2)}) collective-permute-start(f32[125,1,16]{0,2,1:T(8,128)S(1)} %get-tuple-element.121), channel_id=1, source_target_pairs={{0,3},{1,4},{2,5},{3,6},{4,7},{5,0},{6,1},{7,2},{8,11},{9,12},{10,... | collective-permute-start | bytes 24008 | tf_op jit(solution)/shard_map/ppermute | solution.py:21
  22.2 10.1 %collective-permute-start.3 = (f32[125,1,16]{0,2,1:T(8,128)S(1)}, f32[125,1,16]{0,2,1:T(8,128)S(1)}, u32[]{:S(2)}, u32[]{:S(2)}) collective-permute-start(f32[125,1,16]{0,2,1:T(8,128)S(1)} %get-tuple-element.120), channel_id=1, source_target_pairs={{0,4},{1,5},{2,6},{3,7},{4,0},{5,1},{6,2},{7,3},{8,12},{9,13},{10,... | collective-permute-start | bytes 24008 | tf_op jit(solution)/shard_map/ppermute | solution.py:21
  32.3 6.9 %collective-permute-start.4 = (f32[125,1,16]{0,2,1:T(8,128)S(1)}, f32[125,1,16]{0,2,1:T(8,128)S(1)}, u32[]{:S(2)}, u32[]{:S(2)}) collective-permute-start(f32[125,1,16]{0,2,1:T(8,128)S(1)} %get-tuple-element.119), channel_id=1, source_target_pairs={{0,5},{1,6},{2,7},{3,0},{4,1},{5,2},{6,3},{7,4},{8,13},{9,14},{10,... | collective-permute-start | bytes 24008 | tf_op jit(solution)/shard_map/ppermute | solution.py:21
  39.4 4.4 %sort.63 = (s32[768]{0:T(1024)}, s32[768]{0:T(1024)S(1)}) sort(s32[768]{0:T(1024)S(1)} %get-tuple-element.55, s32[768]{0:T(1024)S(1)} %iota.61), dimensions={0}, to_apply=%region_1.2 | sort | flops 7680 | bytes 12288 | tf_op jit(solution)/shard_map/jit(argsort)/sort | solution.py:179
  59.9 2.5 %sort.65 = (s32[128]{0:T(128)}, s32[128]{0:T(128)S(1)}) sort(s32[128]{0:T(128)S(1)} %get-tuple-element.142, s32[128]{0:T(128)S(1)} %iota.70), dimensions={0}, to_apply=%region_34.35 | sort | flops 896 | bytes 2048 | tf_op jit(solution)/shard_map/jit(argsort)/sort | solution.py:231
  62.9 2.6 %sort.64 = (s32[128]{0:T(128)}, s32[128]{0:T(128)S(1)}) sort(s32[128]{0:T(128)S(1)} %get-tuple-element.141, s32[128]{0:T(128)S(1)} %iota.67), dimensions={0}, to_apply=%region_32.33 | sort | flops 896 | bytes 2048 | tf_op jit(solution)/shard_map/jit(argsort)/sort | solution.py:231
  70.2 1.9 %collective-permute-start.5 = (f32[125,1,16]{0,2,1:T(8,128)S(1)}, f32[125,1,16]{0,2,1:T(8,128)S(1)}, u32[]{:S(2)}, u32[]{:S(2)}) collective-permute-start(f32[125,1,16]{0,2,1:T(8,128)S(1)} %get-tuple-element.118), channel_id=1, source_target_pairs={{0,6},{1,7},{2,0},{3,1},{4,2},{5,3},{6,4},{7,5},{8,14},{9,15},{10,... | collective-permute-start | bytes 24008 | tf_op jit(solution)/shard_map/ppermute | solution.py:21
  72.1 2.5 %collective-permute-start.6 = (f32[125,1,16]{0,2,1:T(8,128)S(1)}, f32[125,1,16]{0,2,1:T(8,128)S(1)}, u32[]{:S(2)}, u32[]{:S(2)}) collective-permute-start(f32[125,1,16]{0,2,1:T(8,128)S(1)} %get-tuple-element.117), channel_id=1, source_target_pairs={{0,7},{1,0},{2,1},{3,2},{4,3},{5,4},{6,5},{7,6},{8,15},{9,8},{10,9... | collective-permute-start | bytes 24008 | tf_op jit(solution)/shard_map/ppermute | solution.py:21
  74.6 1.9 %collective-permute-start.7 = (f32[125,32]{0,1:T(8,128)S(1)}, f32[125,32]{0,1:T(8,128)S(1)}, u32[]{:S(2)}, u32[]{:S(2)}) collective-permute-start(f32[125,32]{0,1:T(8,128)S(1)} %bitcast.566), channel_id=1, source_target_pairs={{0,8},{8,16},{16,24},{24,32},{32,40},{40,48},{48,56},{56,64},{64,7... | collective-permute-start | bytes 48008 | tf_op jit(solution)/shard_map/ppermute | solution.py:21
  76.6 10.5 %collective-permute-start.8 = (f32[125,32]{0,1:T(8,128)S(1)}, f32[125,32]{0,1:T(8,128)S(1)}, u32[]{:S(2)}, u32[]{:S(2)}) collective-permute-start(f32[125,32]{0,1:T(8,128)S(1)} %bitcast.565), channel_id=1, source_target_pairs={{0,760},{8,0},{16,8},{24,16},{32,24},{40,32},{48,40},{56,48},{64,5... | collective-permute-start | bytes 48008 | tf_op jit(solution)/shard_map/ppermute | solution.py:21
  91.3 1.7 scatter_fusion.1
  93.0 1.7 scatter_fusion.2
  94.7 1.7 scatter_fusion.3
  96.4 1.7 scatter_fusion.4
  98.1 1.7 scatter_fusion.5
  99.8 1.7 scatter_fusion.6
  102.9 1.9 %collective-permute-start.9 = (f32[625,1,16]{0,2,1:T(8,128)S(1)}, f32[625,1,16]{0,2,1:T(8,128)S(1)}, u32[]{:S(2)}, u32[]{:S(2)}) collective-permute-start(f32[625,1,16]{0,2,1:T(8,128)S(1)} %get-tuple-element.103), channel_id=1, source_target_pairs={{0,1},{1,2},{2,3},{3,4},{4,5},{5,6},{6,7},{7,0},{8,9},{9,10},{10,1... | collective-permute-start | bytes 120008 | tf_op jit(solution)/shard_map/ppermute | solution.py:21
  105.9 4.1 %collective-permute-start.10 = (f32[625,1,16]{0,2,1:T(8,128)S(1)}, f32[625,1,16]{0,2,1:T(8,128)S(1)}, u32[]{:S(2)}, u32[]{:S(2)}) collective-permute-start(f32[625,1,16]{0,2,1:T(8,128)S(1)} %get-tuple-element.102), channel_id=1, source_target_pairs={{0,2},{1,3},{2,4},{3,5},{4,6},{5,7},{6,0},{7,1},{8,10},{9,11},{10,... | collective-permute-start | bytes 120008 | tf_op jit(solution)/shard_map/ppermute | solution.py:21
  110.0 3.7 %collective-permute-start.11 = (f32[625,1,16]{0,2,1:T(8,128)S(1)}, f32[625,1,16]{0,2,1:T(8,128)S(1)}, u32[]{:S(2)}, u32[]{:S(2)}) collective-permute-start(f32[625,1,16]{0,2,1:T(8,128)S(1)} %get-tuple-element.101), channel_id=1, source_target_pairs={{0,3},{1,4},{2,5},{3,6},{4,7},{5,0},{6,1},{7,2},{8,11},{9,12},{10,... | collective-permute-start | bytes 120008 | tf_op jit(solution)/shard_map/ppermute | solution.py:21
  113.7 4.4 %collective-permute-start.12 = (f32[625,1,16]{0,2,1:T(8,128)S(1)}, f32[625,1,16]{0,2,1:T(8,128)S(1)}, u32[]{:S(2)}, u32[]{:S(2)}) collective-permute-start(f32[625,1,16]{0,2,1:T(8,128)S(1)} %get-tuple-element.100), channel_id=1, source_target_pairs={{0,4},{1,5},{2,6},{3,7},{4,0},{5,1},{6,2},{7,3},{8,12},{9,13},{10,... | collective-permute-start | bytes 120008 | tf_op jit(solution)/shard_map/ppermute | solution.py:21
  118.1 6.8 %collective-permute-start.13 = (f32[625,1,16]{0,2,1:T(8,128)S(1)}, f32[625,1,16]{0,2,1:T(8,128)S(1)}, u32[]{:S(2)}, u32[]{:S(2)}) collective-permute-start(f32[625,1,16]{0,2,1:T(8,128)S(1)} %get-tuple-element.99), channel_id=1, source_target_pairs={{0,5},{1,6},{2,7},{3,0},{4,1},{5,2},{6,3},{7,4},{8,13},{9,14},{10,... | collective-permute-start | bytes 120008 | tf_op jit(solution)/shard_map/ppermute | solution.py:21
  126.2 1.9 %collective-permute-start.14 = (f32[625,1,16]{0,2,1:T(8,128)S(1)}, f32[625,1,16]{0,2,1:T(8,128)S(1)}, u32[]{:S(2)}, u32[]{:S(2)}) collective-permute-start(f32[625,1,16]{0,2,1:T(8,128)S(1)} %get-tuple-element.98), channel_id=1, source_target_pairs={{0,6},{1,7},{2,0},{3,1},{4,2},{5,3},{6,4},{7,5},{8,14},{9,15},{10,... | collective-permute-start | bytes 120008 | tf_op jit(solution)/shard_map/ppermute | solution.py:21
  128.2 2.8 %collective-permute-start.15 = (f32[625,1,16]{0,2,1:T(8,128)S(1)}, f32[625,1,16]{0,2,1:T(8,128)S(1)}, u32[]{:S(2)}, u32[]{:S(2)}) collective-permute-start(f32[625,1,16]{0,2,1:T(8,128)S(1)} %get-tuple-element.97), channel_id=1, source_target_pairs={{0,7},{1,0},{2,1},{3,2},{4,3},{5,4},{6,5},{7,6},{8,15},{9,8},{10,9... | collective-permute-start | bytes 120008 | tf_op jit(solution)/shard_map/ppermute | solution.py:21
  131.0 1.9 %collective-permute-start.16 = (f32[625,32]{0,1:T(8,128)S(1)}, f32[625,32]{0,1:T(8,128)S(1)}, u32[]{:S(2)}, u32[]{:S(2)}) collective-permute-start(f32[625,32]{0,1:T(8,128)S(1)} %bitcast.564), channel_id=1, source_target_pairs={{0,8},{8,16},{16,24},{24,32},{32,40},{40,48},{48,56},{56,64},{64,7... | collective-permute-start | bytes 240008 | tf_op jit(solution)/shard_map/ppermute | solution.py:21
  133.0 7.0 %collective-permute-start.17 = (f32[625,32]{0,1:T(8,128)S(1)}, f32[625,32]{0,1:T(8,128)S(1)}, u32[]{:S(2)}, u32[]{:S(2)}) collective-permute-start(f32[625,32]{0,1:T(8,128)S(1)} %bitcast.563), channel_id=1, source_target_pairs={{0,760},{8,0},{16,8},{24,16},{32,24},{40,32},{48,40},{56,48},{64,5... | collective-permute-start | bytes 240008 | tf_op jit(solution)/shard_map/ppermute | solution.py:21
  158.5 2.0 %scatter_fusion.8 = f32[5,125,128]{1,0,2:T(8,128)S(1)} fusion(f32[5,125,128]{1,0,2:T(8,128)S(1)} %copy.160, s32[48]{0:T(128)S(1)} %get-tuple-element.152, f32[48,5,125]{2,1,0:T(8,128)S(1)} %fusion.54), kind=kCustom, calls=%fused_computation.40 | custom fusion | bytes 360192 | tf_op jit(solution)/shard_map/scatter | solution.py:222
  161.3 1.9 %collective-permute-start.18 = (f32[625,32]{0,1:T(8,128)S(1)}, f32[625,32]{0,1:T(8,128)S(1)}, u32[]{:S(2)}, u32[]{:S(2)}) collective-permute-start(f32[625,32]{0,1:T(8,128)S(1)} %select_bitcast_fusion.1), channel_id=1, source_target_pairs={{0,8},{8,16},{16,24},{24,32},{32,40},{40,48},{48,56},{56,64},{64,7... | collective-permute-start | bytes 240008 | tf_op jit(solution)/shard_map/ppermute | solution.py:21
  163.9 7.1 %collective-permute-start.19 = (f32[625,32]{0,1:T(8,128)S(1)}, f32[625,32]{0,1:T(8,128)S(1)}, u32[]{:S(2)}, u32[]{:S(2)}) collective-permute-start(f32[625,32]{0,1:T(8,128)S(1)} %select_bitcast_fusion), channel_id=1, source_target_pairs={{0,760},{8,0},{16,8},{24,16},{32,24},{40,32},{48,40},{56,48},{64,5... | collective-permute-start | bytes 240008 | tf_op jit(solution)/shard_map/ppermute | solution.py:21
  171.3 1.7 collective-permute-done.19
  (299 shorter events, 54.9 us)
Async XLA Ops:
  0.0 7.4 %copy-start = (f32[5,125,128]{2,1,0:T(8,128)S(1)}, f32[5,125,128]{2,1,0:T(8,128)}, u32[]{:S(2)}) copy-start(f32[5,125,128]{2,1,0:T(8,128)} %param.36) | copy-start | bytes 960004
  10.2 29.2 %copy-start.4 = (s32[6,128]{1,0:T(8,128)S(1)}, s32[6,128]{1,0:T(8,128)}, u32[]{:S(2)}) copy-start(s32[6,128]{1,0:T(8,128)} %param.38) | copy-start | bytes 9220
  10.2 60.0 %collective-permute-start = (f32[125,1,16]{0,2,1:T(8,128)S(1)}, f32[125,1,16]{0,2,1:T(8,128)S(1)}, u32[]{:S(2)}, u32[]{:S(2)}) collective-permute-start(f32[125,1,16]{0,2,1:T(8,128)S(1)} %get-tuple-element.123), channel_id=1, source_target_pairs={{0,1},{1,2},{2,3},{3,4},{4,5},{5,6},{6,7},{7,0},{8,9},{9,10},{10,1... | collective-permute-start | bytes 24008 | tf_op jit(solution)/shard_map/ppermute | solution.py:21
  13.7 58.4 %collective-permute-start.1 = (f32[125,1,16]{0,2,1:T(8,128)S(1)}, f32[125,1,16]{0,2,1:T(8,128)S(1)}, u32[]{:S(2)}, u32[]{:S(2)}) collective-permute-start(f32[125,1,16]{0,2,1:T(8,128)S(1)} %get-tuple-element.122), channel_id=1, source_target_pairs={{0,2},{1,3},{2,4},{3,5},{4,6},{5,7},{6,0},{7,1},{8,10},{9,11},{10,... | collective-permute-start | bytes 24008 | tf_op jit(solution)/shard_map/ppermute | solution.py:21
  19.4 55.2 %collective-permute-start.2 = (f32[125,1,16]{0,2,1:T(8,128)S(1)}, f32[125,1,16]{0,2,1:T(8,128)S(1)}, u32[]{:S(2)}, u32[]{:S(2)}) collective-permute-start(f32[125,1,16]{0,2,1:T(8,128)S(1)} %get-tuple-element.121), channel_id=1, source_target_pairs={{0,3},{1,4},{2,5},{3,6},{4,7},{5,0},{6,1},{7,2},{8,11},{9,12},{10,... | collective-permute-start | bytes 24008 | tf_op jit(solution)/shard_map/ppermute | solution.py:21
  22.2 54.4 %collective-permute-start.3 = (f32[125,1,16]{0,2,1:T(8,128)S(1)}, f32[125,1,16]{0,2,1:T(8,128)S(1)}, u32[]{:S(2)}, u32[]{:S(2)}) collective-permute-start(f32[125,1,16]{0,2,1:T(8,128)S(1)} %get-tuple-element.120), channel_id=1, source_target_pairs={{0,4},{1,5},{2,6},{3,7},{4,0},{5,1},{6,2},{7,3},{8,12},{9,13},{10,... | collective-permute-start | bytes 24008 | tf_op jit(solution)/shard_map/ppermute | solution.py:21
  32.3 54.8 %collective-permute-start.4 = (f32[125,1,16]{0,2,1:T(8,128)S(1)}, f32[125,1,16]{0,2,1:T(8,128)S(1)}, u32[]{:S(2)}, u32[]{:S(2)}) collective-permute-start(f32[125,1,16]{0,2,1:T(8,128)S(1)} %get-tuple-element.119), channel_id=1, source_target_pairs={{0,5},{1,6},{2,7},{3,0},{4,1},{5,2},{6,3},{7,4},{8,13},{9,14},{10,... | collective-permute-start | bytes 24008 | tf_op jit(solution)/shard_map/ppermute | solution.py:21
  43.8 1.2 copy-start.6
  43.8 1.9 %copy-start.7 = (s32[25]{0:T(128)S(1)}, s32[25]{0:T(128)}, u32[]{:S(2)}) copy-start(s32[25]{0:T(128)} %constant.376) | copy-start | bytes 304
  43.8 1.9 %copy-start.8 = (s32[25]{0:T(128)S(1)}, s32[25]{0:T(128)}, u32[]{:S(2)}) copy-start(s32[25]{0:T(128)} %constant.374) | copy-start | bytes 304
  45.7 1.4 copy-start.9
  48.5 0.9 copy-start.18
  55.9 3.3 %copy-start.12 = (s32[128]{0:T(128)S(1)}, s32[128]{0:T(128)}, u32[]{:S(2)}) copy-start(s32[128]{0:T(128)} %param.41) | copy-start | bytes 1540
  58.4 7.9 %copy-start.2 = (f32[125,125,1]{1,0,2:T(8,128)S(1)}, f32[125,125,1]{1,0,2:T(8,128)}, u32[]{:S(2)}) copy-start(f32[125,125,1]{1,0,2:T(8,128)} %constant.380) | copy-start | bytes 187504
  66.3 1.2 copy-start.3
  66.3 1.2 copy-start.10
  70.2 17.0 %collective-permute-start.5 = (f32[125,1,16]{0,2,1:T(8,128)S(1)}, f32[125,1,16]{0,2,1:T(8,128)S(1)}, u32[]{:S(2)}, u32[]{:S(2)}) collective-permute-start(f32[125,1,16]{0,2,1:T(8,128)S(1)} %get-tuple-element.118), channel_id=1, source_target_pairs={{0,6},{1,7},{2,0},{3,1},{4,2},{5,3},{6,4},{7,5},{8,14},{9,15},{10,... | collective-permute-start | bytes 24008 | tf_op jit(solution)/shard_map/ppermute | solution.py:21
  72.1 15.0 %collective-permute-start.6 = (f32[125,1,16]{0,2,1:T(8,128)S(1)}, f32[125,1,16]{0,2,1:T(8,128)S(1)}, u32[]{:S(2)}, u32[]{:S(2)}) collective-permute-start(f32[125,1,16]{0,2,1:T(8,128)S(1)} %get-tuple-element.117), channel_id=1, source_target_pairs={{0,7},{1,0},{2,1},{3,2},{4,3},{5,4},{6,5},{7,6},{8,15},{9,8},{10,9... | collective-permute-start | bytes 24008 | tf_op jit(solution)/shard_map/ppermute | solution.py:21
  74.6 13.1 %collective-permute-start.7 = (f32[125,32]{0,1:T(8,128)S(1)}, f32[125,32]{0,1:T(8,128)S(1)}, u32[]{:S(2)}, u32[]{:S(2)}) collective-permute-start(f32[125,32]{0,1:T(8,128)S(1)} %bitcast.566), channel_id=1, source_target_pairs={{0,8},{8,16},{16,24},{24,32},{32,40},{40,48},{48,56},{56,64},{64,7... | collective-permute-start | bytes 48008 | tf_op jit(solution)/shard_map/ppermute | solution.py:21
  76.6 11.7 %collective-permute-start.8 = (f32[125,32]{0,1:T(8,128)S(1)}, f32[125,32]{0,1:T(8,128)S(1)}, u32[]{:S(2)}, u32[]{:S(2)}) collective-permute-start(f32[125,32]{0,1:T(8,128)S(1)} %bitcast.565), channel_id=1, source_target_pairs={{0,760},{8,0},{16,8},{24,16},{32,24},{40,32},{48,40},{56,48},{64,5... | collective-permute-start | bytes 48008 | tf_op jit(solution)/shard_map/ppermute | solution.py:21
  102.8 2.6 %copy-start.5 = (f32[125]{0:T(128)S(1)}, f32[125]{0:T(128)}, u32[]{:S(2)}) copy-start(f32[125]{0:T(128)} %constant.349.clone) | copy-start | bytes 1504
  102.9 23.3 %collective-permute-start.9 = (f32[625,1,16]{0,2,1:T(8,128)S(1)}, f32[625,1,16]{0,2,1:T(8,128)S(1)}, u32[]{:S(2)}, u32[]{:S(2)}) collective-permute-start(f32[625,1,16]{0,2,1:T(8,128)S(1)} %get-tuple-element.103), channel_id=1, source_target_pairs={{0,1},{1,2},{2,3},{3,4},{4,5},{5,6},{6,7},{7,0},{8,9},{9,10},{10,1... | collective-permute-start | bytes 120008 | tf_op jit(solution)/shard_map/ppermute | solution.py:21
  105.9 22.3 %collective-permute-start.10 = (f32[625,1,16]{0,2,1:T(8,128)S(1)}, f32[625,1,16]{0,2,1:T(8,128)S(1)}, u32[]{:S(2)}, u32[]{:S(2)}) collective-permute-start(f32[625,1,16]{0,2,1:T(8,128)S(1)} %get-tuple-element.102), channel_id=1, source_target_pairs={{0,2},{1,3},{2,4},{3,5},{4,6},{5,7},{6,0},{7,1},{8,10},{9,11},{10,... | collective-permute-start | bytes 120008 | tf_op jit(solution)/shard_map/ppermute | solution.py:21
  110.0 21.0 %collective-permute-start.11 = (f32[625,1,16]{0,2,1:T(8,128)S(1)}, f32[625,1,16]{0,2,1:T(8,128)S(1)}, u32[]{:S(2)}, u32[]{:S(2)}) collective-permute-start(f32[625,1,16]{0,2,1:T(8,128)S(1)} %get-tuple-element.101), channel_id=1, source_target_pairs={{0,3},{1,4},{2,5},{3,6},{4,7},{5,0},{6,1},{7,2},{8,11},{9,12},{10,... | collective-permute-start | bytes 120008 | tf_op jit(solution)/shard_map/ppermute | solution.py:21
  113.7 19.3 %collective-permute-start.12 = (f32[625,1,16]{0,2,1:T(8,128)S(1)}, f32[625,1,16]{0,2,1:T(8,128)S(1)}, u32[]{:S(2)}, u32[]{:S(2)}) collective-permute-start(f32[625,1,16]{0,2,1:T(8,128)S(1)} %get-tuple-element.100), channel_id=1, source_target_pairs={{0,4},{1,5},{2,6},{3,7},{4,0},{5,1},{6,2},{7,3},{8,12},{9,13},{10,... | collective-permute-start | bytes 120008 | tf_op jit(solution)/shard_map/ppermute | solution.py:21
  118.1 21.9 %collective-permute-start.13 = (f32[625,1,16]{0,2,1:T(8,128)S(1)}, f32[625,1,16]{0,2,1:T(8,128)S(1)}, u32[]{:S(2)}, u32[]{:S(2)}) collective-permute-start(f32[625,1,16]{0,2,1:T(8,128)S(1)} %get-tuple-element.99), channel_id=1, source_target_pairs={{0,5},{1,6},{2,7},{3,0},{4,1},{5,2},{6,3},{7,4},{8,13},{9,14},{10,... | collective-permute-start | bytes 120008 | tf_op jit(solution)/shard_map/ppermute | solution.py:21
  126.2 13.8 %collective-permute-start.14 = (f32[625,1,16]{0,2,1:T(8,128)S(1)}, f32[625,1,16]{0,2,1:T(8,128)S(1)}, u32[]{:S(2)}, u32[]{:S(2)}) collective-permute-start(f32[625,1,16]{0,2,1:T(8,128)S(1)} %get-tuple-element.98), channel_id=1, source_target_pairs={{0,6},{1,7},{2,0},{3,1},{4,2},{5,3},{6,4},{7,5},{8,14},{9,15},{10,... | collective-permute-start | bytes 120008 | tf_op jit(solution)/shard_map/ppermute | solution.py:21
  128.2 11.9 %collective-permute-start.15 = (f32[625,1,16]{0,2,1:T(8,128)S(1)}, f32[625,1,16]{0,2,1:T(8,128)S(1)}, u32[]{:S(2)}, u32[]{:S(2)}) collective-permute-start(f32[625,1,16]{0,2,1:T(8,128)S(1)} %get-tuple-element.97), channel_id=1, source_target_pairs={{0,7},{1,0},{2,1},{3,2},{4,3},{5,4},{6,5},{7,6},{8,15},{9,8},{10,9... | collective-permute-start | bytes 120008 | tf_op jit(solution)/shard_map/ppermute | solution.py:21
  131.0 9.6 %collective-permute-start.16 = (f32[625,32]{0,1:T(8,128)S(1)}, f32[625,32]{0,1:T(8,128)S(1)}, u32[]{:S(2)}, u32[]{:S(2)}) collective-permute-start(f32[625,32]{0,1:T(8,128)S(1)} %bitcast.564), channel_id=1, source_target_pairs={{0,8},{8,16},{16,24},{24,32},{32,40},{40,48},{48,56},{56,64},{64,7... | collective-permute-start | bytes 240008 | tf_op jit(solution)/shard_map/ppermute | solution.py:21
  133.0 9.0 %collective-permute-start.17 = (f32[625,32]{0,1:T(8,128)S(1)}, f32[625,32]{0,1:T(8,128)S(1)}, u32[]{:S(2)}, u32[]{:S(2)}) collective-permute-start(f32[625,32]{0,1:T(8,128)S(1)} %bitcast.563), channel_id=1, source_target_pairs={{0,760},{8,0},{16,8},{24,16},{32,24},{40,32},{48,40},{56,48},{64,5... | collective-permute-start | bytes 240008 | tf_op jit(solution)/shard_map/ppermute | solution.py:21
  161.3 9.9 %collective-permute-start.18 = (f32[625,32]{0,1:T(8,128)S(1)}, f32[625,32]{0,1:T(8,128)S(1)}, u32[]{:S(2)}, u32[]{:S(2)}) collective-permute-start(f32[625,32]{0,1:T(8,128)S(1)} %select_bitcast_fusion.1), channel_id=1, source_target_pairs={{0,8},{8,16},{16,24},{24,32},{32,40},{40,48},{48,56},{56,64},{64,7... | collective-permute-start | bytes 240008 | tf_op jit(solution)/shard_map/ppermute | solution.py:21
  163.9 9.1 %collective-permute-start.19 = (f32[625,32]{0,1:T(8,128)S(1)}, f32[625,32]{0,1:T(8,128)S(1)}, u32[]{:S(2)}, u32[]{:S(2)}) collective-permute-start(f32[625,32]{0,1:T(8,128)S(1)} %select_bitcast_fusion), channel_id=1, source_target_pairs={{0,760},{8,0},{16,8},{24,16},{32,24},{40,32},{48,40},{56,48},{64,5... | collective-permute-start | bytes 240008 | tf_op jit(solution)/shard_map/ppermute | solution.py:21
  (7 other events, 4.9 us)
where the time goes:
time: 175 us; the launch traced here: 174 us
  starting transfers between devices  89.4 us (51%)
  other arithmetic  44.1 us (25%)
  local copies, waits for them, and re-layouts  33.5 us (19%)
  waiting for transfers between devices  3.69 us (2%)
  between operations  2.1 us (1%)
    ppermute x20, starting transfers between devices, from_behind(): return lax.ppermute(value, axis, pairs)  89.4 us
    scatter-add x6, other arithmetic, section_update(): change = change.at[:, face_table[face], :].add(lift)  10.1 us
    sub x6, other arithmetic, weno_combine(): other - cell_mean(other, cell_weights)[:, None, :] + own_mean[:, None, :]  8.83 us
    sort x2, other arithmetic, departures(): jnp.argsort(jnp.where(leaving, elem_ids, elem_count + elem_ids), stable=T...  5.16 us
    sort x1, other arithmetic, shards(): send_order = jnp.argsort(category * slot_count + partner_slot, stable=True)  4.37 us
    gather x6, local copies, waits for them, and re-layouts, shards(): poly_cols[face * elem_count + cells]  4.37 us
    sort x1, other arithmetic, shards(): recv_order = jnp.argsort(category * slot_count + own_slots, stable=True)  4.37 us
    gather x6, local copies, waits for them, and re-layouts, section_update(): inner = state[:, face_table[face], :]  4.06 us
  transfers between devices with their start and end apart: 20, of which 3 were waited for; matrix products, arithmetic and copies ran while one was open for 19% of the time, Pallas kernels for 0%

commit v1 on v0

v1 whole, which is shorter than its diff:
```python
import functools
import math

import jax
import jax.numpy as jnp
import numpy as np
from jax import lax
from jax.experimental import pallas as pl
from jax.experimental.pallas import tpu as pltpu
from jax.sharding import PartitionSpec as P

GROUP_FACES = 16
WIDE_FACES = 32
MOVE_CAP = 32
SECTION_STEP = 0.01
LIFT_GAIN = 10.0

ELEM = 128
VARS = 5
NODES = 125
FACES = 6
GROUP = 8
GROUP_ROWS = GROUP * GROUP_FACES
PAIR0 = GROUP_ROWS
PAIR1 = GROUP_ROWS + WIDE_FACES
ROWS = GROUP_ROWS + 2 * WIDE_FACES
LOCAL = 10

F32 = jnp.float32
BF16 = jnp.bfloat16
I32 = jnp.int32
INTERPRET = False


def gll_tables():
    root = math.sqrt(3.0 / 7.0)
    points = np.array([-1.0, -root, 0.0, root, 1.0])
    weights = np.array([0.1, 49.0 / 90.0, 32.0 / 45.0, 49.0 / 90.0, 0.1])
    bary = np.array(
        [1.0 / np.prod([points[j] - points[k] for k in range(5) if k != j]) for j in range(5)]
    )
    deriv = np.zeros((5, 5))
    for i in range(5):
        for j in range(5):
            if i != j:
                deriv[i, j] = bary[j] / bary[i] / (points[i] - points[j])
        deriv[i, i] = -np.sum(deriv[i])
    ident = np.eye(5)
    diffs = [
        np.kron(np.kron(deriv, ident), ident),
        np.kron(np.kron(ident, deriv), ident),
        np.kron(np.kron(ident, ident), deriv),
    ]
    cell_weights = np.kron(np.kron(weights, weights), weights) / 8.0
    return diffs, cell_weights


def face_rows(face):
    if face < 2:
        return [(100 * face, 25, 1, 0)]
    if face < 4:
        return [(25 * a + 20 * (face - 2), 5, 1, 5 * a) for a in range(5)]
    return [(4 * (face - 4), 25, 5, 0)]


def rows_at(first, count, stride):
    return pl.ds(first, count) if stride == 1 else pl.ds(first, count, stride=stride)


def thirds(x):
    hi = x.astype(BF16)
    rest = x - hi.astype(F32)
    mid = rest.astype(BF16)
    lo = (rest - mid.astype(F32)).astype(BF16)
    return hi, mid, lo


def dot_nn(a, b):
    return lax.dot_general(a, b, (((1,), (0,)), ((), ())), preferred_element_type=F32)


def dot_nt(a, b):
    return lax.dot_general(a, b, (((1,), (1,)), ((), ())), preferred_element_type=F32)


def select_nt(onehot, values):
    hi, mid, lo = thirds(values)
    return dot_nt(onehot, hi) + dot_nt(onehot, mid) + dot_nt(onehot, lo)


def iota(shape, dim):
    return lax.broadcasted_iota(I32, shape, dim)


def onehot(mask):
    return jnp.where(mask, 1.0, 0.0).astype(BF16)


def places():
    wide = lax.axis_index("wide")
    grp = lax.axis_index("grp")
    size = lax.axis_size("wide")
    left = lax.rem(wide + size - 1, size) * GROUP + grp
    right = lax.rem(wide + 1, size) * GROUP + grp
    odd = lax.rem(wide, 2)
    return wide, grp, left, right, odd


def categories(nbr_elem):
    wide, grp, left, _, odd = places()
    owner = lax.shift_right_logical(nbr_elem, 7)
    beside = jnp.where(owner == left, 9 - odd, 8 + odd)
    cat = jnp.where(lax.shift_right_logical(owner, 3) == wide, owner & 7, beside)
    return jnp.where(owner == wide * GROUP + grp, LOCAL, cat)


def strict_upper():
    return onehot(iota((ELEM, ELEM), 0) < iota((ELEM, ELEM), 1))


def pack_kernel(elem_ref, state_ref, grp_ref, pair0_ref, pair1_ref, trace_ref, pick_ref, s_ref):
    cat = categories(elem_ref[...])
    kinds = iota((16, ELEM), 0)
    hot = [jnp.where(cat[f : f + 1, :] == kinds, 1.0, 0.0) for f in range(FACES)]
    upper = jnp.concatenate([strict_upper(), jnp.ones((ELEM, ELEM), BF16)], axis=1)
    counts = dot_nn(jnp.concatenate(hot, axis=0).astype(BF16), upper)
    base = jnp.where(kinds < 9, 16 * kinds, PAIR1).astype(F32)
    pick = jnp.zeros((ROWS, ELEM), F32)
    rows = iota((ROWS, ELEM), 0)
    for f in range(FACES):
        part = counts[16 * f : 16 * f + 16]
        pos = jnp.sum(hot[f] * (part[:, :ELEM] + base), axis=0, keepdims=True)
        base = base + part[:, ELEM:]
        pos = jnp.where(cat[f : f + 1, :] == LOCAL, -1, pos.astype(I32))
        chosen = jnp.where(rows == pos, 1.0, 0.0)
        pick = pick + chosen
        s_ref[:, f * ELEM : (f + 1) * ELEM] = chosen.astype(BF16)
    pick_ref[...] = pick.astype(BF16)
    for f in range(FACES):
        for v in range(VARS):
            for first, count, stride, place in face_rows(f):
                trace_ref[25 * v + place : 25 * v + place + count, f * ELEM : (f + 1) * ELEM] = state_ref[
                    v, rows_at(first, count, stride), :
                ]
    trace_ref[125:128, :] = jnp.zeros((3, FACES * ELEM), F32)
    sent = select_nt(s_ref[...], trace_ref[...])
    grp_ref[...] = sent[:GROUP_ROWS]
    pair0_ref[...] = sent[PAIR0:PAIR1]
    pair1_ref[...] = sent[PAIR1:]


def primitives(u):
    inv = 1.0 / u[0]
    vel = [u[1] * inv, u[2] * inv, u[3] * inv]
    kinetic = u[1] * vel[0] + u[2] * vel[1] + u[3] * vel[2]
    pressure = 0.4 * (u[4] - 0.5 * kinetic)
    return inv, vel, pressure


def flux(u, vel, pressure, a):
    w = vel[a]
    rows = [u[1 + a], u[1] * w, u[2] * w, u[3] * w, (u[4] + pressure) * w]
    rows[1 + a] = rows[1 + a] + pressure
    return rows


def speed(inv, vel, pressure, a):
    return jnp.abs(vel[a]) + jnp.sqrt(1.4 * pressure * inv)


def face_values(ref, f):
    return [ref[25 * v : 25 * v + 25, f * ELEM : (f + 1) * ELEM] for v in range(VARS)]


def add_face(ref, f, v, value):
    for first, count, stride, place in face_rows(f):
        at = rows_at(first, count, stride)
        ref[v, at, :] = ref[v, at, :] + value[place : place + count]


def local_kernel(
    elem_ref, face_ref, state_ref, metric_ref, trace_ref, diff_ref,
    base_ref, speed_ref, near_ref, take_ref, pos_ref, f_ref, key_ref,
):
    metric = metric_ref[...]
    u = [state_ref[v] for v in range(VARS)]
    inv, vel, pressure = primitives(u)
    for a in range(3):
        for v, row in enumerate(flux(u, vel, pressure, a)):
            f_ref[128 * a : 128 * a + NODES, v * ELEM : (v + 1) * ELEM] = row
        f_ref[128 * a + NODES : 128 * a + 128, :] = jnp.zeros((3, VARS * ELEM), F32)
    volume = jnp.dot(diff_ref[...], f_ref[...], precision=lax.Precision.HIGHEST, preferred_element_type=F32)
    for v in range(VARS):
        base_ref[v] = u[v] - (SECTION_STEP * metric) * volume[:NODES, v * ELEM : (v + 1) * ELEM]
    half = (0.5 * LIFT_GAIN * SECTION_STEP) * metric
    for f in range(FACES):
        a = f // 2
        scale = half if f % 2 else -half
        inner = face_values(trace_ref, f)
        inv, vel, pressure = primitives(inner)
        speed_ref[f] = speed(inv, vel, pressure, a)
        for v, row in enumerate(flux(inner, vel, pressure, a)):
            add_face(base_ref, f, v, scale * row)
    cat = categories(elem_ref[...])
    partner = face_ref[...] * ELEM + (elem_ref[...] & (ELEM - 1))
    _, grp, _, _, _ = places()
    key = jnp.concatenate([cat * (FACES * ELEM) + partner, jnp.zeros((2, ELEM), I32)], axis=0)
    key_ref[...] = key.astype(F32).T
    keys = key.astype(F32)
    rank = [jnp.zeros((ELEM, ELEM), F32) for _ in range(FACES)]
    for g in range(FACES):
        column = key_ref[:, g : g + 1]
        for f in range(FACES):
            rank[f] = rank[f] + jnp.where(column < keys[f : f + 1, :], 1.0, 0.0)
    rows = iota((ROWS, ELEM), 0)
    slots = iota((FACES * ELEM, ELEM), 0)
    hi, mid, lo = thirds(trace_ref[...])
    stacked = jnp.concatenate([hi, mid, lo], axis=0)
    for f in range(FACES):
        own = cat[f : f + 1, :]
        pos = jnp.sum(rank[f], axis=0, keepdims=True).astype(I32)
        pos = pos + jnp.where(own > grp, GROUP_FACES, 0)
        pos = jnp.where(own == LOCAL, -1, pos)
        pos_ref[f : f + 1, :] = pos
        take_ref[:, f * ELEM : (f + 1) * ELEM] = onehot(rows == pos)
        inside = jnp.where(own == LOCAL, partner[f : f + 1, :], -1)
        got = dot_nn(stacked, onehot(slots == inside))
        near_ref[:, f * ELEM : (f + 1) * ELEM] = got[:128] + got[128:256] + got[256:]
    pos_ref[6:8, :] = jnp.zeros((2, ELEM), I32)


def section_kernel(
    grp_ref, pair0_ref, pair1_ref, base_ref, speed_ref, near_ref, take_ref, trace_ref, pick_ref, metric_ref, weight_ref,
    send_ref, send0_ref, send1_ref, sec_ref, donor_ref, mean_ref, outer_ref,
):
    got = jnp.concatenate([grp_ref[...], pair0_ref[...], pair1_ref[...]], axis=0).T
    hi, mid, lo = thirds(got)
    far = dot_nn(jnp.concatenate([hi, mid, lo], axis=0), take_ref[...])
    outer_ref[...] = near_ref[...] + far[:128] + far[128:256] + far[256:]
    half = (0.5 * LIFT_GAIN * SECTION_STEP) * metric_ref[...]
    sec_ref[...] = base_ref[...]
    for f in range(FACES):
        a = f // 2
        sign = 1.0 if f % 2 else -1.0
        inner = face_values(trace_ref, f)
        outer = face_values(outer_ref, f)
        inv, vel, pressure = primitives(outer)
        lam = half * jnp.maximum(speed_ref[f], speed(inv, vel, pressure, a))
        for v, row in enumerate(flux(outer, vel, pressure, a)):
            add_face(sec_ref, f, v, lam * (outer[v] - inner[v]) - (sign * half) * row)
    weight = weight_ref[...]
    for v in range(VARS):
        q = sec_ref[v]
        mean = jnp.sum(weight * q, axis=0, keepdims=True)
        dev = q - mean
        beta = 1e-06 + jnp.sum(weight * dev * dev, axis=0, keepdims=True)
        omega = 0.1 / (beta * beta)
        donor_ref[128 * v : 128 * v + NODES, :] = omega * dev
        donor_ref[128 * v + NODES : 128 * v + NODES + 1, :] = omega
        donor_ref[128 * v + NODES + 1 : 128 * v + 128, :] = jnp.zeros((2, ELEM), F32)
        mean_ref[v : v + 1, :] = mean
    sent = select_nt(pick_ref[...], donor_ref[...])
    send_ref[...] = sent[:GROUP_ROWS]
    send0_ref[...] = sent[PAIR0:PAIR1]
    send1_ref[...] = sent[PAIR1:]


def inside_kernel(
    elem_ref, troubled_ref, owner_ref, pos_ref, donor_ref,
    sum_ref, far_ref, move_ref, mask_ref,
):
    _, grp, left, right, odd = places()
    own = lax.axis_index("wide") * GROUP + grp
    elem = elem_ref[...]
    cells = jnp.where(troubled_ref[...] == iota((ELEM, 48), 0), 1.0, 0.0).astype(BF16)
    mask = dot_nt(jnp.ones((8, 48), BF16), cells)[0:1, :]
    mask_ref[0:1, :] = mask
    local = jnp.where(lax.shift_right_logical(elem, 7) == own, elem & (ELEM - 1), -1)
    rows = iota((ROWS, ELEM), 0)
    elems = iota((ELEM, ELEM), 0)
    near = jnp.zeros((ELEM, ELEM), F32)
    far = jnp.zeros((ROWS, ELEM), F32)
    for f in range(FACES):
        near = near + jnp.where(elems == local[f : f + 1, :], 1.0, 0.0)
        far = far + jnp.where(rows == pos_ref[f : f + 1, :], 1.0, 0.0)
    far_ref[...] = far.astype(BF16)
    near = near.astype(BF16)
    hi, mid, lo = thirds(donor_ref[...])
    sum_ref[...] = dot_nn(hi, near) + dot_nn(mid, near) + dot_nn(lo, near)
    owner = owner_ref[...]
    mask_ref[1:2, :] = jnp.where(owner == own, 1.0, 0.0)
    out0 = jnp.where(odd == 1, left, right)
    out1 = jnp.where(odd == 1, right, left)
    go0 = jnp.where(owner == out0, 1.0, 0.0)
    go1 = jnp.where(owner == out1, 1.0, 0.0)
    go = jnp.concatenate([go0, go1, jnp.zeros((6, ELEM), F32)], axis=0)
    order = dot_nn(go.astype(BF16), strict_upper())
    place = jnp.where(go0 > 0.5, order[0:1, :], jnp.where(go1 > 0.5, MOVE_CAP + order[1:2, :], -1.0))
    move_ref[...] = onehot(iota((2 * MOVE_CAP, ELEM), 0) == place.astype(I32))


def limit_kernel(
    grp_ref, pair0_ref, pair1_ref, sum_ref, far_ref, move_ref, mask_ref, donor_ref, mean_ref, sec_ref,
    limited_ref, go0_ref, go1_ref, flat_ref,
):
    got = jnp.concatenate([grp_ref[...], pair0_ref[...], pair1_ref[...]], axis=0)
    hi, mid, lo = thirds(got)
    far = far_ref[...]
    turned = far.astype(F32).T.astype(BF16)
    add = dot_nn(turned, hi) + dot_nn(turned, mid) + dot_nn(turned, lo)
    total = sum_ref[...] + add.T
    troubled = mask_ref[0:1, :] > 0.5
    for v in range(VARS):
        block = total[128 * v : 128 * v + 128]
        weights = block[NODES : NODES + 1]
        own = 4.0 * donor_ref[128 * v + NODES : 128 * v + NODES + 1, :]
        q = sec_ref[v]
        inv = 1.0 / (own + weights)
        value = (own * inv) * q + inv * block[:NODES] + (weights * inv) * mean_ref[v : v + 1, :]
        value = jnp.where(troubled, value, q)
        limited_ref[v] = value
        flat_ref[128 * v : 128 * v + NODES, :] = value
        flat_ref[128 * v + NODES : 128 * v + 128, :] = jnp.zeros((3, ELEM), F32)
    moved = select_nt(move_ref[...], flat_ref[...])
    go0_ref[...] = moved[:MOVE_CAP]
    go1_ref[...] = moved[MOVE_CAP:]


def keep_kernel(limited_ref, mask_ref, out_ref):
    stays = mask_ref[1:2, :] > 0.5
    for v in range(VARS):
        out_ref[v] = jnp.where(stays, limited_ref[v], 0.0)


def arrive_kernel(in0_ref, in1_ref, kept_ref, out_ref):
    odd = lax.rem(lax.axis_index("wide"), 2) == 1
    from_left = jnp.where(odd, in0_ref[...], in1_ref[...])
    from_right = jnp.where(odd, in1_ref[...], in0_ref[...])
    both = jnp.concatenate([from_left, from_right, jnp.zeros((64, VARS * 128), F32)], axis=0).T
    for v in range(VARS):
        out_ref[v] = both[128 * v : 128 * v + NODES]


VMEM = pl.BlockSpec(memory_space=pltpu.VMEM)


def call(kernel, shapes, scratch, *args):
    return pl.pallas_call(
        kernel,
        out_shape=[jax.ShapeDtypeStruct(shape, dtype) for shape, dtype in shapes],
        in_specs=[VMEM] * len(args),
        out_specs=[VMEM] * len(shapes),
        scratch_shapes=[pltpu.VMEM(shape, dtype) for shape, dtype in scratch],
        interpret=INTERPRET,
    )(*args)


def exchange(blocks, pair0, pair1):
    size = lax.axis_size("wide")
    first = [(i, i ^ 1) for i in range(size)]
    second = [(i, (i + 1) % size if i % 2 else (i - 1) % size) for i in range(size)]
    lanes = blocks.shape[1]
    got = lax.all_to_all(blocks.reshape(GROUP, GROUP_FACES, lanes), "grp", 0, 0)
    return (
        got.reshape(GROUP_ROWS, lanes),
        lax.ppermute(pair0, "wide", first),
        lax.ppermute(pair1, "wide", second),
    )


def swap(pair0, pair1):
    size = lax.axis_size("wide")
    first = [(i, i ^ 1) for i in range(size)]
    second = [(i, (i + 1) % size if i % 2 else (i - 1) % size) for i in range(size)]
    return lax.ppermute(pair0, "wide", first), lax.ppermute(pair1, "wide", second)


def shards(state, metric, nbr_elem, nbr_face, troubled, new_owner):
    diffs, weights = gll_tables()
    diff = np.zeros((128, 384), np.float32)
    for a in range(3):
        diff[:NODES, 128 * a : 128 * a + NODES] = diffs[a]
    diff = jnp.asarray(diff)
    weight = jnp.asarray(np.repeat(weights[:, None], ELEM, axis=1), F32)
    metric = metric.reshape(1, ELEM)
    troubled = troubled.reshape(1, 48)
    new_owner = new_owner.reshape(1, ELEM)
    cols = VARS * 128
    wide_lanes = FACES * ELEM

    blocks, pair0, pair1, trace, pick = call(
        pack_kernel,
        [((GROUP_ROWS, 128), F32), ((32, 128), F32), ((32, 128), F32), ((128, wide_lanes), F32), ((ROWS, ELEM), BF16)],
        [((ROWS, wide_lanes), BF16)],
        nbr_elem, state,
    )
    got, got0, got1 = exchange(blocks, pair0, pair1)
    base, speeds, near, take, pos = call(
        local_kernel,
        [((VARS, NODES, ELEM), F32), ((FACES, 25, ELEM), F32), ((128, wide_lanes), F32), ((ROWS, wide_lanes), BF16), ((8, ELEM), I32)],
        [((384, cols), F32), ((ELEM, 8), F32)],
        nbr_elem, nbr_face, state, metric, trace, diff,
    )
    blocks, pair0, pair1, sec, donor, mean = call(
        section_kernel,
        [((GROUP_ROWS, cols), F32), ((32, cols), F32), ((32, cols), F32), ((VARS, NODES, ELEM), F32), ((cols, ELEM), F32), ((8, ELEM), F32)],
        [((128, wide_lanes), F32)],
        got, got0, got1, base, speeds, near, take, trace, pick, metric, weight,
    )
    got, got0, got1 = exchange(blocks, pair0, pair1)
    total, far, move, mask = call(
        inside_kernel,
        [((cols, ELEM), F32), ((ROWS, ELEM), BF16), ((2 * MOVE_CAP, ELEM), BF16), ((8, ELEM), F32)],
        [],
        nbr_elem, troubled, new_owner, pos, donor,
    )
    limited, go0, go1 = call(
        limit_kernel,
        [((VARS, NODES, ELEM), F32), ((MOVE_CAP, cols), F32), ((MOVE_CAP, cols), F32)],
        [((cols, ELEM), F32)],
        got, got0, got1, total, far, move, mask, donor, mean, sec,
    )
    in0, in1 = swap(go0, go1)
    out_shape = jax.ShapeDtypeStruct((VARS, NODES, ELEM + 2 * MOVE_CAP), F32)
    whole = lambda shape: pl.BlockSpec(shape, lambda i: (0,) * len(shape))
    kept = pl.pallas_call(
        keep_kernel,
        out_shape=out_shape,
        grid=(1,),
        in_specs=[whole((VARS, NODES, ELEM)), whole((8, ELEM))],
        out_specs=pl.BlockSpec((VARS, NODES, ELEM), lambda i: (0, 0, 0)),
        interpret=INTERPRET,
    )(limited, mask)
    return pl.pallas_call(
        arrive_kernel,
        out_shape=out_shape,
        grid=(1,),
        in_specs=[whole((MOVE_CAP, cols)), whole((MOVE_CAP, cols)), pl.BlockSpec(memory_space=pl.ANY)],
        out_specs=pl.BlockSpec((VARS, NODES, ELEM), lambda i: (0, 0, 1)),
        input_output_aliases={2: 0},
        interpret=INTERPRET,
    )(in0, in1, kept)


def solution(mesh):
    placed = (
        P(None, None, ("wide", "grp")),
        P(("wide", "grp")),
        P(None, ("wide", "grp")),
        P(None, ("wide", "grp")),
        P(("wide", "grp")),
        P(("wide", "grp")),
    )
    return jax.shard_map(
        shards,
        mesh=mesh,
        in_specs=placed,
        out_specs=P(None, None, ("wide", "grp")),
        check_vma=False,
    )
```

time: 175 us -> 75.6 us (0.43)
  other arithmetic: 44.1 us -> 0 us
  starting transfers between devices: 89.4 us -> 45.7 us
  local copies, waits for them, and re-layouts: 33.5 us -> 4.11 us
  Pallas kernels: 0 us -> 18.5 us
  waiting for transfers between devices: 3.69 us -> 6.39 us
  between operations: 2.1 us -> 0.14 us
    ppermute x20 -> x6, starting transfers between devices: 89.4 us -> 25.5 us  [the longest x2 15.4 us: exchange(): lax.ppermute(pair1, 'wide', second)]
    gather x35 -> x0, local copies, waits for them, and re-layouts: 23.2 us -> none  [the longest x6 4.37 us: shards(): poly_cols[face * elem_count + cells]]
    all_to_all x0 -> x2, starting transfers between devices: none -> 20.2 us  [exchange(): got = lax.all_to_all(blocks.reshape(GROUP, GROUP_FACES, lanes), 'grp', 0, 0)]
    pallas_call x0 -> x7, Pallas kernels: none -> 18.5 us  [the longest x5 14.9 us: call(): pl.pallas_call(kernel, out_shape=[jax.ShapeDtypeStruct(shape, dtype) for...]
    sort x4 -> x0, other arithmetic: 13.9 us -> none  [the longest x2 5.16 us: departures(): jnp.argsort(jnp.where(leaving, elem_ids, elem_count + elem_ids), stable=T...]
    scatter-add x6 -> x0, other arithmetic: 10.1 us -> none  [section_update(): change = change.at[:, face_table[face], :].add(lift)]
    sub x12 -> x0, other arithmetic: 10.1 us -> none  [the longest x6 8.83 us: weno_combine(): other - cell_mean(other, cell_weights)[:, None, :] + own_mean[:, None, :]]
    scatter x3 -> x0, local copies, waits for them, and re-layouts: 4.26 us -> none  [the longest x1 1.95 us: shards(): sectioned.at[:, :, jnp.where(valid, cells, elem_count)]]
  transfers between devices with their start and end apart: 20 -> 8, of which waited for: 3 -> 2; matrix products, arithmetic and copies ran while one was open for 19% -> 0% of each run, Pallas kernels for 0% -> 11%
where the time goes in v1:
time: 75.6 us; the launch traced here: 74.8 us
  starting transfers between devices  45.7 us (60%)
  Pallas kernels  18.5 us (24%)
  waiting for transfers between devices  6.39 us (8%)
  local copies, waits for them, and re-layouts  4.11 us (5%)
    all_to_all x2, starting transfers between devices, exchange(): got = lax.all_to_all(blocks.reshape(GROUP, GROUP_FACES, lanes), 'grp', 0, 0)  20.2 us
    ppermute x2, starting transfers between devices, exchange(): lax.ppermute(pair1, 'wide', second)  15.4 us
    pallas_call x5, Pallas kernels, call(): pl.pallas_call(kernel, out_shape=[jax.ShapeDtypeStruct(shape, dtype) for...  14.9 us
    ppermute x1, starting transfers between devices, swap(): lax.ppermute(pair1, 'wide', second)  4.36 us
    ppermute x2, starting transfers between devices, exchange(): lax.ppermute(pair0, 'wide', first)  3.82 us
    ppermute x2, waiting for transfers between devices, exchange(): lax.ppermute(pair1, 'wide', second)  3.22 us
    ppermute x1, waiting for transfers between devices, swap(): lax.ppermute(pair1, 'wide', second)  3.16 us
    pallas_call x1, local copies, waits for them, and re-layouts, shards(): pl.pallas_call(arrive_kernel, out_shape=out_shape, grid=(1,), in_specs=[w...  2.11 us
  transfers between devices with their start and end apart: 8, of which 2 were waited for; matrix products, arithmetic and copies ran while one was open for 0% of the time, Pallas kernels for 11%

profile of v1, /device:TPU:8, one launch (start us, length us, event | category | flops | bytes accessed | tf_op | source)
XLA Modules:
  0.0 74.8 jit_solution(8631183821568748508)
XLA Ops:
  0.0 2.2 %shard_map.82 = (f32[128,128]{1,0:T(8,128)}, f32[32,128]{1,0:T(8,128)}, f32[32,128]{1,0:T(8,128)}, f32[128,768]{1,0:T(8,128)}, bf16[192,128]{1,0:T(8,128)(2,1)}) custom-call(s32[6,128]{1,0:T(8,128)} %elem_ref.5, f32[5,125,128]{2,1,0:T(8,128)} %state_ref.3), custom_call_target="tpu_custom_call" | custom-call | tf_op jit(solution)/shard_map/pallas_call | solution.py:348
  2.2 12.8 %all-to-all-start = ((f32[8,16,128]{2,1,0:T(8,128)}), f32[8,16,128]{2,1,0:T(8,128)S(1)}, u32[]{:S(2)}, u32[]{:S(2)}) async-start(f32[8,16,128]{2,1,0:T(8,128)} %bitcast.10), calls=%async_computation | async-start | bytes 131072 | tf_op jit(solution)/shard_map/all_to_all | solution.py:363
  15.0 0.0 copy-done.11
  15.0 1.9 %collective-permute-start = (f32[32,128]{1,0:T(8,128)S(1)}, f32[32,128]{1,0:T(8,128)S(1)}, u32[]{:S(2)}, u32[]{:S(2)}) collective-permute-start(f32[32,128]{1,0:T(8,128)S(1)} %copy-done.11), channel_id=1, source_target_pairs={{0,8},{8,0},{16,24},{24,16},{32,40},{40,32},{48,56},{56,48},{64,72... | collective-permute-start | bytes 49160 | tf_op jit(solution)/shard_map/ppermute | solution.py:366
  17.0 11.7 %collective-permute-start.1 = (f32[32,128]{1,0:T(8,128)S(1)}, f32[32,128]{1,0:T(8,128)S(1)}, u32[]{:S(2)}, u32[]{:S(2)}) collective-permute-start(f32[32,128]{1,0:T(8,128)S(1)} %copy-done.10), channel_id=1, source_target_pairs={{0,760},{8,16},{16,8},{24,32},{32,24},{40,48},{48,40},{56,64},{64,... | collective-permute-start | bytes 49160 | tf_op jit(solution)/shard_map/ppermute | solution.py:367
  28.7 4.1 %shard_map.83 = (f32[5,125,128]{2,1,0:T(8,128)}, f32[6,25,128]{2,1,0:T(8,128)}, f32[128,768]{1,0:T(8,128)}, bf16[192,768]{1,0:T(8,128)(2,1)}, s32[8,128]{1,0:T(8,128)}) custom-call(s32[6,128]{1,0:T(8,128)} %elem_ref.5, s32[6,128]{1,0:T(8,128)} %face_ref.1, f32[5,125,128]{2,1,0:T(8,128)} %state_ref.3, f32[1,128]{1,0:T(1,128)} %bitcast.11, ...), custom_call_target="tpu_custom_call" | custom-call | tf_op jit(solution)/shard_map/pallas_call | solution.py:348
  32.8 0.0 collective-permute-done.pair0_ref
  32.8 0.0 collective-permute-done.1.pair1_ref
  32.8 0.0 all-to-all-done
  32.9 0.6 copy-done.6
  33.4 0.0 copy-done.7
  33.4 0.0 copy-done.1
  33.5 3.4 %shard_map.84 = (f32[128,640]{1,0:T(8,128)}, f32[32,640]{1,0:T(8,128)}, f32[32,640]{1,0:T(8,128)}, f32[5,125,128]{2,1,0:T(8,128)}, f32[640,128]{1,0:T(8,128)}, /*index=5*/f32[8,128]{1,0:T(8,128)}) custom-call(f32[128,128]{1,0:T(8,128)} %bitcast.9, f32[32,128]{1,0:T(8,128)} %copy-done.6, f32[32,128]{1,0:T(8,128)} %copy-done.7, ...), custom_call_target="tpu_custom_call" | custom-call | tf_op jit(solution)/shard_map/pallas_call | solution.py:348
  36.9 7.4 %all-to-all-start.1 = ((f32[8,16,640]{2,1,0:T(8,128)}), f32[8,16,640]{2,1,0:T(8,128)S(1)}, u32[]{:S(2)}, u32[]{:S(2)}) async-start(f32[8,16,640]{2,1,0:T(8,128)} %bitcast.8), calls=%async_computation.1 | async-start | bytes 655360 | tf_op jit(solution)/shard_map/all_to_all | solution.py:363
  44.3 1.9 %collective-permute-start.2 = (f32[32,640]{1,0:T(8,128)S(1)}, f32[32,640]{1,0:T(8,128)S(1)}, u32[]{:S(2)}, u32[]{:S(2)}) collective-permute-start(f32[32,640]{1,0:T(8,128)S(1)} %copy-done.9), channel_id=1, source_target_pairs={{0,8},{8,0},{16,24},{24,16},{32,40},{40,32},{48,56},{56,48},{64,72... | collective-permute-start | bytes 245768 | tf_op jit(solution)/shard_map/ppermute | solution.py:366
  46.2 3.7 %collective-permute-start.3 = (f32[32,640]{1,0:T(8,128)S(1)}, f32[32,640]{1,0:T(8,128)S(1)}, u32[]{:S(2)}, u32[]{:S(2)}) collective-permute-start(f32[32,640]{1,0:T(8,128)S(1)} %copy-done.8), channel_id=1, source_target_pairs={{0,760},{8,16},{16,8},{24,32},{32,24},{40,48},{48,40},{56,64},{64,... | collective-permute-start | bytes 245768 | tf_op jit(solution)/shard_map/ppermute | solution.py:367
  49.9 2.2 %shard_map.85 = (f32[640,128]{1,0:T(8,128)}, bf16[192,128]{1,0:T(8,128)(2,1)}, bf16[64,128]{1,0:T(8,128)(2,1)}, f32[8,128]{1,0:T(8,128)}) custom-call(s32[6,128]{1,0:T(8,128)} %elem_ref.5, s32[1,48]{1,0:T(1,128)} %bitcast.13, s32[1,128]{1,0:T(1,128)} %bitcast.14, s32[8,128]{1,0:T(8,128)} %get-tuple-element.40.pos_ref, f32[640,128]{1,0:T(8,128)} %get-tuple-element.41.donor_ref), custom_call_target="tpu_custom_call" | custom-call | tf_op jit(solution)/shard_map/pallas_call | solution.py:348
  52.1 0.0 collective-permute-done.2.pair0_ref
  52.1 3.2 %collective-permute-done.3.pair1_ref = f32[32,640]{1,0:T(8,128)S(1)} collective-permute-done((f32[32,640]{1,0:T(8,128)S(1)}, f32[32,640]{1,0:T(8,128)S(1)}, u32[]{:S(2)}, u32[]{:S(2)}) %collective-permute-start.3) | collective-permute-done | bytes 81952 | tf_op jit(solution)/shard_map/ppermute | solution.py:367
  55.3 0.0 all-to-all-done.1
  55.3 0.0 copy-done.2
  55.3 0.6 copy-done.3
  55.9 0.1 copy-done
  56.0 3.0 %shard_map.86 = (f32[5,125,128]{2,1,0:T(8,128)}, f32[32,640]{1,0:T(8,128)}, f32[32,640]{1,0:T(8,128)}) custom-call(f32[128,640]{1,0:T(8,128)} %bitcast.7, f32[32,640]{1,0:T(8,128)} %copy-done.2, f32[32,640]{1,0:T(8,128)} %copy-done.3, f32[640,128]{1,0:T(8,128)} %get-tuple-element.42.sum_ref, bf16[192,128]{1,0:T(8,128)(2,1)} %get-tuple-element.43.far_ref, ...), custom_call_target="tpu_custom_call" | custom-call | tf_op jit(solution)/shard_map/pallas_call | solution.py:348
  59.0 1.9 %collective-permute-start.4 = (f32[32,640]{1,0:T(8,128)}, f32[32,640]{1,0:T(8,128)S(1)}, u32[]{:S(2)}, u32[]{:S(2)}) collective-permute-start(f32[32,640]{1,0:T(8,128)} %get-tuple-element.48), channel_id=1, source_target_pairs={{0,8},{8,0},{16,24},{24,16},{32,40},{40,32},{48,56},{56,48},{64,72... | collective-permute-start | bytes 245768 | tf_op jit(solution)/shard_map/ppermute | solution.py:375
  60.9 4.4 %collective-permute-start.5 = (f32[32,640]{1,0:T(8,128)}, f32[32,640]{1,0:T(8,128)S(1)}, u32[]{:S(2)}, u32[]{:S(2)}) collective-permute-start(f32[32,640]{1,0:T(8,128)} %get-tuple-element.49), channel_id=1, source_target_pairs={{0,760},{8,16},{16,8},{24,32},{32,24},{40,48},{48,40},{56,64},{64,... | collective-permute-start | bytes 245768 | tf_op jit(solution)/shard_map/ppermute | solution.py:375
  65.3 1.8 %shard_map.87.kept_ref = f32[5,125,192]{2,1,0:T(8,128)} custom-call(f32[5,125,128]{2,1,0:T(8,128)} %get-tuple-element.50.limited_ref, f32[8,128]{1,0:T(8,128)} %get-tuple-element.45.mask_ref), custom_call_target="tpu_custom_call" | custom-call | tf_op jit(solution)/shard_map/pallas_call | solution.py:426
  67.1 0.0 collective-permute-done.4.in0_ref
  67.1 3.2 %collective-permute-done.5.in1_ref = f32[32,640]{1,0:T(8,128)S(1)} collective-permute-done((f32[32,640]{1,0:T(8,128)}, f32[32,640]{1,0:T(8,128)S(1)}, u32[]{:S(2)}, u32[]{:S(2)}) %collective-permute-start.5) | collective-permute-done | bytes 81952 | tf_op jit(solution)/shard_map/ppermute | solution.py:375
  70.2 0.6 copy-done.5
  70.9 1.9 %shard_map.88 = f32[5,125,192]{2,1,0:T(8,128)} custom-call(f32[32,640]{1,0:T(8,128)} %copy-done.4, f32[32,640]{1,0:T(8,128)} %copy-done.5, f32[5,125,192]{2,1,0:T(8,128)} %shard_map.87.kept_ref), custom_call_target="tpu_custom_call", output_to_operand_aliasing={{}: (2, {})} | custom-call | tf_op jit(solution)/shard_map/pallas_call | solution.py:434
  72.7 2.1 %copy.10 = f32[5,125,192]{1,2,0:T(8,128)} copy(f32[5,125,192]{2,1,0:T(8,128)} %shard_map.88) | data formatting | bytes 960000 | tf_op jit(solution)/shard_map/pallas_call | solution.py:434
  (16 shorter events, 0.0 us)
Async XLA Ops:
  2.2 12.8 %copy-start.11 = (f32[32,128]{1,0:T(8,128)S(1)}, f32[32,128]{1,0:T(8,128)}, u32[]{:S(2)}) copy-start(f32[32,128]{1,0:T(8,128)} %get-tuple-element.29) | copy-start | bytes 49156
  2.2 14.8 %copy-start.10 = (f32[32,128]{1,0:T(8,128)S(1)}, f32[32,128]{1,0:T(8,128)}, u32[]{:S(2)}) copy-start(f32[32,128]{1,0:T(8,128)} %get-tuple-element.30) | copy-start | bytes 49156
  2.2 30.6 %all-to-all-start = ((f32[8,16,128]{2,1,0:T(8,128)}), f32[8,16,128]{2,1,0:T(8,128)S(1)}, u32[]{:S(2)}, u32[]{:S(2)}) async-start(f32[8,16,128]{2,1,0:T(8,128)} %bitcast.10), calls=%async_computation | async-start | bytes 131072 | tf_op jit(solution)/shard_map/all_to_all | solution.py:363
  15.0 17.8 %collective-permute-start = (f32[32,128]{1,0:T(8,128)S(1)}, f32[32,128]{1,0:T(8,128)S(1)}, u32[]{:S(2)}, u32[]{:S(2)}) collective-permute-start(f32[32,128]{1,0:T(8,128)S(1)} %copy-done.11), channel_id=1, source_target_pairs={{0,8},{8,0},{16,24},{24,16},{32,40},{40,32},{48,56},{56,48},{64,72... | collective-permute-start | bytes 49160 | tf_op jit(solution)/shard_map/ppermute | solution.py:366
  17.0 15.9 %collective-permute-start.1 = (f32[32,128]{1,0:T(8,128)S(1)}, f32[32,128]{1,0:T(8,128)S(1)}, u32[]{:S(2)}, u32[]{:S(2)}) collective-permute-start(f32[32,128]{1,0:T(8,128)S(1)} %copy-done.10), channel_id=1, source_target_pairs={{0,760},{8,16},{16,8},{24,32},{32,24},{40,48},{48,40},{56,64},{64,... | collective-permute-start | bytes 49160 | tf_op jit(solution)/shard_map/ppermute | solution.py:367
  32.8 0.6 copy-start.6
  32.8 0.6 copy-start.7
  32.8 0.6 copy-start.1
  36.9 7.4 %copy-start.9 = (f32[32,640]{1,0:T(8,128)S(1)}, f32[32,640]{1,0:T(8,128)}, u32[]{:S(2)}) copy-start(f32[32,640]{1,0:T(8,128)} %get-tuple-element.38) | copy-start | bytes 245764
  36.9 9.3 %copy-start.8 = (f32[32,640]{1,0:T(8,128)S(1)}, f32[32,640]{1,0:T(8,128)}, u32[]{:S(2)}) copy-start(f32[32,640]{1,0:T(8,128)} %get-tuple-element.39) | copy-start | bytes 245764
  36.9 18.4 %all-to-all-start.1 = ((f32[8,16,640]{2,1,0:T(8,128)}), f32[8,16,640]{2,1,0:T(8,128)S(1)}, u32[]{:S(2)}, u32[]{:S(2)}) async-start(f32[8,16,640]{2,1,0:T(8,128)} %bitcast.8), calls=%async_computation.1 | async-start | bytes 655360 | tf_op jit(solution)/shard_map/all_to_all | solution.py:363
  44.3 7.8 %collective-permute-start.2 = (f32[32,640]{1,0:T(8,128)S(1)}, f32[32,640]{1,0:T(8,128)S(1)}, u32[]{:S(2)}, u32[]{:S(2)}) collective-permute-start(f32[32,640]{1,0:T(8,128)S(1)} %copy-done.9), channel_id=1, source_target_pairs={{0,8},{8,0},{16,24},{24,16},{32,40},{40,32},{48,56},{56,48},{64,72... | collective-permute-start | bytes 245768 | tf_op jit(solution)/shard_map/ppermute | solution.py:366
  46.2 9.1 %collective-permute-start.3 = (f32[32,640]{1,0:T(8,128)S(1)}, f32[32,640]{1,0:T(8,128)S(1)}, u32[]{:S(2)}, u32[]{:S(2)}) collective-permute-start(f32[32,640]{1,0:T(8,128)S(1)} %copy-done.8), channel_id=1, source_target_pairs={{0,760},{8,16},{16,8},{24,32},{32,24},{40,48},{48,40},{56,64},{64,... | collective-permute-start | bytes 245768 | tf_op jit(solution)/shard_map/ppermute | solution.py:367
  52.1 3.2 %copy-start.2 = (f32[32,640]{1,0:T(8,128)}, f32[32,640]{1,0:T(8,128)S(1)}, u32[]{:S(2)}) copy-start(f32[32,640]{1,0:T(8,128)S(1)} %collective-permute-done.2.pair0_ref) | copy-start | bytes 245764
  55.3 0.6 copy-start.3
  55.3 0.7 copy-start
  59.0 8.0 %collective-permute-start.4 = (f32[32,640]{1,0:T(8,128)}, f32[32,640]{1,0:T(8,128)S(1)}, u32[]{:S(2)}, u32[]{:S(2)}) collective-permute-start(f32[32,640]{1,0:T(8,128)} %get-tuple-element.48), channel_id=1, source_target_pairs={{0,8},{8,0},{16,24},{24,16},{32,40},{40,32},{48,56},{56,48},{64,72... | collective-permute-start | bytes 245768 | tf_op jit(solution)/shard_map/ppermute | solution.py:375
  60.9 9.3 %collective-permute-start.5 = (f32[32,640]{1,0:T(8,128)}, f32[32,640]{1,0:T(8,128)S(1)}, u32[]{:S(2)}, u32[]{:S(2)}) collective-permute-start(f32[32,640]{1,0:T(8,128)} %get-tuple-element.49), channel_id=1, source_target_pairs={{0,760},{8,16},{16,8},{24,32},{32,24},{40,48},{48,40},{56,64},{64,... | collective-permute-start | bytes 245768 | tf_op jit(solution)/shard_map/ppermute | solution.py:375
  67.1 3.2 %copy-start.4 = (f32[32,640]{1,0:T(8,128)}, f32[32,640]{1,0:T(8,128)S(1)}, u32[]{:S(2)}) copy-start(f32[32,640]{1,0:T(8,128)S(1)} %collective-permute-done.4.in0_ref) | copy-start | bytes 245764
  70.2 0.6 copy-start.5

commit v2 on v1

--- a/solution.py
+++ b/solution.py
@@ -266,31 +266,37 @@
 
 
 def inside_kernel(
-    elem_ref, troubled_ref, owner_ref, pos_ref, donor_ref,
-    sum_ref, far_ref, move_ref, mask_ref,
+    elem_ref, troubled_ref, owner_ref, pos_ref, donor_ref, mean_ref, sec_ref,
+    sum_ref, still_ref, far_ref, move_ref, cell_ref, wide_ref,
 ):
     _, grp, left, right, odd = places()
     own = lax.axis_index("wide") * GROUP + grp
     elem = elem_ref[...]
-    cells = jnp.where(troubled_ref[...] == iota((ELEM, 48), 0), 1.0, 0.0).astype(BF16)
-    mask = dot_nt(jnp.ones((8, 48), BF16), cells)[0:1, :]
-    mask_ref[0:1, :] = mask
+    troubled = jnp.sum(
+        jnp.where(troubled_ref[...] == iota((ELEM, 48), 0), 1.0, 0.0), axis=1, keepdims=True
+    )
     local = jnp.where(lax.shift_right_logical(elem, 7) == own, elem & (ELEM - 1), -1)
     rows = iota((ROWS, ELEM), 0)
     elems = iota((ELEM, ELEM), 0)
-    near = jnp.zeros((ELEM, ELEM), F32)
+    near = jnp.where(elems == iota((ELEM, ELEM), 1), 4.0, 0.0)
     far = jnp.zeros((ROWS, ELEM), F32)
     for f in range(FACES):
         near = near + jnp.where(elems == local[f : f + 1, :], 1.0, 0.0)
         far = far + jnp.where(rows == pos_ref[f : f + 1, :], 1.0, 0.0)
-    far_ref[...] = far.astype(BF16)
-    near = near.astype(BF16)
-    hi, mid, lo = thirds(donor_ref[...])
-    sum_ref[...] = dot_nn(hi, near) + dot_nn(mid, near) + dot_nn(lo, near)
+    far_ref[...] = jnp.concatenate([far, jnp.zeros((64, ELEM), F32)], axis=0).T[:, :ROWS].astype(BF16)
+    sum_ref[...] = select_nt(near.T.astype(BF16), donor_ref[...])
+    for v in range(VARS):
+        wide_ref[0:NODES, :] = sec_ref[v]
+        wide_ref[NODES:128, :] = jnp.zeros((3, ELEM), F32)
+        value = wide_ref[...].T
+        mean = jnp.broadcast_to(mean_ref[v : v + 1, :], (ELEM, ELEM)).T
+        still_ref[:, 128 * v : 128 * v + 128] = jnp.where(troubled > 0.5, mean, value)
     owner = owner_ref[...]
-    mask_ref[1:2, :] = jnp.where(owner == own, 1.0, 0.0)
     out0 = jnp.where(odd == 1, left, right)
     out1 = jnp.where(odd == 1, right, left)
+    stays = jnp.where(owner == own, 1.0, 0.0)
+    cell_ref[:, 0:128] = jnp.broadcast_to(troubled, (ELEM, ELEM))
+    cell_ref[:, 128:256] = jnp.broadcast_to(stays, (ELEM, ELEM)).T
     go0 = jnp.where(owner == out0, 1.0, 0.0)
     go1 = jnp.where(owner == out1, 1.0, 0.0)
     go = jnp.concatenate([go0, go1, jnp.zeros((6, ELEM), F32)], axis=0)
@@ -300,57 +306,53 @@
 
 
 def limit_kernel(
-    grp_ref, pair0_ref, pair1_ref, sum_ref, far_ref, move_ref, mask_ref, donor_ref, mean_ref, sec_ref,
-    limited_ref, go0_ref, go1_ref, flat_ref,
+    grp_ref, pair0_ref, pair1_ref, sum_ref, still_ref, far_ref, move_ref, cell_ref,
+    limited_ref, go0_ref, go1_ref,
 ):
     got = jnp.concatenate([grp_ref[...], pair0_ref[...], pair1_ref[...]], axis=0)
     hi, mid, lo = thirds(got)
     far = far_ref[...]
-    turned = far.astype(F32).T.astype(BF16)
-    add = dot_nn(turned, hi) + dot_nn(turned, mid) + dot_nn(turned, lo)
-    total = sum_ref[...] + add.T
-    troubled = mask_ref[0:1, :] > 0.5
-    for v in range(VARS):
-        block = total[128 * v : 128 * v + 128]
-        weights = block[NODES : NODES + 1]
-        own = 4.0 * donor_ref[128 * v + NODES : 128 * v + NODES + 1, :]
-        q = sec_ref[v]
-        inv = 1.0 / (own + weights)
-        value = (own * inv) * q + inv * block[:NODES] + (weights * inv) * mean_ref[v : v + 1, :]
-        value = jnp.where(troubled, value, q)
-        limited_ref[v] = value
-        flat_ref[128 * v : 128 * v + NODES, :] = value
-        flat_ref[128 * v + NODES : 128 * v + 128, :] = jnp.zeros((3, ELEM), F32)
-    moved = select_nt(move_ref[...], flat_ref[...])
+    total = sum_ref[...] + (dot_nn(far, hi) + dot_nn(far, mid) + dot_nn(far, lo))
+    troubled = cell_ref[:, 0:1] > 0.5
+    for v in range(VARS):
+        cols = slice(128 * v, 128 * v + 128)
+        scale = jnp.where(troubled, 1.0 / total[:, 128 * v + NODES : 128 * v + NODES + 1], 0.0)
+        limited_ref[:, cols] = still_ref[:, cols] + scale * total[:, cols]
+    hi, mid, lo = thirds(limited_ref[...])
+    move = move_ref[...]
+    moved = dot_nn(move, hi) + dot_nn(move, mid) + dot_nn(move, lo)
     go0_ref[...] = moved[:MOVE_CAP]
     go1_ref[...] = moved[MOVE_CAP:]
 
 
-def keep_kernel(limited_ref, mask_ref, out_ref):
-    stays = mask_ref[1:2, :] > 0.5
-    for v in range(VARS):
-        out_ref[v] = jnp.where(stays, limited_ref[v], 0.0)
+def keep_kernel(limited_ref, cell_ref, out_ref):
+    stays = cell_ref[:, 128:256] > 0.5
+    for v in range(VARS):
+        out_ref[v] = jnp.where(stays, limited_ref[:, 128 * v : 128 * v + 128], 0.0)[:, :NODES]
 
 
 def arrive_kernel(in0_ref, in1_ref, kept_ref, out_ref):
     odd = lax.rem(lax.axis_index("wide"), 2) == 1
     from_left = jnp.where(odd, in0_ref[...], in1_ref[...])
     from_right = jnp.where(odd, in1_ref[...], in0_ref[...])
-    both = jnp.concatenate([from_left, from_right, jnp.zeros((64, VARS * 128), F32)], axis=0).T
-    for v in range(VARS):
-        out_ref[v] = both[128 * v : 128 * v + NODES]
+    for v in range(VARS):
+        out_ref[v, 0:MOVE_CAP, :] = from_left[:, 128 * v : 128 * v + NODES]
+        out_ref[v, MOVE_CAP:, :] = from_right[:, 128 * v : 128 * v + NODES]
 
 
 VMEM = pl.BlockSpec(memory_space=pltpu.VMEM)
+PARAMS = pltpu.CompilerParams(vmem_limit_bytes=16 * 1024 * 1024)
 
 
 def call(kernel, shapes, scratch, *args):
+    args = [pltpu.with_memory_space_constraint(arg, pltpu.VMEM) for arg in args]
     return pl.pallas_call(
         kernel,
-        out_shape=[jax.ShapeDtypeStruct(shape, dtype) for shape, dtype in shapes],
+        out_shape=[pltpu.VMEM(shape, dtype) for shape, dtype in shapes],
         in_specs=[VMEM] * len(args),
         out_specs=[VMEM] * len(shapes),
         scratch_shapes=[pltpu.VMEM(shape, dtype) for shape, dtype in scratch],
+        compiler_params=PARAMS,
         interpret=INTERPRET,
     )(*args)
 
@@ -408,38 +410,41 @@
         got, got0, got1, base, speeds, near, take, trace, pick, metric, weight,
     )
     got, got0, got1 = exchange(blocks, pair0, pair1)
-    total, far, move, mask = call(
+    total, still, far, move, cell = call(
         inside_kernel,
-        [((cols, ELEM), F32), ((ROWS, ELEM), BF16), ((2 * MOVE_CAP, ELEM), BF16), ((8, ELEM), F32)],
-        [],
-        nbr_elem, troubled, new_owner, pos, donor,
+        [((ELEM, cols), F32), ((ELEM, cols), F32), ((ELEM, ROWS), BF16), ((2 * MOVE_CAP, ELEM), BF16), ((ELEM, 256), F32)],
+        [((128, ELEM), F32)],
+        nbr_elem, troubled, new_owner, pos, donor, mean, sec,
     )
     limited, go0, go1 = call(
         limit_kernel,
-        [((VARS, NODES, ELEM), F32), ((MOVE_CAP, cols), F32), ((MOVE_CAP, cols), F32)],
-        [((cols, ELEM), F32)],
-        got, got0, got1, total, far, move, mask, donor, mean, sec,
+        [((ELEM, cols), F32), ((MOVE_CAP, cols), F32), ((MOVE_CAP, cols), F32)],
+        [],
+        got, got0, got1, total, still, far, move, cell,
     )
     in0, in1 = swap(go0, go1)
-    out_shape = jax.ShapeDtypeStruct((VARS, NODES, ELEM + 2 * MOVE_CAP), F32)
-    whole = lambda shape: pl.BlockSpec(shape, lambda i: (0,) * len(shape))
+    out_shape = jax.ShapeDtypeStruct((VARS, ELEM + 2 * MOVE_CAP, NODES), F32)
+    vmem = lambda x: pltpu.with_memory_space_constraint(x, pltpu.VMEM)
     kept = pl.pallas_call(
         keep_kernel,
         out_shape=out_shape,
         grid=(1,),
-        in_specs=[whole((VARS, NODES, ELEM)), whole((8, ELEM))],
-        out_specs=pl.BlockSpec((VARS, NODES, ELEM), lambda i: (0, 0, 0)),
+        in_specs=[VMEM, VMEM],
+        out_specs=pl.BlockSpec((VARS, ELEM, NODES), lambda i: (0, 0, 0)),
+        compiler_params=PARAMS,
         interpret=INTERPRET,
-    )(limited, mask)
-    return pl.pallas_call(
+    )(vmem(limited), vmem(cell))
+    moved = pl.pallas_call(
         arrive_kernel,
         out_shape=out_shape,
         grid=(1,),
-        in_specs=[whole((MOVE_CAP, cols)), whole((MOVE_CAP, cols)), pl.BlockSpec(memory_space=pl.ANY)],
-        out_specs=pl.BlockSpec((VARS, NODES, ELEM), lambda i: (0, 0, 1)),
+        in_specs=[VMEM, VMEM, pl.BlockSpec(memory_space=pl.ANY)],
+        out_specs=pl.BlockSpec((VARS, 2 * MOVE_CAP, NODES), lambda i: (0, 2, 0)),
         input_output_aliases={2: 0},
+        compiler_params=PARAMS,
         interpret=INTERPRET,
-    )(in0, in1, kept)
+    )(vmem(in0), vmem(in1), kept)
+    return jnp.transpose(moved, (0, 2, 1))
 
 
 def solution(mesh):

time: 75.6 us -> 66.5 us (0.88)
  Pallas kernels: 18.5 us -> 7.93 us
  waiting for transfers between devices: 6.39 us -> 7.84 us
    pallas_call x7, Pallas kernels: 18.5 us -> 7.93 us  [the longest x5 6.48 us: call(): pl.pallas_call(kernel, out_shape=[pltpu.VMEM(shape, dtype) for shape, dty...]
    pallas_call x1 -> x0, local copies, waits for them, and re-layouts: 2.11 us -> none  [shards(): pl.pallas_call(arrive_kernel, out_shape=out_shape, grid=(1,), in_specs=[w...]
    unnamed x24 -> x20, local copies, waits for them, and re-layouts: 2 us -> 3.88 us
  transfers between devices with their start and end apart: 8 -> 8, of which waited for: 2 -> 2; matrix products, arithmetic and copies ran while one was open for 0% -> 0% of each run, Pallas kernels for 11% -> 5%
where the time goes in v2:
time: 66.5 us; the launch traced here: 65.9 us
  starting transfers between devices  46.1 us (69%)
  Pallas kernels  7.93 us (12%)
  waiting for transfers between devices  7.84 us (12%)
  local copies, waits for them, and re-layouts  3.88 us (6%)
    all_to_all x2, starting transfers between devices, exchange(): got = lax.all_to_all(blocks.reshape(GROUP, GROUP_FACES, lanes), 'grp', 0, 0)  20 us
    ppermute x2, starting transfers between devices, exchange(): lax.ppermute(pair1, 'wide', second)  15.8 us
    pallas_call x5, Pallas kernels, call(): pl.pallas_call(kernel, out_shape=[pltpu.VMEM(shape, dtype) for shape, dty...  6.48 us
    ppermute x1, starting transfers between devices, swap(): lax.ppermute(pair1, 'wide', second)  4.4 us
    ppermute x2, starting transfers between devices, exchange(): lax.ppermute(pair0, 'wide', first)  3.95 us
    ppermute x2, waiting for transfers between devices, exchange(): lax.ppermute(pair1, 'wide', second)  3.92 us
    ppermute x1, waiting for transfers between devices, swap(): lax.ppermute(pair1, 'wide', second)  3.91 us
    unnamed x20, local copies, waits for them, and re-layouts  3.88 us
  transfers between devices with their start and end apart: 8, of which 2 were waited for; matrix products, arithmetic and copies ran while one was open for 0% of the time, Pallas kernels for 5%

profile of v2, /device:TPU:8, one launch (start us, length us, event | category | flops | bytes accessed | tf_op | source)
XLA Modules:
  0.0 65.9 jit_solution(3348889304996220829)
XLA Ops:
  0.0 1.0 %copy-done = f32[5,125,128]{2,1,0:T(8,128)S(1)} copy-done((f32[5,125,128]{2,1,0:T(8,128)S(1)}, f32[5,125,128]{2,1,0:T(8,128)}, u32[]{:S(2)}) %copy-start) | copy-done | bytes 320024
  1.0 0.7 %copy-done.4 = s32[6,128]{1,0:T(8,128)S(1)} copy-done((s32[6,128]{1,0:T(8,128)S(1)}, s32[6,128]{1,0:T(8,128)}, u32[]{:S(2)}) %copy-start.4) | copy-done | bytes 3096
  1.7 1.2 %shard_map.82 = (f32[128,128]{1,0:T(8,128)}, f32[32,128]{1,0:T(8,128)S(1)}, f32[32,128]{1,0:T(8,128)S(1)}, f32[128,768]{1,0:T(8,128)S(1)}, bf16[192,128]{1,0:T(8,128)(2,1)S(1)}) custom-call(s32[6,128]{1,0:T(8,128)S(1)} %copy-done.4, f32[5,125,128]{2,1,0:T(8,128)S(1)} %copy-done), custom_call_target="tpu_custom_call" | custom-call | tf_op jit(solution)/shard_map/pallas_call | solution.py:349
  2.9 12.8 %all-to-all-start = ((f32[8,16,128]{2,1,0:T(8,128)}), f32[8,16,128]{2,1,0:T(8,128)S(1)}, u32[]{:S(2)}, u32[]{:S(2)}) async-start(f32[8,16,128]{2,1,0:T(8,128)} %bitcast), calls=%async_computation | async-start | bytes 131072 | tf_op jit(solution)/shard_map/all_to_all | solution.py:365
  15.7 2.0 %collective-permute-start = (f32[32,128]{1,0:T(8,128)S(1)}, f32[32,128]{1,0:T(8,128)S(1)}, u32[]{:S(2)}, u32[]{:S(2)}) collective-permute-start(f32[32,128]{1,0:T(8,128)S(1)} %get-tuple-element.30), channel_id=1, source_target_pairs={{0,8},{8,0},{16,24},{24,16},{32,40},{40,32},{48,56},{56,48},{64,72... | collective-permute-start | bytes 49160 | tf_op jit(solution)/shard_map/ppermute | solution.py:368
  17.7 11.7 %collective-permute-start.1 = (f32[32,128]{1,0:T(8,128)S(1)}, f32[32,128]{1,0:T(8,128)S(1)}, u32[]{:S(2)}, u32[]{:S(2)}) collective-permute-start(f32[32,128]{1,0:T(8,128)S(1)} %get-tuple-element.31), channel_id=1, source_target_pairs={{0,760},{8,16},{16,8},{24,32},{32,24},{40,48},{48,40},{56,64},{64,... | collective-permute-start | bytes 49160 | tf_op jit(solution)/shard_map/ppermute | solution.py:369
  29.5 0.0 copy-start.7
  29.5 0.6 copy-done.7
  30.1 0.9 %copy-done.2 = f32[128,384]{1,0:T(8,128)S(1)} copy-done((f32[128,384]{1,0:T(8,128)S(1)}, f32[128,384]{1,0:T(8,128)}, u32[]{:S(2)}) %copy-start.2) | copy-done | bytes 196632
  31.1 2.2 %shard_map.83 = (f32[5,125,128]{2,1,0:T(8,128)S(1)}, f32[6,25,128]{2,1,0:T(8,128)S(1)}, f32[128,768]{1,0:T(8,128)S(1)}, bf16[192,768]{1,0:T(8,128)(2,1)S(1)}, s32[8,128]{1,0:T(8,128)S(1)}) custom-call(s32[6,128]{1,0:T(8,128)S(1)} %copy-done.5, s32[6,128]{1,0:T(8,128)S(1)} %copy-done.6, f32[5,125,128]{2,1,0:T(8,128)S(1)} %copy-done.1, f32[1,128]{1,0:T(1,128)S(1)} %bitcast.10, ...), custom_call_target="tpu_custom_call" | custom-call | tf_op jit(solution)/shard_map/pallas_call | solution.py:349
  33.2 0.0 collective-permute-done.pair0_ref
  33.2 0.0 collective-permute-done.1.pair1_ref
  33.2 0.0 all-to-all-done
  33.3 2.0 %shard_map.84 = (f32[128,640]{1,0:T(8,128)}, f32[32,640]{1,0:T(8,128)S(1)}, f32[32,640]{1,0:T(8,128)S(1)}, f32[5,125,128]{2,1,0:T(8,128)S(1)}, f32[640,128]{1,0:T(8,128)S(1)}, /*index=5*/f32[8,128]{1,0:T(8,128)S(1)}) custom-call(f32[128,128]{1,0:T(8,128)S(1)} %bitcast.9, f32[32,128]{1,0:T(8,128)S(1)} %collective-permute-done.pair0_ref, ...), custom_call_target="tpu_custom_call" | custom-call | tf_op jit(solution)/shard_map/pallas_call | solution.py:349
  35.2 7.2 %all-to-all-start.1 = ((f32[8,16,640]{2,1,0:T(8,128)}), f32[8,16,640]{2,1,0:T(8,128)S(1)}, u32[]{:S(2)}, u32[]{:S(2)}) async-start(f32[8,16,640]{2,1,0:T(8,128)} %bitcast.3), calls=%async_computation.1 | async-start | bytes 655360 | tf_op jit(solution)/shard_map/all_to_all | solution.py:365
  42.4 1.9 %collective-permute-start.2 = (f32[32,640]{1,0:T(8,128)S(1)}, f32[32,640]{1,0:T(8,128)S(1)}, u32[]{:S(2)}, u32[]{:S(2)}) collective-permute-start(f32[32,640]{1,0:T(8,128)S(1)} %get-tuple-element.39), channel_id=1, source_target_pairs={{0,8},{8,0},{16,24},{24,16},{32,40},{40,32},{48,56},{56,48},{64,72... | collective-permute-start | bytes 245768 | tf_op jit(solution)/shard_map/ppermute | solution.py:368
  44.3 4.0 %collective-permute-start.3 = (f32[32,640]{1,0:T(8,128)S(1)}, f32[32,640]{1,0:T(8,128)S(1)}, u32[]{:S(2)}, u32[]{:S(2)}) collective-permute-start(f32[32,640]{1,0:T(8,128)S(1)} %get-tuple-element.40), channel_id=1, source_target_pairs={{0,760},{8,16},{16,8},{24,32},{32,24},{40,48},{48,40},{56,64},{64,... | collective-permute-start | bytes 245768 | tf_op jit(solution)/shard_map/ppermute | solution.py:369
  48.4 0.0 copy-start.8
  48.4 0.0 copy-start.9
  48.4 0.6 copy-done.8
  49.0 0.0 copy-done.9
  49.1 0.4 shard_map.85
  49.5 0.0 collective-permute-done.2.pair0_ref
  49.5 3.9 %collective-permute-done.3.pair1_ref = f32[32,640]{1,0:T(8,128)S(1)} collective-permute-done((f32[32,640]{1,0:T(8,128)S(1)}, f32[32,640]{1,0:T(8,128)S(1)}, u32[]{:S(2)}, u32[]{:S(2)}) %collective-permute-start.3) | collective-permute-done | bytes 81952 | tf_op jit(solution)/shard_map/ppermute | solution.py:369
  53.4 0.0 all-to-all-done.1
  53.4 0.7 %shard_map.86 = (f32[128,640]{1,0:T(8,128)S(1)}, f32[32,640]{1,0:T(8,128)S(1)}, f32[32,640]{1,0:T(8,128)S(1)}) custom-call(f32[128,640]{1,0:T(8,128)S(1)} %bitcast.8, f32[32,640]{1,0:T(8,128)S(1)} %collective-permute-done.2.pair0_ref, f32[32,640]{1,0:T(8,128)S(1)} %collective-permute-done.3.pair1_ref, f32[128,640]{1,0:T(8,128)S(1)} %get-tuple-element.45.sum_ref, ...), custom_call_target="tpu_custom_call" | custom-call | tf_op jit(solution)/shard_map/pallas_call | solution.py:349
  54.2 1.9 %collective-permute-start.4 = (f32[32,640]{1,0:T(8,128)S(1)}, f32[32,640]{1,0:T(8,128)S(1)}, u32[]{:S(2)}, u32[]{:S(2)}) collective-permute-start(f32[32,640]{1,0:T(8,128)S(1)} %get-tuple-element.50), channel_id=1, source_target_pairs={{0,8},{8,0},{16,24},{24,16},{32,40},{40,32},{48,56},{56,48},{64,72... | collective-permute-start | bytes 245768 | tf_op jit(solution)/shard_map/ppermute | solution.py:377
  56.1 4.4 %collective-permute-start.5 = (f32[32,640]{1,0:T(8,128)S(1)}, f32[32,640]{1,0:T(8,128)S(1)}, u32[]{:S(2)}, u32[]{:S(2)}) collective-permute-start(f32[32,640]{1,0:T(8,128)S(1)} %get-tuple-element.51), channel_id=1, source_target_pairs={{0,760},{8,16},{16,8},{24,32},{32,24},{40,48},{48,40},{56,64},{64,... | collective-permute-start | bytes 245768 | tf_op jit(solution)/shard_map/ppermute | solution.py:377
  60.5 0.8 %shard_map.87.kept_ref = f32[5,192,125]{2,1,0:T(8,128)} custom-call(f32[128,640]{1,0:T(8,128)S(1)} %get-tuple-element.52.limited_ref, f32[128,256]{1,0:T(8,128)S(1)} %get-tuple-element.49.cell_ref), custom_call_target="tpu_custom_call" | custom-call | tf_op jit(solution)/shard_map/pallas_call | solution.py:428
  61.3 0.0 collective-permute-done.4.in0_ref
  61.3 3.9 %collective-permute-done.5.in1_ref = f32[32,640]{1,0:T(8,128)S(1)} collective-permute-done((f32[32,640]{1,0:T(8,128)S(1)}, f32[32,640]{1,0:T(8,128)S(1)}, u32[]{:S(2)}, u32[]{:S(2)}) %collective-permute-start.5) | collective-permute-done | bytes 81952 | tf_op jit(solution)/shard_map/ppermute | solution.py:377
  65.2 0.7 %shard_map.88 = f32[5,192,125]{2,1,0:T(8,128)} custom-call(f32[32,640]{1,0:T(8,128)S(1)} %collective-permute-done.4.in0_ref, f32[32,640]{1,0:T(8,128)S(1)} %collective-permute-done.5.in1_ref, f32[5,192,125]{2,1,0:T(8,128)} %shard_map.87.kept_ref), custom_call_target="tpu_custom_call", output_to_operand_aliasing={{}: (2, {})} | custom-call | tf_op jit(solution)/shard_map/pallas_call | solution.py:437
  (11 shorter events, 0.0 us)
Async XLA Ops:
  0.0 1.0 %copy-start = (f32[5,125,128]{2,1,0:T(8,128)S(1)}, f32[5,125,128]{2,1,0:T(8,128)}, u32[]{:S(2)}) copy-start(f32[5,125,128]{2,1,0:T(8,128)} %state_ref.3) | copy-start | bytes 960004
  1.0 0.7 %copy-start.4 = (s32[6,128]{1,0:T(8,128)S(1)}, s32[6,128]{1,0:T(8,128)}, u32[]{:S(2)}) copy-start(s32[6,128]{1,0:T(8,128)} %elem_ref.5) | copy-start | bytes 9220
  1.7 27.8 %copy-start.1 = (f32[5,125,128]{2,1,0:T(8,128)S(1)}, f32[5,125,128]{2,1,0:T(8,128)}, u32[]{:S(2)}) copy-start(f32[5,125,128]{2,1,0:T(8,128)} %state_ref.3) | copy-start | bytes 960004
  2.9 26.6 %copy-start.6 = (s32[6,128]{1,0:T(8,128)S(1)}, s32[6,128]{1,0:T(8,128)}, u32[]{:S(2)}) copy-start(s32[6,128]{1,0:T(8,128)} %face_ref.1) | copy-start | bytes 9220
  2.9 30.4 %all-to-all-start = ((f32[8,16,128]{2,1,0:T(8,128)}), f32[8,16,128]{2,1,0:T(8,128)S(1)}, u32[]{:S(2)}, u32[]{:S(2)}) async-start(f32[8,16,128]{2,1,0:T(8,128)} %bitcast), calls=%async_computation | async-start | bytes 131072 | tf_op jit(solution)/shard_map/all_to_all | solution.py:365
  15.7 13.8 %copy-start.5 = (s32[6,128]{1,0:T(8,128)S(1)}, s32[6,128]{1,0:T(8,128)}, u32[]{:S(2)}) copy-start(s32[6,128]{1,0:T(8,128)} %elem_ref.5) | copy-start | bytes 9220
  15.7 17.5 %collective-permute-start = (f32[32,128]{1,0:T(8,128)S(1)}, f32[32,128]{1,0:T(8,128)S(1)}, u32[]{:S(2)}, u32[]{:S(2)}) collective-permute-start(f32[32,128]{1,0:T(8,128)S(1)} %get-tuple-element.30), channel_id=1, source_target_pairs={{0,8},{8,0},{16,24},{24,16},{32,40},{40,32},{48,56},{56,48},{64,72... | collective-permute-start | bytes 49160 | tf_op jit(solution)/shard_map/ppermute | solution.py:368
  17.7 15.5 %collective-permute-start.1 = (f32[32,128]{1,0:T(8,128)S(1)}, f32[32,128]{1,0:T(8,128)S(1)}, u32[]{:S(2)}, u32[]{:S(2)}) collective-permute-start(f32[32,128]{1,0:T(8,128)S(1)} %get-tuple-element.31), channel_id=1, source_target_pairs={{0,760},{8,16},{16,8},{24,32},{32,24},{40,48},{48,40},{56,64},{64,... | collective-permute-start | bytes 49160 | tf_op jit(solution)/shard_map/ppermute | solution.py:369
  29.5 0.7 copy-start.7
  30.1 0.9 %copy-start.2 = (f32[128,384]{1,0:T(8,128)S(1)}, f32[128,384]{1,0:T(8,128)}, u32[]{:S(2)}) copy-start(f32[128,384]{1,0:T(8,128)} %constant.4.clone.diff_ref) | copy-start | bytes 589828
  31.1 2.2 %copy-start.3 = (f32[125,128]{1,0:T(8,128)S(1)}, f32[125,128]{1,0:T(8,128)}, u32[]{:S(2)}) copy-start(f32[125,128]{1,0:T(8,128)} %constant.5.clone.weight_ref) | copy-start | bytes 192004
  35.2 18.2 %all-to-all-start.1 = ((f32[8,16,640]{2,1,0:T(8,128)}), f32[8,16,640]{2,1,0:T(8,128)S(1)}, u32[]{:S(2)}, u32[]{:S(2)}) async-start(f32[8,16,640]{2,1,0:T(8,128)} %bitcast.3), calls=%async_computation.1 | async-start | bytes 655360 | tf_op jit(solution)/shard_map/all_to_all | solution.py:365
  42.4 7.1 %collective-permute-start.2 = (f32[32,640]{1,0:T(8,128)S(1)}, f32[32,640]{1,0:T(8,128)S(1)}, u32[]{:S(2)}, u32[]{:S(2)}) collective-permute-start(f32[32,640]{1,0:T(8,128)S(1)} %get-tuple-element.39), channel_id=1, source_target_pairs={{0,8},{8,0},{16,24},{24,16},{32,40},{40,32},{48,56},{56,48},{64,72... | collective-permute-start | bytes 245768 | tf_op jit(solution)/shard_map/ppermute | solution.py:368
  44.3 9.1 %collective-permute-start.3 = (f32[32,640]{1,0:T(8,128)S(1)}, f32[32,640]{1,0:T(8,128)S(1)}, u32[]{:S(2)}, u32[]{:S(2)}) collective-permute-start(f32[32,640]{1,0:T(8,128)S(1)} %get-tuple-element.40), channel_id=1, source_target_pairs={{0,760},{8,16},{16,8},{24,32},{32,24},{40,48},{48,40},{56,64},{64,... | collective-permute-start | bytes 245768 | tf_op jit(solution)/shard_map/ppermute | solution.py:369
  48.4 0.7 copy-start.8
  48.4 0.7 %copy-start.9 = (s32[128]{0:T(128)S(1)}, s32[128]{0:T(128)}, u32[]{:S(2)}) copy-start(s32[128]{0:T(128)} %param.13) | copy-start | bytes 1540
  54.2 7.1 %collective-permute-start.4 = (f32[32,640]{1,0:T(8,128)S(1)}, f32[32,640]{1,0:T(8,128)S(1)}, u32[]{:S(2)}, u32[]{:S(2)}) collective-permute-start(f32[32,640]{1,0:T(8,128)S(1)} %get-tuple-element.50), channel_id=1, source_target_pairs={{0,8},{8,0},{16,24},{24,16},{32,40},{40,32},{48,56},{56,48},{64,72... | collective-permute-start | bytes 245768 | tf_op jit(solution)/shard_map/ppermute | solution.py:377
  56.1 9.1 %collective-permute-start.5 = (f32[32,640]{1,0:T(8,128)S(1)}, f32[32,640]{1,0:T(8,128)S(1)}, u32[]{:S(2)}, u32[]{:S(2)}) collective-permute-start(f32[32,640]{1,0:T(8,128)S(1)} %get-tuple-element.51), channel_id=1, source_target_pairs={{0,760},{8,16},{16,8},{24,32},{32,24},{40,48},{48,40},{56,64},{64,... | collective-permute-start | bytes 245768 | tf_op jit(solution)/shard_map/ppermute | solution.py:377

commit v3 on v2

--- a/solution.py
+++ b/solution.py
@@ -1,4 +1,3 @@
-import functools
 import math
 
 import jax
@@ -8,6 +7,7 @@
 from jax.experimental import pallas as pl
 from jax.experimental.pallas import tpu as pltpu
 from jax.sharding import PartitionSpec as P
+
 
 GROUP_FACES = 16
 WIDE_FACES = 32
@@ -118,7 +118,31 @@
     return onehot(iota((ELEM, ELEM), 0) < iota((ELEM, ELEM), 1))
 
 
-def pack_kernel(elem_ref, state_ref, grp_ref, pair0_ref, pair1_ref, trace_ref, pick_ref, s_ref):
+def pack_kernel(
+    elem_hbm, state_hbm, face_hbm, metric_hbm, troubled_hbm, owner_hbm, diff_hbm, weight_hbm,
+    grp_ref, pair0_ref, pair1_ref, trace_ref, pick_ref,
+    elem_ref, state_ref, face_ref, metric_ref, troubled_ref, owner_ref, diff_ref, weight_ref,
+    s_ref, sems,
+):
+    first = pltpu.make_async_copy(elem_hbm, elem_ref, sems.at[0])
+    first.start()
+    second = pltpu.make_async_copy(state_hbm, state_ref, sems.at[1])
+    second.start()
+    later = []
+    for k, (source, target) in enumerate(
+        (
+            (face_hbm, face_ref),
+            (metric_hbm, metric_ref),
+            (troubled_hbm, troubled_ref),
+            (owner_hbm, owner_ref),
+            (diff_hbm, diff_ref),
+            (weight_hbm, weight_ref),
+        )
+    ):
+        copy = pltpu.make_async_copy(source, target, sems.at[2 + k])
+        copy.start()
+        later.append(copy)
+    first.wait()
     cat = categories(elem_ref[...])
     kinds = iota((16, ELEM), 0)
     hot = [jnp.where(cat[f : f + 1, :] == kinds, 1.0, 0.0) for f in range(FACES)]
@@ -136,6 +160,7 @@
         pick = pick + chosen
         s_ref[:, f * ELEM : (f + 1) * ELEM] = chosen.astype(BF16)
     pick_ref[...] = pick.astype(BF16)
+    second.wait()
     for f in range(FACES):
         for v in range(VARS):
             for first, count, stride, place in face_rows(f):
@@ -147,6 +172,8 @@
     grp_ref[...] = sent[:GROUP_ROWS]
     pair0_ref[...] = sent[PAIR0:PAIR1]
     pair1_ref[...] = sent[PAIR1:]
+    for copy in later:
+        copy.wait()
 
 
 def primitives(u):
@@ -357,24 +384,19 @@
     )(*args)
 
 
-def exchange(blocks, pair0, pair1):
-    size = lax.axis_size("wide")
-    first = [(i, i ^ 1) for i in range(size)]
-    second = [(i, (i + 1) % size if i % 2 else (i - 1) % size) for i in range(size)]
-    lanes = blocks.shape[1]
-    got = lax.all_to_all(blocks.reshape(GROUP, GROUP_FACES, lanes), "grp", 0, 0)
-    return (
-        got.reshape(GROUP_ROWS, lanes),
-        lax.ppermute(pair0, "wide", first),
-        lax.ppermute(pair1, "wide", second),
-    )
-
-
 def swap(pair0, pair1):
     size = lax.axis_size("wide")
     first = [(i, i ^ 1) for i in range(size)]
     second = [(i, (i + 1) % size if i % 2 else (i - 1) % size) for i in range(size)]
-    return lax.ppermute(pair0, "wide", first), lax.ppermute(pair1, "wide", second)
+    got1 = lax.ppermute(pair1, "wide", second)
+    got0 = lax.ppermute(pair0, "wide", first)
+    return got0, got1
+
+
+def exchange(blocks, pair0, pair1):
+    lanes = blocks.shape[1]
+    got = lax.all_to_all(blocks.reshape(GROUP, GROUP_FACES, lanes), "grp", 0, 0)
+    return (got.reshape(GROUP_ROWS, lanes), *swap(pair0, pair1))
 
 
 def shards(state, metric, nbr_elem, nbr_face, troubled, new_owner):
@@ -390,12 +412,25 @@
     cols = VARS * 128
     wide_lanes = FACES * ELEM
 
-    blocks, pair0, pair1, trace, pick = call(
+    loaded = [
+        pltpu.with_memory_space_constraint(x, pltpu.HBM)
+        for x in (nbr_elem, state, nbr_face, metric, troubled, new_owner, diff, weight)
+    ]
+    blocks, pair0, pair1, trace, pick, nbr_elem, state, nbr_face, metric, troubled, new_owner, diff, weight = pl.pallas_call(
         pack_kernel,
-        [((GROUP_ROWS, 128), F32), ((32, 128), F32), ((32, 128), F32), ((128, wide_lanes), F32), ((ROWS, ELEM), BF16)],
-        [((ROWS, wide_lanes), BF16)],
-        nbr_elem, state,
-    )
+        out_shape=[
+            pltpu.VMEM(shape, dtype)
+            for shape, dtype in (
+                ((GROUP_ROWS, 128), F32), ((32, 128), F32), ((32, 128), F32), ((128, wide_lanes), F32), ((ROWS, ELEM), BF16)
+            )
+        ]
+        + [pltpu.VMEM(x.shape, x.dtype) for x in loaded],
+        in_specs=[pl.BlockSpec(memory_space=pltpu.HBM)] * len(loaded),
+        out_specs=[VMEM] * (5 + len(loaded)),
+        scratch_shapes=[pltpu.VMEM((ROWS, wide_lanes), BF16), pltpu.SemaphoreType.DMA((len(loaded),))],
+        compiler_params=PARAMS,
+        interpret=INTERPRET,
+    )(*loaded)
     got, got0, got1 = exchange(blocks, pair0, pair1)
     base, speeds, near, take, pos = call(
         local_kernel,

time: 66.5 us -> 63.8 us (0.959)
  local copies, waits for them, and re-layouts: 3.88 us -> 0 us
  starting transfers between devices: 46.1 us -> 48.6 us
  waiting for transfers between devices: 7.84 us -> 5.72 us
  Pallas kernels: 7.93 us -> 8.88 us
    unnamed x20 -> x0, local copies, waits for them, and re-layouts: 3.88 us -> none
    ppermute x6, starting transfers between devices: 26 us -> 28.7 us  [the longest x3 23 us: swap(): got1 = lax.ppermute(pair1, 'wide', second)]
    pallas_call x0 -> x1, Pallas kernels: none -> 2.13 us  [shards(): pl.pallas_call(pack_kernel, out_shape=[pltpu.VMEM(shape, dtype) for shape...]
    ppermute x6, waiting for transfers between devices: 7.84 us -> 5.71 us  [the longest x3 5.7 us: swap(): got1 = lax.ppermute(pair1, 'wide', second)]
    pallas_call x5 -> x4, Pallas kernels: 6.48 us -> 5.29 us  [call(): pl.pallas_call(kernel, out_shape=[pltpu.VMEM(shape, dtype) for shape, dty...]
where the time goes in v3:
time: 63.8 us; the launch traced here: 63.3 us
  starting transfers between devices  48.6 us (76%)
  Pallas kernels  8.88 us (14%)
  waiting for transfers between devices  5.72 us (9%)
    ppermute x3, starting transfers between devices, swap(): got1 = lax.ppermute(pair1, 'wide', second)  23 us
    all_to_all x2, starting transfers between devices, exchange(): got = lax.all_to_all(blocks.reshape(GROUP, GROUP_FACES, lanes), 'grp', 0, 0)  19.9 us
    ppermute x3, starting transfers between devices, swap(): got0 = lax.ppermute(pair0, 'wide', first)  5.73 us
    ppermute x3, waiting for transfers between devices, swap(): got1 = lax.ppermute(pair1, 'wide', second)  5.7 us
    pallas_call x4, Pallas kernels, call(): pl.pallas_call(kernel, out_shape=[pltpu.VMEM(shape, dtype) for shape, dty...  5.29 us
    pallas_call x1, Pallas kernels, shards(): pl.pallas_call(pack_kernel, out_shape=[pltpu.VMEM(shape, dtype) for shape...  2.13 us
  transfers between devices with their start and end apart: 8, of which 2 were waited for; matrix products, arithmetic and copies ran while one was open for 0% of the time, Pallas kernels for 5%

profile of v3, /device:TPU:8, one launch (start us, length us, event | category | flops | bytes accessed | tf_op | source)
XLA Modules:
  0.0 63.3 jit_solution(15106693115391223704)
XLA Ops:
  0.0 2.1 %shard_map.82 = (f32[128,128]{1,0:T(8,128)}, f32[32,128]{1,0:T(8,128)S(1)}, f32[32,128]{1,0:T(8,128)S(1)}, f32[128,768]{1,0:T(8,128)S(1)}, bf16[192,128]{1,0:T(8...) custom-call(s32[6,128]{1,0:T(8,128)} %elem_hbm.1, ...), custom_call_target="tpu_custom_call" | custom-call | tf_op jit(solution)/shard_map/pallas_call | solution.py:419
  2.1 12.7 %all-to-all-start = ((f32[8,16,128]{2,1,0:T(8,128)}), f32[8,16,128]{2,1,0:T(8,128)S(1)}, u32[]{:S(2)}, u32[]{:S(2)}) async-start(f32[8,16,128]{2,1,0:T(8,128)} %bitcast.3), calls=%async_computation | async-start | bytes 131072 | tf_op jit(solution)/shard_map/all_to_all | solution.py:398
  14.8 1.9 %collective-permute-start = (f32[32,128]{1,0:T(8,128)S(1)}, f32[32,128]{1,0:T(8,128)S(1)}, u32[]{:S(2)}, u32[]{:S(2)}) collective-permute-start(f32[32,128]{1,0:T(8,128)S(1)} %get-tuple-element.38), channel_id=1, source_target_pairs={{0,8},{8,0},{16,24},{24,16},{32,40},{40,32},{48,56},{56,48},{64,72... | collective-permute-start | bytes 49160 | tf_op jit(solution)/shard_map/ppermute | solution.py:392
  16.8 11.7 %collective-permute-start.1 = (f32[32,128]{1,0:T(8,128)S(1)}, f32[32,128]{1,0:T(8,128)S(1)}, u32[]{:S(2)}, u32[]{:S(2)}) collective-permute-start(f32[32,128]{1,0:T(8,128)S(1)} %get-tuple-element.39), channel_id=1, source_target_pairs={{0,760},{8,16},{16,8},{24,32},{32,24},{40,48},{48,40},{56,64},{64,... | collective-permute-start | bytes 49160 | tf_op jit(solution)/shard_map/ppermute | solution.py:391
  28.5 2.2 %shard_map.83 = (f32[5,125,128]{2,1,0:T(8,128)S(1)}, f32[6,25,128]{2,1,0:T(8,128)S(1)}, f32[128,768]{1,0:T(8,128)S(1)}, bf16[192,768]{1,0:T(8,128)(2,1)S(1)}, s32[8,128]{1,0:T(8,128)S(1)}) custom-call(s32[6,128]{1,0:T(8,128)S(1)} %get-tuple-element.40.elem_ref, s32[6,128]{1,0:T(8,128)S(1)} %get-tuple-element.41.face_ref, ...), custom_call_target="tpu_custom_call" | custom-call | tf_op jit(solution)/shard_map/pallas_call | solution.py:376
  30.7 0.0 collective-permute-done.pair0_ref
  30.7 0.0 collective-permute-done.1.pair1_ref
  30.7 0.0 all-to-all-done
  30.7 2.0 %shard_map.84 = (f32[128,640]{1,0:T(8,128)}, f32[32,640]{1,0:T(8,128)S(1)}, f32[32,640]{1,0:T(8,128)S(1)}, f32[5,125,128]{2,1,0:T(8,128)S(1)}, f32[640,128]{1,0:T(8,128)S(1)}, /*index=5*/f32[8,128]{1,0:T(8,128)S(1)}) custom-call(f32[128,128]{1,0:T(8,128)S(1)} %bitcast.9, f32[32,128]{1,0:T(8,128)S(1)} %collective-permute-done.pair0_ref, ...), custom_call_target="tpu_custom_call" | custom-call | tf_op jit(solution)/shard_map/pallas_call | solution.py:376
  32.7 7.2 %all-to-all-start.1 = ((f32[8,16,640]{2,1,0:T(8,128)}), f32[8,16,640]{2,1,0:T(8,128)S(1)}, u32[]{:S(2)}, u32[]{:S(2)}) async-start(f32[8,16,640]{2,1,0:T(8,128)} %bitcast.5), calls=%async_computation.1 | async-start | bytes 655360 | tf_op jit(solution)/shard_map/all_to_all | solution.py:398
  39.9 1.9 %collective-permute-start.2 = (f32[32,640]{1,0:T(8,128)S(1)}, f32[32,640]{1,0:T(8,128)S(1)}, u32[]{:S(2)}, u32[]{:S(2)}) collective-permute-start(f32[32,640]{1,0:T(8,128)S(1)} %get-tuple-element.53), channel_id=1, source_target_pairs={{0,8},{8,0},{16,24},{24,16},{32,40},{40,32},{48,56},{56,48},{64,72... | collective-permute-start | bytes 245768 | tf_op jit(solution)/shard_map/ppermute | solution.py:392
  41.8 5.6 %collective-permute-start.3 = (f32[32,640]{1,0:T(8,128)S(1)}, f32[32,640]{1,0:T(8,128)S(1)}, u32[]{:S(2)}, u32[]{:S(2)}) collective-permute-start(f32[32,640]{1,0:T(8,128)S(1)} %get-tuple-element.54), channel_id=1, source_target_pairs={{0,760},{8,16},{16,8},{24,32},{32,24},{40,48},{48,40},{56,64},{64,... | collective-permute-start | bytes 245768 | tf_op jit(solution)/shard_map/ppermute | solution.py:391
  47.4 0.4 shard_map.85
  47.8 0.0 collective-permute-done.2.pair0_ref
  47.9 3.0 %collective-permute-done.3.pair1_ref = f32[32,640]{1,0:T(8,128)S(1)} collective-permute-done((f32[32,640]{1,0:T(8,128)S(1)}, f32[32,640]{1,0:T(8,128)S(1)}, u32[]{:S(2)}, u32[]{:S(2)}) %collective-permute-start.3) | collective-permute-done | bytes 81952 | tf_op jit(solution)/shard_map/ppermute | solution.py:391
  50.9 0.0 all-to-all-done.1
  50.9 0.7 %shard_map.86 = (f32[128,640]{1,0:T(8,128)S(1)}, f32[32,640]{1,0:T(8,128)S(1)}, f32[32,640]{1,0:T(8,128)S(1)}) custom-call(f32[128,640]{1,0:T(8,128)S(1)} %bitcast.8, f32[32,640]{1,0:T(8,128)S(1)} %collective-permute-done.2.pair0_ref, f32[32,640]{1,0:T(8,128)S(1)} %collective-permute-done.3.pair1_ref, f32[128,640]{1,0:T(8,128)S(1)} %get-tuple-element.61.sum_ref, ...), custom_call_target="tpu_custom_call" | custom-call | tf_op jit(solution)/shard_map/pallas_call | solution.py:376
  51.6 1.9 %collective-permute-start.4 = (f32[32,640]{1,0:T(8,128)S(1)}, f32[32,640]{1,0:T(8,128)S(1)}, u32[]{:S(2)}, u32[]{:S(2)}) collective-permute-start(f32[32,640]{1,0:T(8,128)S(1)} %get-tuple-element.66), channel_id=1, source_target_pairs={{0,8},{8,0},{16,24},{24,16},{32,40},{40,32},{48,56},{56,48},{64,72... | collective-permute-start | bytes 245768 | tf_op jit(solution)/shard_map/ppermute | solution.py:392
  53.5 5.6 %collective-permute-start.5 = (f32[32,640]{1,0:T(8,128)S(1)}, f32[32,640]{1,0:T(8,128)S(1)}, u32[]{:S(2)}, u32[]{:S(2)}) collective-permute-start(f32[32,640]{1,0:T(8,128)S(1)} %get-tuple-element.67), channel_id=1, source_target_pairs={{0,760},{8,16},{16,8},{24,32},{32,24},{40,48},{48,40},{56,64},{64,... | collective-permute-start | bytes 245768 | tf_op jit(solution)/shard_map/ppermute | solution.py:391
  59.1 0.8 %shard_map.87.kept_ref = f32[5,192,125]{2,1,0:T(8,128)} custom-call(f32[128,640]{1,0:T(8,128)S(1)} %get-tuple-element.68.limited_ref, f32[128,256]{1,0:T(8,128)S(1)} %get-tuple-element.65.cell_ref), custom_call_target="tpu_custom_call" | custom-call | tf_op jit(solution)/shard_map/pallas_call | solution.py:463
  59.9 0.0 collective-permute-done.4.in0_ref
  59.9 2.7 %collective-permute-done.5.in1_ref = f32[32,640]{1,0:T(8,128)S(1)} collective-permute-done((f32[32,640]{1,0:T(8,128)S(1)}, f32[32,640]{1,0:T(8,128)S(1)}, u32[]{:S(2)}, u32[]{:S(2)}) %collective-permute-start.5) | collective-permute-done | bytes 81952 | tf_op jit(solution)/shard_map/ppermute | solution.py:391
  62.6 0.7 %shard_map.88 = f32[5,192,125]{2,1,0:T(8,128)} custom-call(f32[32,640]{1,0:T(8,128)S(1)} %collective-permute-done.4.in0_ref, f32[32,640]{1,0:T(8,128)S(1)} %collective-permute-done.5.in1_ref, f32[5,192,125]{2,1,0:T(8,128)} %shard_map.87.kept_ref), custom_call_target="tpu_custom_call", output_to_operand_aliasing={{}: (2, {})} | custom-call | tf_op jit(solution)/shard_map/pallas_call | solution.py:472
Async XLA Ops:
  2.1 28.6 %all-to-all-start = ((f32[8,16,128]{2,1,0:T(8,128)}), f32[8,16,128]{2,1,0:T(8,128)S(1)}, u32[]{:S(2)}, u32[]{:S(2)}) async-start(f32[8,16,128]{2,1,0:T(8,128)} %bitcast.3), calls=%async_computation | async-start | bytes 131072 | tf_op jit(solution)/shard_map/all_to_all | solution.py:398
  14.8 15.8 %collective-permute-start = (f32[32,128]{1,0:T(8,128)S(1)}, f32[32,128]{1,0:T(8,128)S(1)}, u32[]{:S(2)}, u32[]{:S(2)}) collective-permute-start(f32[32,128]{1,0:T(8,128)S(1)} %get-tuple-element.38), channel_id=1, source_target_pairs={{0,8},{8,0},{16,24},{24,16},{32,40},{40,32},{48,56},{56,48},{64,72... | collective-permute-start | bytes 49160 | tf_op jit(solution)/shard_map/ppermute | solution.py:392
  16.8 13.9 %collective-permute-start.1 = (f32[32,128]{1,0:T(8,128)S(1)}, f32[32,128]{1,0:T(8,128)S(1)}, u32[]{:S(2)}, u32[]{:S(2)}) collective-permute-start(f32[32,128]{1,0:T(8,128)S(1)} %get-tuple-element.39), channel_id=1, source_target_pairs={{0,760},{8,16},{16,8},{24,32},{32,24},{40,48},{48,40},{56,64},{64,... | collective-permute-start | bytes 49160 | tf_op jit(solution)/shard_map/ppermute | solution.py:391
  32.7 18.2 %all-to-all-start.1 = ((f32[8,16,640]{2,1,0:T(8,128)}), f32[8,16,640]{2,1,0:T(8,128)S(1)}, u32[]{:S(2)}, u32[]{:S(2)}) async-start(f32[8,16,640]{2,1,0:T(8,128)} %bitcast.5), calls=%async_computation.1 | async-start | bytes 655360 | tf_op jit(solution)/shard_map/all_to_all | solution.py:398
  39.9 8.0 %collective-permute-start.2 = (f32[32,640]{1,0:T(8,128)S(1)}, f32[32,640]{1,0:T(8,128)S(1)}, u32[]{:S(2)}, u32[]{:S(2)}) collective-permute-start(f32[32,640]{1,0:T(8,128)S(1)} %get-tuple-element.53), channel_id=1, source_target_pairs={{0,8},{8,0},{16,24},{24,16},{32,40},{40,32},{48,56},{56,48},{64,72... | collective-permute-start | bytes 245768 | tf_op jit(solution)/shard_map/ppermute | solution.py:392
  41.8 9.1 %collective-permute-start.3 = (f32[32,640]{1,0:T(8,128)S(1)}, f32[32,640]{1,0:T(8,128)S(1)}, u32[]{:S(2)}, u32[]{:S(2)}) collective-permute-start(f32[32,640]{1,0:T(8,128)S(1)} %get-tuple-element.54), channel_id=1, source_target_pairs={{0,760},{8,16},{16,8},{24,32},{32,24},{40,48},{48,40},{56,64},{64,... | collective-permute-start | bytes 245768 | tf_op jit(solution)/shard_map/ppermute | solution.py:391
  51.6 8.3 %collective-permute-start.4 = (f32[32,640]{1,0:T(8,128)S(1)}, f32[32,640]{1,0:T(8,128)S(1)}, u32[]{:S(2)}, u32[]{:S(2)}) collective-permute-start(f32[32,640]{1,0:T(8,128)S(1)} %get-tuple-element.66), channel_id=1, source_target_pairs={{0,8},{8,0},{16,24},{24,16},{32,40},{40,32},{48,56},{56,48},{64,72... | collective-permute-start | bytes 245768 | tf_op jit(solution)/shard_map/ppermute | solution.py:392
  53.5 9.1 %collective-permute-start.5 = (f32[32,640]{1,0:T(8,128)S(1)}, f32[32,640]{1,0:T(8,128)S(1)}, u32[]{:S(2)}, u32[]{:S(2)}) collective-permute-start(f32[32,640]{1,0:T(8,128)S(1)} %get-tuple-element.67), channel_id=1, source_target_pairs={{0,760},{8,16},{16,8},{24,32},{32,24},{40,48},{48,40},{56,64},{64,... | collective-permute-start | bytes 245768 | tf_op jit(solution)/shard_map/ppermute | solution.py:391

commit v4 on v2

v4 whole, which is shorter than its diff:
```python
import math

import jax
import jax.numpy as jnp
import numpy as np
from jax import lax
from jax.experimental import pallas as pl
from jax.experimental.pallas import tpu as pltpu
from jax.sharding import PartitionSpec as P


GROUP_FACES = 16
WIDE_FACES = 32
MOVE_CAP = 32
SECTION_STEP = 0.01
LIFT_GAIN = 10.0

ELEM = 128
VARS = 5
NODES = 125
FACES = 6
GROUP = 8
GROUP_ROWS = GROUP * GROUP_FACES
PAIR1 = GROUP_ROWS + WIDE_FACES
ROWS = GROUP_ROWS + 2 * WIDE_FACES
LOCAL = 10

F32 = jnp.float32
BF16 = jnp.bfloat16
I32 = jnp.int32
INTERPRET = False


def gll_tables():
    root = math.sqrt(3.0 / 7.0)
    points = np.array([-1.0, -root, 0.0, root, 1.0])
    weights = np.array([0.1, 49.0 / 90.0, 32.0 / 45.0, 49.0 / 90.0, 0.1])
    bary = np.array(
        [1.0 / np.prod([points[j] - points[k] for k in range(5) if k != j]) for j in range(5)]
    )
    deriv = np.zeros((5, 5))
    for i in range(5):
        for j in range(5):
            if i != j:
                deriv[i, j] = bary[j] / bary[i] / (points[i] - points[j])
        deriv[i, i] = -np.sum(deriv[i])
    ident = np.eye(5)
    diffs = [
        np.kron(np.kron(deriv, ident), ident),
        np.kron(np.kron(ident, deriv), ident),
        np.kron(np.kron(ident, ident), deriv),
    ]
    cell_weights = np.kron(np.kron(weights, weights), weights) / 8.0
    return diffs, cell_weights


def halves_of(table):
    hi = table.astype(jnp.bfloat16)
    return hi, (table - hi.astype(np.float32)).astype(jnp.bfloat16)


def face_rows(face):
    if face < 2:
        return [(100 * face, 25, 1, 0)]
    if face < 4:
        return [(25 * a + 20 * (face - 2), 5, 1, 5 * a) for a in range(5)]
    return [(4 * (face - 4), 25, 5, 0)]


def rows_at(first, count, stride):
    return pl.ds(first, count) if stride == 1 else pl.ds(first, count, stride=stride)


def thirds(x):
    hi = x.astype(BF16)
    rest = x - hi.astype(F32)
    mid = rest.astype(BF16)
    lo = (rest - mid.astype(F32)).astype(BF16)
    return hi, mid, lo


def halves(x):
    hi = x.astype(BF16)
    return hi, (x - hi.astype(F32)).astype(BF16)


def dot_nn(a, b):
    return lax.dot_general(a, b, (((1,), (0,)), ((), ())), preferred_element_type=F32)


def dot_nt(a, b):
    return lax.dot_general(a, b, (((1,), (1,)), ((), ())), preferred_element_type=F32)


def select_nt(onehot, values):
    hi, mid, lo = thirds(values)
    return dot_nt(onehot, hi) + dot_nt(onehot, mid) + dot_nt(onehot, lo)


def iota(shape, dim):
    return lax.broadcasted_iota(I32, shape, dim)


def onehot(mask):
    return jnp.where(mask, 1.0, 0.0).astype(BF16)


def places():
    wide = lax.axis_index("wide")
    grp = lax.axis_index("grp")
    size = lax.axis_size("wide")
    left = lax.rem(wide + size - 1, size) * GROUP + grp
    right = lax.rem(wide + 1, size) * GROUP + grp
    odd = lax.rem(wide, 2)
    return wide, grp, left, right, odd


def categories(nbr_elem):
    wide, grp, left, _, odd = places()
    owner = lax.shift_right_logical(nbr_elem, 7)
    beside = jnp.where(owner == left, 9 - odd, 8 + odd)
    cat = jnp.where(lax.shift_right_logical(owner, 3) == wide, owner & 7, beside)
    return jnp.where(owner == wide * GROUP + grp, LOCAL, cat)


def strict_upper():
    return onehot(iota((ELEM, ELEM), 0) < iota((ELEM, ELEM), 1))


def pack_kernel(
    elem_hbm, face_hbm, state_hbm, metric_hbm, troubled_hbm, owner_hbm, diff_hbm, weight_hbm,
    grp_hbm, pair0_ref, pair1_ref, trace_ref, pick_ref,
    elem_ref, face_ref, state_ref, metric_ref, troubled_ref, owner_ref, diff_ref, weight_ref,
    s_ref, grp_ref, sems,
):
    pairs = [(elem_hbm, elem_ref), (face_hbm, face_ref)]
    pairs += [(state_hbm.at[v], state_ref.at[v]) for v in range(VARS)]
    pairs += [(metric_hbm, metric_ref), (troubled_hbm, troubled_ref), (owner_hbm, owner_ref)]
    pairs += [(diff_hbm, diff_ref), (weight_hbm, weight_ref)]
    copies = [pltpu.make_async_copy(x, y, sems.at[k]) for k, (x, y) in enumerate(pairs)]
    for copy in copies:
        copy.start()
    copies[0].wait()
    copies[1].wait()
    elem = elem_ref[...]
    cat = categories(elem)
    partner = face_ref[...] * ELEM + (elem & (ELEM - 1)) + 1
    kinds = iota((16, ELEM), 0)
    hot = [jnp.where(cat[f : f + 1, :] == kinds, 1.0, 0.0) for f in range(FACES)]
    upper = jnp.concatenate([strict_upper(), jnp.ones((ELEM, ELEM), BF16)], axis=1)
    counts = dot_nn(jnp.concatenate(hot, axis=0).astype(BF16), upper)
    base = jnp.where(kinds < 9, 16 * kinds, PAIR1).astype(F32)
    pick = jnp.zeros((ROWS, ELEM), F32)
    rows = iota((ROWS, ELEM), 0)
    trace_ref[126:128, :] = jnp.zeros((2, FACES * ELEM), F32)
    for f in range(FACES):
        part = counts[16 * f : 16 * f + 16]
        pos = jnp.sum(hot[f] * (part[:, :ELEM] + base), axis=0, keepdims=True)
        base = base + part[:, ELEM:]
        pos = jnp.where(cat[f : f + 1, :] == LOCAL, -1, pos.astype(I32))
        chosen = jnp.where(rows == pos, 1.0, 0.0)
        pick = pick + chosen
        s_ref[:, f * ELEM : (f + 1) * ELEM] = chosen.astype(BF16)
        trace_ref[125:126, f * ELEM : (f + 1) * ELEM] = partner[f : f + 1, :].astype(F32)
    pick_ref[...] = pick.astype(BF16)
    for v in range(VARS):
        copies[2 + v].wait()
        for f in range(FACES):
            for first, count, stride, place in face_rows(f):
                trace_ref[25 * v + place : 25 * v + place + count, f * ELEM : (f + 1) * ELEM] = state_ref[
                    v, rows_at(first, count, stride), :
                ]
    pieces = thirds(trace_ref[...])
    grp_ref[...] = sum(dot_nt(s_ref[:GROUP_ROWS], x) for x in pieces)
    send = pltpu.make_async_copy(grp_ref, grp_hbm, sems.at[len(copies)])
    send.start()
    sent = sum(dot_nt(s_ref[GROUP_ROWS:], x) for x in pieces)
    pair0_ref[...] = sent[:WIDE_FACES]
    pair1_ref[...] = sent[WIDE_FACES:]
    for copy in copies[2 + VARS :]:
        copy.wait()
    send.wait()


def primitives(u):
    inv = 1.0 / u[0]
    vel = [u[1] * inv, u[2] * inv, u[3] * inv]
    kinetic = u[1] * vel[0] + u[2] * vel[1] + u[3] * vel[2]
    pressure = 0.4 * (u[4] - 0.5 * kinetic)
    return inv, vel, pressure


def flux(u, vel, pressure, a):
    w = vel[a]
    rows = [u[1 + a], u[1] * w, u[2] * w, u[3] * w, (u[4] + pressure) * w]
    rows[1 + a] = rows[1 + a] + pressure
    return rows


def speed(inv, vel, pressure, a):
    return jnp.abs(vel[a]) + jnp.sqrt(1.4 * pressure * inv)


def face_values(ref, f):
    return [ref[25 * v : 25 * v + 25, f * ELEM : (f + 1) * ELEM] for v in range(VARS)]


def add_face(ref, f, v, value):
    for first, count, stride, place in face_rows(f):
        at = rows_at(first, count, stride)
        ref[v, at, :] = ref[v, at, :] + value[place : place + count]


def local_kernel(
    elem_ref, face_ref, state_ref, metric_ref, trace_ref, diff_ref,
    base_ref, speed_ref, near_ref, f_ref, volume_ref,
):
    metric = metric_ref[...]
    u = [state_ref[v] for v in range(VARS)]
    inv, vel, pressure = primitives(u)
    for a in range(3):
        for v, row in enumerate(flux(u, vel, pressure, a)):
            f_ref[128 * a : 128 * a + NODES, v * ELEM : (v + 1) * ELEM] = row
        f_ref[128 * a + NODES : 128 * a + 128, :] = jnp.zeros((3, VARS * ELEM), F32)
    hi, mid = halves(f_ref[...])
    wide = dot_nn(diff_ref[...], hi)
    volume_ref[...] = wide[:128] + wide[128:] + dot_nn(diff_ref[0:128, :], mid)
    for v in range(VARS):
        base_ref[v] = state_ref[v]
    elem = elem_ref[...]
    _, grp, _, _, _ = places()
    own = lax.axis_index("wide") * GROUP + grp
    here = lax.shift_right_logical(elem, 7) == own
    local = elem & (ELEM - 1)
    side = face_ref[...]
    at = [jnp.where(here & (side == g), local, -1).astype(F32).astype(BF16) for g in range(FACES)]
    elems = iota((ELEM, 2 * ELEM), 0).astype(F32).astype(BF16)
    one, zero = jnp.ones((), BF16), jnp.zeros((), BF16)
    stacked = jnp.concatenate(halves(trace_ref[...]), axis=0)
    half = (0.5 * LIFT_GAIN * SECTION_STEP) * metric
    for pair in range(3):
        blocks = []
        for g in range(FACES):
            row = jnp.concatenate([at[g][2 * pair : 2 * pair + 1], at[g][2 * pair + 1 : 2 * pair + 2]], axis=1)
            blocks.append(jnp.where(elems == row, one, zero))
        got = dot_nn(stacked, jnp.concatenate(blocks, axis=0))
        near_ref[:, 2 * pair * ELEM : 2 * (pair + 1) * ELEM] = got[:128] + got[128:]
        for f in (2 * pair, 2 * pair + 1):
            scale = half if f % 2 else -half
            inner = face_values(trace_ref, f)
            inv, vel, pressure = primitives(inner)
            speed_ref[f] = speed(inv, vel, pressure, pair)
            for v, row in enumerate(flux(inner, vel, pressure, pair)):
                add_face(base_ref, f, v, scale * row)
    for v in range(VARS):
        base_ref[v] = base_ref[v] - (SECTION_STEP * metric) * volume_ref[:NODES, v * ELEM : (v + 1) * ELEM]


def section_kernel(
    grp_ref, pair0_ref, pair1_ref, base_ref, speed_ref, near_ref, trace_ref, pick_ref, metric_ref, weight_ref,
    send_hbm, send0_ref, send1_ref, sec_ref, donor_ref, mean_ref, came_ref, outer_ref, send_ref, sem,
):
    got = jnp.concatenate([grp_ref[...], pair0_ref[...], pair1_ref[...]], axis=0)
    slot = jnp.broadcast_to(got[:, NODES : NODES + 1], (ROWS, ELEM))
    lanes = iota((1, ELEM), 1).astype(F32) + 1.0
    stacked = jnp.concatenate(halves(got.T), axis=0)
    for pair in range(3):
        takes = [jnp.where(slot == lanes + float(f * ELEM), 1.0, 0.0) for f in (2 * pair, 2 * pair + 1)]
        far = dot_nn(stacked, jnp.concatenate(takes, axis=1).astype(BF16))
        cols = slice(2 * pair * ELEM, 2 * (pair + 1) * ELEM)
        outer_ref[:, cols] = near_ref[:, cols] + far[:128] + far[128:]
    came_ref[...] = slot
    half = (0.5 * LIFT_GAIN * SECTION_STEP) * metric_ref[...]
    sec_ref[...] = base_ref[...]
    for f in range(FACES):
        a = f // 2
        sign = 1.0 if f % 2 else -1.0
        inner = face_values(trace_ref, f)
        outer = face_values(outer_ref, f)
        inv, vel, pressure = primitives(outer)
        lam = half * jnp.maximum(speed_ref[f], speed(inv, vel, pressure, a))
        for v, row in enumerate(flux(outer, vel, pressure, a)):
            add_face(sec_ref, f, v, lam * (outer[v] - inner[v]) - (sign * half) * row)
    weight = weight_ref[...]
    for v in range(VARS):
        q = sec_ref[v]
        mean = jnp.sum(weight * q, axis=0, keepdims=True)
        dev = q - mean
        beta = 1e-06 + jnp.sum(weight * dev * dev, axis=0, keepdims=True)
        omega = 0.1 / (beta * beta)
        donor_ref[128 * v : 128 * v + NODES, :] = omega * dev
        donor_ref[128 * v + NODES : 128 * v + NODES + 1, :] = omega
        donor_ref[128 * v + NODES + 1 : 128 * v + 128, :] = jnp.zeros((2, ELEM), F32)
        mean_ref[v : v + 1, :] = mean
    pieces = thirds(donor_ref[...])
    send_ref[...] = sum(dot_nt(pick_ref[:GROUP_ROWS], x) for x in pieces)
    send = pltpu.make_async_copy(send_ref, send_hbm, sem.at[0])
    send.start()
    sent = sum(dot_nt(pick_ref[GROUP_ROWS:], x) for x in pieces)
    send0_ref[...] = sent[:WIDE_FACES]
    send1_ref[...] = sent[WIDE_FACES:]
    send.wait()


def inside_kernel(
    elem_ref, troubled_ref, owner_ref, came_ref, donor_ref, mean_ref, sec_ref,
    sum_ref, still_ref, far_ref, move_ref, cell_ref, wide_ref,
):
    _, grp, left, right, odd = places()
    own = lax.axis_index("wide") * GROUP + grp
    elem = elem_ref[...]
    troubled = jnp.sum(
        jnp.where(troubled_ref[...] == iota((ELEM, 48), 0), 1.0, 0.0), axis=1, keepdims=True
    )
    local = jnp.where(lax.shift_right_logical(elem, 7) == own, elem & (ELEM - 1), -1)
    elems = iota((ELEM, ELEM), 0)
    near = jnp.where(elems == iota((ELEM, ELEM), 1), 4.0, 0.0)
    for f in range(FACES):
        near = near + jnp.where(elems == local[f : f + 1, :], 1.0, 0.0)
    slot = came_ref[...].astype(I32) - 1
    came = jnp.where((slot & (ELEM - 1)) == jnp.where(slot < 0, -1, iota((ROWS, ELEM), 1)), 1.0, 0.0)
    far_ref[...] = jnp.concatenate([came, jnp.zeros((64, ELEM), F32)], axis=0).T[:, :ROWS].astype(BF16)
    sum_ref[...] = select_nt(near.T.astype(BF16), donor_ref[...])
    for v in range(VARS):
        wide_ref[0:NODES, :] = sec_ref[v]
        wide_ref[NODES:128, :] = jnp.zeros((3, ELEM), F32)
        value = wide_ref[...].T
        mean = jnp.broadcast_to(mean_ref[v : v + 1, :], (ELEM, ELEM)).T
        still_ref[:, 128 * v : 128 * v + 128] = jnp.where(troubled > 0.5, mean, value)
    owner = owner_ref[...]
    out0 = jnp.where(odd == 1, left, right)
    out1 = jnp.where(odd == 1, right, left)
    stays = jnp.where(owner == own, 1.0, 0.0)
    cell_ref[:, 0:128] = jnp.broadcast_to(troubled, (ELEM, ELEM))
    cell_ref[:, 128:256] = jnp.broadcast_to(stays, (ELEM, ELEM)).T
    go0 = jnp.where(owner == out0, 1.0, 0.0)
    go1 = jnp.where(owner == out1, 1.0, 0.0)
    go = jnp.concatenate([go0, go1, jnp.zeros((6, ELEM), F32)], axis=0)
    order = dot_nn(go.astype(BF16), strict_upper())
    place = jnp.where(go0 > 0.5, order[0:1, :], jnp.where(go1 > 0.5, MOVE_CAP + order[1:2, :], -1.0))
    move_ref[...] = onehot(iota((2 * MOVE_CAP, ELEM), 0) == place.astype(I32))


def limit_kernel(
    grp_ref, pair0_ref, pair1_ref, sum_ref, still_ref, far_ref, move_ref, cell_ref,
    limited_ref, go0_ref, go1_ref,
):
    got = jnp.concatenate([grp_ref[...], pair0_ref[...], pair1_ref[...]], axis=0)
    hi, mid = halves(got)
    far = far_ref[...]
    total = sum_ref[...] + (dot_nn(far, hi) + dot_nn(far, mid))
    troubled = cell_ref[:, 0:1] > 0.5
    for v in range(VARS):
        cols = slice(128 * v, 128 * v + 128)
        scale = jnp.where(troubled, 1.0 / total[:, 128 * v + NODES : 128 * v + NODES + 1], 0.0)
        limited_ref[:, cols] = still_ref[:, cols] + scale * total[:, cols]
    hi, mid, lo = thirds(limited_ref[...])
    move = move_ref[...]
    moved = dot_nn(move, hi) + dot_nn(move, mid) + dot_nn(move, lo)
    for v in range(VARS):
        go0_ref[v] = moved[:MOVE_CAP, 128 * v : 128 * v + NODES]
        go1_ref[v] = moved[MOVE_CAP:, 128 * v : 128 * v + NODES]


def keep_kernel(limited_ref, cell_ref, out_ref):
    stays = cell_ref[:, 128:256] > 0.5
    for v in range(VARS):
        out_ref[v] = jnp.where(stays, limited_ref[:, 128 * v : 128 * v + 128], 0.0)[:, :NODES]


def arrive_kernel(in0_ref, in1_ref, kept_ref, out_ref, sems):
    odd = lax.rem(lax.axis_index("wide"), 2)
    copies = []
    for k, (ref, place) in enumerate(((in0_ref, 1 - odd), (in1_ref, odd))):
        at = pl.ds(pl.multiple_of(ELEM + MOVE_CAP * place, 32), MOVE_CAP)
        copies.append(pltpu.make_async_copy(ref, out_ref.at[:, at, :], sems.at[k]))
    for copy in copies:
        copy.start()
    for copy in copies:
        copy.wait()


VMEM = pl.BlockSpec(memory_space=pltpu.VMEM)
PARAMS = pltpu.CompilerParams(vmem_limit_bytes=16 * 1024 * 1024)


def call(kernel, shapes, scratch, args, hbm=(), to_hbm=0):
    inputs = [pltpu.with_memory_space_constraint(arg, pltpu.VMEM) for arg in args]
    inputs += [pltpu.with_memory_space_constraint(arg, pltpu.HBM) for arg in hbm]
    spaces = [pltpu.HBM] * to_hbm + [pltpu.VMEM] * (len(shapes) - to_hbm)
    return pl.pallas_call(
        kernel,
        out_shape=[space(shape, dtype) for space, (shape, dtype) in zip(spaces, shapes)],
        in_specs=[VMEM] * len(args) + [pl.BlockSpec(memory_space=pltpu.HBM)] * len(hbm),
        out_specs=[pl.BlockSpec(memory_space=space) for space in spaces],
        scratch_shapes=scratch,
        compiler_params=PARAMS,
        interpret=INTERPRET,
    )(*inputs)


def swap(pair0, pair1):
    size = lax.axis_size("wide")
    first = [(i, i ^ 1) for i in range(size)]
    second = [(i, (i + 1) % size if i % 2 else (i - 1) % size) for i in range(size)]
    got1 = lax.ppermute(pair1, "wide", second)
    got0 = lax.ppermute(pair0, "wide", first)
    return got0, got1


def exchange(blocks, pair0, pair1):
    lanes = blocks.shape[1]
    got = lax.all_to_all(blocks.reshape(GROUP, GROUP_FACES, lanes), "grp", 0, 0)
    return (got.reshape(GROUP_ROWS, lanes), *swap(pair0, pair1))


def shards(state, metric, nbr_elem, nbr_face, troubled, new_owner):
    diffs, weights = gll_tables()
    diff = np.zeros((128, 384), np.float32)
    for a in range(3):
        diff[:NODES, 128 * a : 128 * a + NODES] = diffs[a]
    diff = jnp.asarray(np.concatenate(halves_of(diff), axis=0))
    weight = jnp.asarray(np.repeat(weights[:, None], ELEM, axis=1), F32)
    metric = metric.reshape(1, ELEM)
    troubled = troubled.reshape(1, 48)
    new_owner = new_owner.reshape(1, ELEM)
    cols = VARS * 128
    slots = FACES * ELEM
    dma = pltpu.SemaphoreType.DMA

    loaded = (nbr_elem, nbr_face, state, metric, troubled, new_owner, diff, weight)
    blocks, pair0, pair1, trace, pick, nbr_elem, nbr_face, state, metric, troubled, new_owner, diff, weight = call(
        pack_kernel,
        [((GROUP_ROWS, 128), F32), ((32, 128), F32), ((32, 128), F32), ((128, slots), F32), ((ROWS, ELEM), BF16)]
        + [(x.shape, x.dtype) for x in loaded],
        [pltpu.VMEM((ROWS, slots), BF16), pltpu.VMEM((GROUP_ROWS, 128), F32), dma((8 + VARS,))],
        (), loaded, 1,
    )
    got, got0, got1 = exchange(blocks, pair0, pair1)
    base, speeds, near = call(
        local_kernel,
        [((VARS, NODES, ELEM), F32), ((FACES, 25, ELEM), F32), ((128, slots), F32)],
        [pltpu.VMEM((384, cols), F32), pltpu.VMEM((128, cols), F32)],
        (nbr_elem, nbr_face, state, metric, trace, diff),
    )
    blocks, pair0, pair1, sec, donor, mean, came = call(
        section_kernel,
        [((GROUP_ROWS, cols), F32), ((32, cols), F32), ((32, cols), F32), ((VARS, NODES, ELEM), F32),
         ((cols, ELEM), F32), ((8, ELEM), F32), ((ROWS, ELEM), F32)],
        [pltpu.VMEM((128, slots), F32), pltpu.VMEM((GROUP_ROWS, cols), F32), dma((1,))],
        (got, got0, got1, base, speeds, near, trace, pick, metric, weight), (), 1,
    )
    got, got0, got1 = exchange(blocks, pair0, pair1)
    total, still, far, move, cell = call(
        inside_kernel,
        [((ELEM, cols), F32), ((ELEM, cols), F32), ((ELEM, ROWS), BF16), ((2 * MOVE_CAP, ELEM), BF16), ((ELEM, 256), F32)],
        [pltpu.VMEM((128, ELEM), F32)],
        (nbr_elem, troubled, new_owner, came, donor, mean, sec),
    )
    limited, go0, go1 = call(
        limit_kernel,
        [((ELEM, cols), F32), ((VARS, MOVE_CAP, NODES), F32), ((VARS, MOVE_CAP, NODES), F32)],
        [],
        (got, got0, got1, total, still, far, move, cell),
    )
    in0, in1 = swap(go0, go1)
    out_shape = jax.ShapeDtypeStruct((VARS, ELEM + 2 * MOVE_CAP, NODES), F32)
    vmem = lambda x: pltpu.with_memory_space_constraint(x, pltpu.VMEM)
    kept = pl.pallas_call(
        keep_kernel,
        out_shape=out_shape,
        grid=(1,),
        in_specs=[VMEM, VMEM],
        out_specs=pl.BlockSpec((VARS, ELEM, NODES), lambda i: (0, 0, 0)),
        compiler_params=PARAMS,
        interpret=INTERPRET,
    )(vmem(limited), vmem(cell))
    moved = pl.pallas_call(
        arrive_kernel,
        out_shape=out_shape,
        in_specs=[VMEM, VMEM, pl.BlockSpec(memory_space=pl.ANY)],
        out_specs=pl.BlockSpec(memory_space=pl.ANY),
        input_output_aliases={2: 0},
        scratch_shapes=[dma((2,))],
        compiler_params=PARAMS,
        interpret=INTERPRET,
    )(vmem(in0), vmem(in1), kept)
    return jnp.transpose(moved, (0, 2, 1))


def solution(mesh):
    placed = (
        P(None, None, ("wide", "grp")),
        P(("wide", "grp")),
        P(None, ("wide", "grp")),
        P(None, ("wide", "grp")),
        P(("wide", "grp")),
        P(("wide", "grp")),
    )
    return jax.shard_map(
        shards,
        mesh=mesh,
        in_specs=placed,
        out_specs=P(None, None, ("wide", "grp")),
        check_vma=False,
    )
```

time: 66.5 us -> 63.1 us (0.949)
  starting transfers between devices: 46.1 us -> 50.2 us
  local copies, waits for them, and re-layouts: 3.88 us -> 0 us
  waiting for transfers between devices: 7.84 us -> 4.58 us
    ppermute x6, starting transfers between devices: 26 us -> 30.3 us  [the longest x3 24.5 us: swap(): got1 = lax.ppermute(pair1, 'wide', second)]
    unnamed x20 -> x0, local copies, waits for them, and re-layouts: 3.88 us -> none
    ppermute x6, waiting for transfers between devices: 7.84 us -> 4.57 us  [the longest x3 4.56 us: swap(): got1 = lax.ppermute(pair1, 'wide', second)]
  transfers between devices with their start and end apart: 8 -> 8, of which waited for: 2 -> 3; matrix products, arithmetic and copies ran while one was open for 0% -> 0% of each run, Pallas kernels for 5% -> 3%
where the time goes in v4:
time: 63.1 us; the launch traced here: 62.6 us
  starting transfers between devices  50.2 us (80%)
  Pallas kernels  7.79 us (12%)
  waiting for transfers between devices  4.58 us (7%)
    ppermute x3, starting transfers between devices, swap(): got1 = lax.ppermute(pair1, 'wide', second)  24.5 us
    all_to_all x2, starting transfers between devices, exchange(): got = lax.all_to_all(blocks.reshape(GROUP, GROUP_FACES, lanes), 'grp', 0, 0)  19.9 us
    pallas_call x5, Pallas kernels, call(): pl.pallas_call(kernel, out_shape=[space(shape, dtype) for space, (shape,...  6.35 us
    ppermute x3, starting transfers between devices, swap(): got0 = lax.ppermute(pair0, 'wide', first)  5.74 us
    ppermute x3, waiting for transfers between devices, swap(): got1 = lax.ppermute(pair1, 'wide', second)  4.56 us
  transfers between devices with their start and end apart: 8, of which 3 were waited for; matrix products, arithmetic and copies ran while one was open for 0% of the time, Pallas kernels for 3%

profile of v4, /device:TPU:8, one launch (start us, length us, event | category | flops | bytes accessed | tf_op | source)
XLA Modules:
  0.0 62.6 jit_solution(12983318045682557805)
XLA Ops:
  0.0 2.3 %shard_map.82 = (f32[128,128]{1,0:T(8,128)}, f32[32,128]{1,0:T(8,128)S(1)}, f32[32,128]{1,0:T(8,128)S(1)}, f32[128,768]{1,0:T(8,128)S(1)}, bf16[192,128]{1,0:T(8...) custom-call(s32[6,128]{1,0:T(8,128)} %elem_hbm.1, ...), custom_call_target="tpu_custom_call" | custom-call | tf_op jit(solution)/shard_map/pallas_call | solution.py:391
  2.3 12.7 %all-to-all-start = ((f32[8,16,128]{2,1,0:T(8,128)}), f32[8,16,128]{2,1,0:T(8,128)S(1)}, u32[]{:S(2)}, u32[]{:S(2)}) async-start(f32[8,16,128]{2,1,0:T(8,128)} %bitcast.11), calls=%async_computation | async-start | bytes 131072 | tf_op jit(solution)/shard_map/all_to_all | solution.py:413
  15.0 1.9 %collective-permute-start = (f32[32,128]{1,0:T(8,128)S(1)}, f32[32,128]{1,0:T(8,128)S(1)}, u32[]{:S(2)}, u32[]{:S(2)}) collective-permute-start(f32[32,128]{1,0:T(8,128)S(1)} %get-tuple-element.37), channel_id=1, source_target_pairs={{0,8},{8,0},{16,24},{24,16},{32,40},{40,32},{48,56},{56,48},{64,72... | collective-permute-start | bytes 49160 | tf_op jit(solution)/shard_map/ppermute | solution.py:407
  16.9 11.7 %collective-permute-start.1 = (f32[32,128]{1,0:T(8,128)S(1)}, f32[32,128]{1,0:T(8,128)S(1)}, u32[]{:S(2)}, u32[]{:S(2)}) collective-permute-start(f32[32,128]{1,0:T(8,128)S(1)} %get-tuple-element.38), channel_id=1, source_target_pairs={{0,760},{8,16},{16,8},{24,32},{32,24},{40,48},{48,40},{56,64},{64,... | collective-permute-start | bytes 49160 | tf_op jit(solution)/shard_map/ppermute | solution.py:406
  28.7 1.0 %shard_map.83 = (f32[5,125,128]{2,1,0:T(8,128)S(1)}, f32[6,25,128]{2,1,0:T(8,128)S(1)}, f32[128,768]{1,0:T(8,128)S(1)}) custom-call(s32[6,128]{1,0:T(8,128)S(1)} %get-tuple-element.39.elem_ref, s32[6,128]{1,0:T(8,128)S(1)} %get-tuple-element.40.face_ref, f32[5,125,128]{2,1,0:T(8,128)S(1)} %get-tuple-element.41.state_ref, ...), custom_call_target="tpu_custom_call" | custom-call | tf_op jit(solution)/shard_map/pallas_call | solution.py:391
  29.7 0.0 collective-permute-done.pair0_ref
  29.7 0.4 collective-permute-done.1.pair1_ref
  30.1 0.0 all-to-all-done
  30.1 2.0 %shard_map.84 = (f32[128,640]{1,0:T(8,128)}, f32[32,640]{1,0:T(8,128)S(1)}, f32[32,640]{1,0:T(8,128)S(1)}, f32[5,125,128]{2,1,0:T(8,128)S(1)}, f32[640,128]{1,0:...) custom-call(f32[128,128]{1,0:T(8,128)S(1)} %bitcast.9, f32[32,128]{1,0:T(8,128)S(1)} %collective-permute-done.pair0_ref, ...), custom_call_target="tpu_custom_call" | custom-call | tf_op jit(solution)/shard_map/pallas_call | solution.py:391
  32.1 7.2 %all-to-all-start.1 = ((f32[8,16,640]{2,1,0:T(8,128)}), f32[8,16,640]{2,1,0:T(8,128)S(1)}, u32[]{:S(2)}, u32[]{:S(2)}) async-start(f32[8,16,640]{2,1,0:T(8,128)} %bitcast.10), calls=%async_computation.1 | async-start | bytes 655360 | tf_op jit(solution)/shard_map/all_to_all | solution.py:413
  39.3 1.9 %collective-permute-start.2 = (f32[32,640]{1,0:T(8,128)S(1)}, f32[32,640]{1,0:T(8,128)S(1)}, u32[]{:S(2)}, u32[]{:S(2)}) collective-permute-start(f32[32,640]{1,0:T(8,128)S(1)} %get-tuple-element.51), channel_id=1, source_target_pairs={{0,8},{8,0},{16,24},{24,16},{32,40},{40,32},{48,56},{56,48},{64,72... | collective-permute-start | bytes 245768 | tf_op jit(solution)/shard_map/ppermute | solution.py:407
  41.2 6.4 %collective-permute-start.3 = (f32[32,640]{1,0:T(8,128)S(1)}, f32[32,640]{1,0:T(8,128)S(1)}, u32[]{:S(2)}, u32[]{:S(2)}) collective-permute-start(f32[32,640]{1,0:T(8,128)S(1)} %get-tuple-element.52), channel_id=1, source_target_pairs={{0,760},{8,16},{16,8},{24,32},{32,24},{40,48},{48,40},{56,64},{64,... | collective-permute-start | bytes 245768 | tf_op jit(solution)/shard_map/ppermute | solution.py:406
  47.6 0.4 shard_map.85
  48.0 0.0 collective-permute-done.2.pair0_ref
  48.0 2.3 %collective-permute-done.3.pair1_ref = f32[32,640]{1,0:T(8,128)S(1)} collective-permute-done((f32[32,640]{1,0:T(8,128)S(1)}, f32[32,640]{1,0:T(8,128)S(1)}, u32[]{:S(2)}, u32[]{:S(2)}) %collective-permute-start.3) | collective-permute-done | bytes 81952 | tf_op jit(solution)/shard_map/ppermute | solution.py:406
  50.3 0.0 all-to-all-done.1
  50.3 0.7 %shard_map.86 = (f32[128,640]{1,0:T(8,128)S(1)}, f32[5,32,125]{2,1,0:T(8,128)S(1)}, f32[5,32,125]{2,1,0:T(8,128)S(1)}) custom-call(f32[128,640]{1,0:T(8,128)S(1)} %bitcast.8, f32[32,640]{1,0:T(8,128)S(1)} %collective-permute-done.2.pair0_ref, f32[32,640]{1,0:T(8,128)S(1)} %collective-permute-done.3.pair1_ref, f32[128,640]{1,0:T(8,128)S(1)} %get-tuple-element.59.sum_ref, ...), custom_call_target="tpu_custom_call" | custom-call | tf_op jit(solution)/shard_map/pallas_call | solution.py:391
  51.0 1.9 %collective-permute-start.4 = (f32[5,32,125]{2,1,0:T(8,128)S(1)}, f32[5,32,125]{2,1,0:T(8,128)S(1)}, u32[]{:S(2)}, u32[]{:S(2)}) collective-permute-start(f32[5,32,125]{2,1,0:T(8,128)S(1)} %get-tuple-element.64), channel_id=1, source_target_pairs={{0,8},{8,0},{16,24},{24,16},{32,40},{40,32},{48,56},{56,48},{64,72... | collective-permute-start | bytes 240008 | tf_op jit(solution)/shard_map/ppermute | solution.py:407
  52.9 6.4 %collective-permute-start.5 = (f32[5,32,125]{2,1,0:T(8,128)S(1)}, f32[5,32,125]{2,1,0:T(8,128)S(1)}, u32[]{:S(2)}, u32[]{:S(2)}) collective-permute-start(f32[5,32,125]{2,1,0:T(8,128)S(1)} %get-tuple-element.65), channel_id=1, source_target_pairs={{0,760},{8,16},{16,8},{24,32},{32,24},{40,48},{48,40},{56,64},{64,... | collective-permute-start | bytes 240008 | tf_op jit(solution)/shard_map/ppermute | solution.py:406
  59.3 0.8 %shard_map.87.kept_ref = f32[5,192,125]{2,1,0:T(8,128)} custom-call(f32[128,640]{1,0:T(8,128)S(1)} %get-tuple-element.66.limited_ref, f32[128,256]{1,0:T(8,128)S(1)} %get-tuple-element.63.cell_ref), custom_call_target="tpu_custom_call" | custom-call | tf_op jit(solution)/shard_map/pallas_call | solution.py:469
  60.0 0.0 collective-permute-done.4.in0_ref
  60.0 1.9 %collective-permute-done.5.in1_ref = f32[5,32,125]{2,1,0:T(8,128)S(1)} collective-permute-done((f32[5,32,125]{2,1,0:T(8,128)S(1)}, f32[5,32,125]{2,1,0:T(8,128)S(1)}, u32[]{:S(2)}, u32[]{:S(2)}) %collective-permute-start.5) | collective-permute-done | bytes 80032 | tf_op jit(solution)/shard_map/ppermute | solution.py:406
  62.0 0.7 %shard_map.88 = f32[5,192,125]{2,1,0:T(8,128)} custom-call(f32[5,32,125]{2,1,0:T(8,128)S(1)} %collective-permute-done.4.in0_ref, f32[5,32,125]{2,1,0:T(8,128)S(1)} %collective-permute-done.5.in1_ref, f32[5,192,125]{2,1,0:T(8,128)} %shard_map.87.kept_ref), custom_call_target="tpu_custom_call", output_to_operand_aliasing={{}: (2, {})} | custom-call | tf_op jit(solution)/shard_map/pallas_call | solution.py:478
Async XLA Ops:
  2.3 27.8 %all-to-all-start = ((f32[8,16,128]{2,1,0:T(8,128)}), f32[8,16,128]{2,1,0:T(8,128)S(1)}, u32[]{:S(2)}, u32[]{:S(2)}) async-start(f32[8,16,128]{2,1,0:T(8,128)} %bitcast.11), calls=%async_computation | async-start | bytes 131072 | tf_op jit(solution)/shard_map/all_to_all | solution.py:413
  15.0 14.7 %collective-permute-start = (f32[32,128]{1,0:T(8,128)S(1)}, f32[32,128]{1,0:T(8,128)S(1)}, u32[]{:S(2)}, u32[]{:S(2)}) collective-permute-start(f32[32,128]{1,0:T(8,128)S(1)} %get-tuple-element.37), channel_id=1, source_target_pairs={{0,8},{8,0},{16,24},{24,16},{32,40},{40,32},{48,56},{56,48},{64,72... | collective-permute-start | bytes 49160 | tf_op jit(solution)/shard_map/ppermute | solution.py:407
  16.9 13.2 %collective-permute-start.1 = (f32[32,128]{1,0:T(8,128)S(1)}, f32[32,128]{1,0:T(8,128)S(1)}, u32[]{:S(2)}, u32[]{:S(2)}) collective-permute-start(f32[32,128]{1,0:T(8,128)S(1)} %get-tuple-element.38), channel_id=1, source_target_pairs={{0,760},{8,16},{16,8},{24,32},{32,24},{40,48},{48,40},{56,64},{64,... | collective-permute-start | bytes 49160 | tf_op jit(solution)/shard_map/ppermute | solution.py:406
  32.1 18.2 %all-to-all-start.1 = ((f32[8,16,640]{2,1,0:T(8,128)}), f32[8,16,640]{2,1,0:T(8,128)S(1)}, u32[]{:S(2)}, u32[]{:S(2)}) async-start(f32[8,16,640]{2,1,0:T(8,128)} %bitcast.10), calls=%async_computation.1 | async-start | bytes 655360 | tf_op jit(solution)/shard_map/all_to_all | solution.py:413
  39.3 8.7 %collective-permute-start.2 = (f32[32,640]{1,0:T(8,128)S(1)}, f32[32,640]{1,0:T(8,128)S(1)}, u32[]{:S(2)}, u32[]{:S(2)}) collective-permute-start(f32[32,640]{1,0:T(8,128)S(1)} %get-tuple-element.51), channel_id=1, source_target_pairs={{0,8},{8,0},{16,24},{24,16},{32,40},{40,32},{48,56},{56,48},{64,72... | collective-permute-start | bytes 245768 | tf_op jit(solution)/shard_map/ppermute | solution.py:407
  41.2 9.1 %collective-permute-start.3 = (f32[32,640]{1,0:T(8,128)S(1)}, f32[32,640]{1,0:T(8,128)S(1)}, u32[]{:S(2)}, u32[]{:S(2)}) collective-permute-start(f32[32,640]{1,0:T(8,128)S(1)} %get-tuple-element.52), channel_id=1, source_target_pairs={{0,760},{8,16},{16,8},{24,32},{32,24},{40,48},{48,40},{56,64},{64,... | collective-permute-start | bytes 245768 | tf_op jit(solution)/shard_map/ppermute | solution.py:406
  51.0 9.1 %collective-permute-start.4 = (f32[5,32,125]{2,1,0:T(8,128)S(1)}, f32[5,32,125]{2,1,0:T(8,128)S(1)}, u32[]{:S(2)}, u32[]{:S(2)}) collective-permute-start(f32[5,32,125]{2,1,0:T(8,128)S(1)} %get-tuple-element.64), channel_id=1, source_target_pairs={{0,8},{8,0},{16,24},{24,16},{32,40},{40,32},{48,56},{56,48},{64,72... | collective-permute-start | bytes 240008 | tf_op jit(solution)/shard_map/ppermute | solution.py:407
  52.9 9.1 %collective-permute-start.5 = (f32[5,32,125]{2,1,0:T(8,128)S(1)}, f32[5,32,125]{2,1,0:T(8,128)S(1)}, u32[]{:S(2)}, u32[]{:S(2)}) collective-permute-start(f32[5,32,125]{2,1,0:T(8,128)S(1)} %get-tuple-element.65), channel_id=1, source_target_pairs={{0,760},{8,16},{16,8},{24,32},{32,24},{40,48},{48,40},{56,64},{64,... | collective-permute-start | bytes 240008 | tf_op jit(solution)/shard_map/ppermute | solution.py:406

commit v5 on v4

--- a/solution.py
+++ b/solution.py
@@ -129,9 +129,9 @@
 
 def pack_kernel(
     elem_hbm, face_hbm, state_hbm, metric_hbm, troubled_hbm, owner_hbm, diff_hbm, weight_hbm,
-    grp_hbm, pair0_ref, pair1_ref, trace_ref, pick_ref,
-    elem_ref, face_ref, state_ref, metric_ref, troubled_ref, owner_ref, diff_ref, weight_ref,
-    s_ref, grp_ref, sems,
+    grp_hbm, pair0_ref, pair1_ref, trace_ref, pick_ref, base_ref,
+    elem_ref, face_ref, metric_ref, troubled_ref, owner_ref, weight_ref,
+    state_ref, diff_ref, s_ref, grp_ref, f_ref, sems,
 ):
     pairs = [(elem_hbm, elem_ref), (face_hbm, face_ref)]
     pairs += [(state_hbm.at[v], state_ref.at[v]) for v in range(VARS)]
@@ -170,15 +170,27 @@
                 trace_ref[25 * v + place : 25 * v + place + count, f * ELEM : (f + 1) * ELEM] = state_ref[
                     v, rows_at(first, count, stride), :
                 ]
-    pieces = thirds(trace_ref[...])
+    pieces = halves(trace_ref[...])
     grp_ref[...] = sum(dot_nt(s_ref[:GROUP_ROWS], x) for x in pieces)
     send = pltpu.make_async_copy(grp_ref, grp_hbm, sems.at[len(copies)])
     send.start()
     sent = sum(dot_nt(s_ref[GROUP_ROWS:], x) for x in pieces)
     pair0_ref[...] = sent[:WIDE_FACES]
     pair1_ref[...] = sent[WIDE_FACES:]
+    u = [state_ref[v] for v in range(VARS)]
+    _, vel, pressure = primitives(u)
+    for a in range(3):
+        for v, row in enumerate(flux(u, vel, pressure, a)):
+            f_ref[128 * a : 128 * a + NODES, v * ELEM : (v + 1) * ELEM] = row
+        f_ref[128 * a + NODES : 128 * a + 128, :] = jnp.zeros((3, VARS * ELEM), F32)
+    hi, mid = halves(f_ref[...])
     for copy in copies[2 + VARS :]:
         copy.wait()
+    wide = dot_nn(diff_ref[...], hi)
+    volume = wide[:128] + wide[128:] + dot_nn(diff_ref[0:128, :], mid)
+    step = SECTION_STEP * metric_ref[...]
+    for v in range(VARS):
+        base_ref[v] = state_ref[v] - step * volume[:NODES, v * ELEM : (v + 1) * ELEM]
     send.wait()
 
 
@@ -212,21 +224,12 @@
 
 
 def local_kernel(
-    elem_ref, face_ref, state_ref, metric_ref, trace_ref, diff_ref,
-    base_ref, speed_ref, near_ref, f_ref, volume_ref,
+    elem_ref, face_ref, start_ref, metric_ref, trace_ref,
+    base_ref, speed_ref, near_ref,
 ):
     metric = metric_ref[...]
-    u = [state_ref[v] for v in range(VARS)]
-    inv, vel, pressure = primitives(u)
-    for a in range(3):
-        for v, row in enumerate(flux(u, vel, pressure, a)):
-            f_ref[128 * a : 128 * a + NODES, v * ELEM : (v + 1) * ELEM] = row
-        f_ref[128 * a + NODES : 128 * a + 128, :] = jnp.zeros((3, VARS * ELEM), F32)
-    hi, mid = halves(f_ref[...])
-    wide = dot_nn(diff_ref[...], hi)
-    volume_ref[...] = wide[:128] + wide[128:] + dot_nn(diff_ref[0:128, :], mid)
-    for v in range(VARS):
-        base_ref[v] = state_ref[v]
+    for v in range(VARS):
+        base_ref[v] = start_ref[v]
     elem = elem_ref[...]
     _, grp, _, _, _ = places()
     own = lax.axis_index("wide") * GROUP + grp
@@ -252,8 +255,6 @@
             speed_ref[f] = speed(inv, vel, pressure, pair)
             for v, row in enumerate(flux(inner, vel, pressure, pair)):
                 add_face(base_ref, f, v, scale * row)
-    for v in range(VARS):
-        base_ref[v] = base_ref[v] - (SECTION_STEP * metric) * volume_ref[:NODES, v * ELEM : (v + 1) * ELEM]
 
 
 def section_kernel(
@@ -292,7 +293,7 @@
         donor_ref[128 * v + NODES : 128 * v + NODES + 1, :] = omega
         donor_ref[128 * v + NODES + 1 : 128 * v + 128, :] = jnp.zeros((2, ELEM), F32)
         mean_ref[v : v + 1, :] = mean
-    pieces = thirds(donor_ref[...])
+    pieces = halves(donor_ref[...])
     send_ref[...] = sum(dot_nt(pick_ref[:GROUP_ROWS], x) for x in pieces)
     send = pltpu.make_async_copy(send_ref, send_hbm, sem.at[0])
     send.start()
@@ -429,19 +430,23 @@
     dma = pltpu.SemaphoreType.DMA
 
     loaded = (nbr_elem, nbr_face, state, metric, troubled, new_owner, diff, weight)
-    blocks, pair0, pair1, trace, pick, nbr_elem, nbr_face, state, metric, troubled, new_owner, diff, weight = call(
+    results = call(
         pack_kernel,
-        [((GROUP_ROWS, 128), F32), ((32, 128), F32), ((32, 128), F32), ((128, slots), F32), ((ROWS, ELEM), BF16)]
-        + [(x.shape, x.dtype) for x in loaded],
-        [pltpu.VMEM((ROWS, slots), BF16), pltpu.VMEM((GROUP_ROWS, 128), F32), dma((8 + VARS,))],
+        [((GROUP_ROWS, 128), F32), ((32, 128), F32), ((32, 128), F32), ((128, slots), F32), ((ROWS, ELEM), BF16),
+         ((VARS, NODES, ELEM), F32)]
+        + [(x.shape, x.dtype) for x in (nbr_elem, nbr_face, metric, troubled, new_owner, weight)],
+        [pltpu.VMEM(state.shape, F32), pltpu.VMEM(diff.shape, BF16), pltpu.VMEM((ROWS, slots), BF16),
+         pltpu.VMEM((GROUP_ROWS, 128), F32), pltpu.VMEM((384, cols), F32), dma((8 + VARS,))],
         (), loaded, 1,
     )
+    blocks, pair0, pair1, trace, pick, start = results[:6]
+    nbr_elem, nbr_face, metric, troubled, new_owner, weight = results[6:]
     got, got0, got1 = exchange(blocks, pair0, pair1)
     base, speeds, near = call(
         local_kernel,
         [((VARS, NODES, ELEM), F32), ((FACES, 25, ELEM), F32), ((128, slots), F32)],
-        [pltpu.VMEM((384, cols), F32), pltpu.VMEM((128, cols), F32)],
-        (nbr_elem, nbr_face, state, metric, trace, diff),
+        [],
+        (nbr_elem, nbr_face, start, metric, trace),
     )
     blocks, pair0, pair1, sec, donor, mean, came = call(
         section_kernel,

time: 63.1 us -> 63.1 us (level)
  no operation moved by 1% of the time
where the time goes in v5:
time: 63.1 us; the launch traced here: 62.7 us
  starting transfers between devices  50.2 us (80%)
  Pallas kernels  7.47 us (12%)
  waiting for transfers between devices  4.93 us (8%)
    ppermute x3, starting transfers between devices, swap(): got1 = lax.ppermute(pair1, 'wide', second)  24.5 us
    all_to_all x2, starting transfers between devices, exchange(): got = lax.all_to_all(blocks.reshape(GROUP, GROUP_FACES, lanes), 'grp', 0, 0)  19.9 us
    pallas_call x5, Pallas kernels, call(): pl.pallas_call(kernel, out_shape=[space(shape, dtype) for space, (shape,...  6.04 us
    ppermute x3, starting transfers between devices, swap(): got0 = lax.ppermute(pair0, 'wide', first)  5.74 us
    ppermute x3, waiting for transfers between devices, swap(): got1 = lax.ppermute(pair1, 'wide', second)  4.92 us
  transfers between devices with their start and end apart: 8, of which 3 were waited for; matrix products, arithmetic and copies ran while one was open for 0% of the time, Pallas kernels for 3%

profile of v5, /device:TPU:8, one launch (start us, length us, event | category | flops | bytes accessed | tf_op | source)
XLA Modules:
  0.0 62.7 jit_solution(12203508039640122371)
XLA Ops:
  0.0 2.5 %shard_map.82 = (f32[128,128]{1,0:T(8,128)}, f32[32,128]{1,0:T(8,128)S(1)}, f32[32,128]{1,0:T(8,128)S(1)}, f32[128,768]{1,0:T(8,128)S(1)}, bf16[192,128]{1,0:T(8...) custom-call(s32[6,128]{1,0:T(8,128)} %elem_hbm.1, ...), custom_call_target="tpu_custom_call" | custom-call | tf_op jit(solution)/shard_map/pallas_call | solution.py:392
  2.5 12.7 %all-to-all-start = ((f32[8,16,128]{2,1,0:T(8,128)}), f32[8,16,128]{2,1,0:T(8,128)S(1)}, u32[]{:S(2)}, u32[]{:S(2)}) async-start(f32[8,16,128]{2,1,0:T(8,128)} %bitcast.11), calls=%async_computation | async-start | bytes 131072 | tf_op jit(solution)/shard_map/all_to_all | solution.py:414
  15.2 1.9 %collective-permute-start = (f32[32,128]{1,0:T(8,128)S(1)}, f32[32,128]{1,0:T(8,128)S(1)}, u32[]{:S(2)}, u32[]{:S(2)}) collective-permute-start(f32[32,128]{1,0:T(8,128)S(1)} %get-tuple-element.36), channel_id=1, source_target_pairs={{0,8},{8,0},{16,24},{24,16},{32,40},{40,32},{48,56},{56,48},{64,72... | collective-permute-start | bytes 49160 | tf_op jit(solution)/shard_map/ppermute | solution.py:408
  17.1 11.7 %collective-permute-start.1 = (f32[32,128]{1,0:T(8,128)S(1)}, f32[32,128]{1,0:T(8,128)S(1)}, u32[]{:S(2)}, u32[]{:S(2)}) collective-permute-start(f32[32,128]{1,0:T(8,128)S(1)} %get-tuple-element.37), channel_id=1, source_target_pairs={{0,760},{8,16},{16,8},{24,32},{32,24},{40,48},{48,40},{56,64},{64,... | collective-permute-start | bytes 49160 | tf_op jit(solution)/shard_map/ppermute | solution.py:407
  28.8 0.7 %shard_map.83 = (f32[5,125,128]{2,1,0:T(8,128)S(1)}, f32[6,25,128]{2,1,0:T(8,128)S(1)}, f32[128,768]{1,0:T(8,128)S(1)}) custom-call(s32[6,128]{1,0:T(8,128)S(1)} %get-tuple-element.38.elem_ref, s32[6,128]{1,0:T(8,128)S(1)} %get-tuple-element.39.face_ref, f32[5,125,128]{2,1,0:T(8,128)S(1)} %get-tuple-element.40.start_ref, ...), custom_call_target="tpu_custom_call" | custom-call | tf_op jit(solution)/shard_map/pallas_call | solution.py:392
  29.5 0.0 collective-permute-done.pair0_ref
  29.5 0.7 %collective-permute-done.1.pair1_ref = f32[32,128]{1,0:T(8,128)S(1)} collective-permute-done((f32[32,128]{1,0:T(8,128)S(1)}, f32[32,128]{1,0:T(8,128)S(1)}, u32[]{:S(2)}, u32[]{:S(2)}) %collective-permute-start.1) | collective-permute-done | bytes 16416 | tf_op jit(solution)/shard_map/ppermute | solution.py:407
  30.3 0.0 all-to-all-done
  30.3 1.8 %shard_map.84 = (f32[128,640]{1,0:T(8,128)}, f32[32,640]{1,0:T(8,128)S(1)}, f32[32,640]{1,0:T(8,128)S(1)}, f32[5,125,128]{2,1,0:T(8,128)S(1)}, f32[640,128]{1,0:...) custom-call(f32[128,128]{1,0:T(8,128)S(1)} %bitcast.9, f32[32,128]{1,0:T(8,128)S(1)} %collective-permute-done.pair0_ref, ...), custom_call_target="tpu_custom_call" | custom-call | tf_op jit(solution)/shard_map/pallas_call | solution.py:392
  32.1 7.2 %all-to-all-start.1 = ((f32[8,16,640]{2,1,0:T(8,128)}), f32[8,16,640]{2,1,0:T(8,128)S(1)}, u32[]{:S(2)}, u32[]{:S(2)}) async-start(f32[8,16,640]{2,1,0:T(8,128)} %bitcast.10), calls=%async_computation.1 | async-start | bytes 655360 | tf_op jit(solution)/shard_map/all_to_all | solution.py:414
  39.3 1.9 %collective-permute-start.2 = (f32[32,640]{1,0:T(8,128)S(1)}, f32[32,640]{1,0:T(8,128)S(1)}, u32[]{:S(2)}, u32[]{:S(2)}) collective-permute-start(f32[32,640]{1,0:T(8,128)S(1)} %get-tuple-element.49), channel_id=1, source_target_pairs={{0,8},{8,0},{16,24},{24,16},{32,40},{40,32},{48,56},{56,48},{64,72... | collective-permute-start | bytes 245768 | tf_op jit(solution)/shard_map/ppermute | solution.py:408
  41.2 6.4 %collective-permute-start.3 = (f32[32,640]{1,0:T(8,128)S(1)}, f32[32,640]{1,0:T(8,128)S(1)}, u32[]{:S(2)}, u32[]{:S(2)}) collective-permute-start(f32[32,640]{1,0:T(8,128)S(1)} %get-tuple-element.50), channel_id=1, source_target_pairs={{0,760},{8,16},{16,8},{24,32},{32,24},{40,48},{48,40},{56,64},{64,... | collective-permute-start | bytes 245768 | tf_op jit(solution)/shard_map/ppermute | solution.py:407
  47.6 0.4 shard_map.85
  48.0 0.0 collective-permute-done.2.pair0_ref
  48.0 2.3 %collective-permute-done.3.pair1_ref = f32[32,640]{1,0:T(8,128)S(1)} collective-permute-done((f32[32,640]{1,0:T(8,128)S(1)}, f32[32,640]{1,0:T(8,128)S(1)}, u32[]{:S(2)}, u32[]{:S(2)}) %collective-permute-start.3) | collective-permute-done | bytes 81952 | tf_op jit(solution)/shard_map/ppermute | solution.py:407
  50.3 0.0 all-to-all-done.1
  50.3 0.7 %shard_map.86 = (f32[128,640]{1,0:T(8,128)S(1)}, f32[5,32,125]{2,1,0:T(8,128)S(1)}, f32[5,32,125]{2,1,0:T(8,128)S(1)}) custom-call(f32[128,640]{1,0:T(8,128)S(1)} %bitcast.8, f32[32,640]{1,0:T(8,128)S(1)} %collective-permute-done.2.pair0_ref, f32[32,640]{1,0:T(8,128)S(1)} %collective-permute-done.3.pair1_ref, f32[128,640]{1,0:T(8,128)S(1)} %get-tuple-element.57.sum_ref, ...), custom_call_target="tpu_custom_call" | custom-call | tf_op jit(solution)/shard_map/pallas_call | solution.py:392
  51.0 1.9 %collective-permute-start.4 = (f32[5,32,125]{2,1,0:T(8,128)S(1)}, f32[5,32,125]{2,1,0:T(8,128)S(1)}, u32[]{:S(2)}, u32[]{:S(2)}) collective-permute-start(f32[5,32,125]{2,1,0:T(8,128)S(1)} %get-tuple-element.62), channel_id=1, source_target_pairs={{0,8},{8,0},{16,24},{24,16},{32,40},{40,32},{48,56},{56,48},{64,72... | collective-permute-start | bytes 240008 | tf_op jit(solution)/shard_map/ppermute | solution.py:408
  52.9 6.4 %collective-permute-start.5 = (f32[5,32,125]{2,1,0:T(8,128)S(1)}, f32[5,32,125]{2,1,0:T(8,128)S(1)}, u32[]{:S(2)}, u32[]{:S(2)}) collective-permute-start(f32[5,32,125]{2,1,0:T(8,128)S(1)} %get-tuple-element.63), channel_id=1, source_target_pairs={{0,760},{8,16},{16,8},{24,32},{32,24},{40,48},{48,40},{56,64},{64,... | collective-permute-start | bytes 240008 | tf_op jit(solution)/shard_map/ppermute | solution.py:407
  59.3 0.8 %shard_map.87.kept_ref = f32[5,192,125]{2,1,0:T(8,128)} custom-call(f32[128,640]{1,0:T(8,128)S(1)} %get-tuple-element.64.limited_ref, f32[128,256]{1,0:T(8,128)S(1)} %get-tuple-element.61.cell_ref), custom_call_target="tpu_custom_call" | custom-call | tf_op jit(solution)/shard_map/pallas_call | solution.py:474
  60.1 0.0 collective-permute-done.4.in0_ref
  60.1 1.9 %collective-permute-done.5.in1_ref = f32[5,32,125]{2,1,0:T(8,128)S(1)} collective-permute-done((f32[5,32,125]{2,1,0:T(8,128)S(1)}, f32[5,32,125]{2,1,0:T(8,128)S(1)}, u32[]{:S(2)}, u32[]{:S(2)}) %collective-permute-start.5) | collective-permute-done | bytes 80032 | tf_op jit(solution)/shard_map/ppermute | solution.py:407
  62.0 0.7 %shard_map.88 = f32[5,192,125]{2,1,0:T(8,128)} custom-call(f32[5,32,125]{2,1,0:T(8,128)S(1)} %collective-permute-done.4.in0_ref, f32[5,32,125]{2,1,0:T(8,128)S(1)} %collective-permute-done.5.in1_ref, f32[5,192,125]{2,1,0:T(8,128)} %shard_map.87.kept_ref), custom_call_target="tpu_custom_call", output_to_operand_aliasing={{}: (2, {})} | custom-call | tf_op jit(solution)/shard_map/pallas_call | solution.py:483
Async XLA Ops:
  2.5 27.8 %all-to-all-start = ((f32[8,16,128]{2,1,0:T(8,128)}), f32[8,16,128]{2,1,0:T(8,128)S(1)}, u32[]{:S(2)}, u32[]{:S(2)}) async-start(f32[8,16,128]{2,1,0:T(8,128)} %bitcast.11), calls=%async_computation | async-start | bytes 131072 | tf_op jit(solution)/shard_map/all_to_all | solution.py:414
  15.2 14.4 %collective-permute-start = (f32[32,128]{1,0:T(8,128)S(1)}, f32[32,128]{1,0:T(8,128)S(1)}, u32[]{:S(2)}, u32[]{:S(2)}) collective-permute-start(f32[32,128]{1,0:T(8,128)S(1)} %get-tuple-element.36), channel_id=1, source_target_pairs={{0,8},{8,0},{16,24},{24,16},{32,40},{40,32},{48,56},{56,48},{64,72... | collective-permute-start | bytes 49160 | tf_op jit(solution)/shard_map/ppermute | solution.py:408
  17.1 13.2 %collective-permute-start.1 = (f32[32,128]{1,0:T(8,128)S(1)}, f32[32,128]{1,0:T(8,128)S(1)}, u32[]{:S(2)}, u32[]{:S(2)}) collective-permute-start(f32[32,128]{1,0:T(8,128)S(1)} %get-tuple-element.37), channel_id=1, source_target_pairs={{0,760},{8,16},{16,8},{24,32},{32,24},{40,48},{48,40},{56,64},{64,... | collective-permute-start | bytes 49160 | tf_op jit(solution)/shard_map/ppermute | solution.py:407
  32.1 18.2 %all-to-all-start.1 = ((f32[8,16,640]{2,1,0:T(8,128)}), f32[8,16,640]{2,1,0:T(8,128)S(1)}, u32[]{:S(2)}, u32[]{:S(2)}) async-start(f32[8,16,640]{2,1,0:T(8,128)} %bitcast.10), calls=%async_computation.1 | async-start | bytes 655360 | tf_op jit(solution)/shard_map/all_to_all | solution.py:414
  39.3 8.7 %collective-permute-start.2 = (f32[32,640]{1,0:T(8,128)S(1)}, f32[32,640]{1,0:T(8,128)S(1)}, u32[]{:S(2)}, u32[]{:S(2)}) collective-permute-start(f32[32,640]{1,0:T(8,128)S(1)} %get-tuple-element.49), channel_id=1, source_target_pairs={{0,8},{8,0},{16,24},{24,16},{32,40},{40,32},{48,56},{56,48},{64,72... | collective-permute-start | bytes 245768 | tf_op jit(solution)/shard_map/ppermute | solution.py:408
  41.2 9.1 %collective-permute-start.3 = (f32[32,640]{1,0:T(8,128)S(1)}, f32[32,640]{1,0:T(8,128)S(1)}, u32[]{:S(2)}, u32[]{:S(2)}) collective-permute-start(f32[32,640]{1,0:T(8,128)S(1)} %get-tuple-element.50), channel_id=1, source_target_pairs={{0,760},{8,16},{16,8},{24,32},{32,24},{40,48},{48,40},{56,64},{64,... | collective-permute-start | bytes 245768 | tf_op jit(solution)/shard_map/ppermute | solution.py:407
  51.0 9.1 %collective-permute-start.4 = (f32[5,32,125]{2,1,0:T(8,128)S(1)}, f32[5,32,125]{2,1,0:T(8,128)S(1)}, u32[]{:S(2)}, u32[]{:S(2)}) collective-permute-start(f32[5,32,125]{2,1,0:T(8,128)S(1)} %get-tuple-element.62), channel_id=1, source_target_pairs={{0,8},{8,0},{16,24},{24,16},{32,40},{40,32},{48,56},{56,48},{64,72... | collective-permute-start | bytes 240008 | tf_op jit(solution)/shard_map/ppermute | solution.py:408
  52.9 9.1 %collective-permute-start.5 = (f32[5,32,125]{2,1,0:T(8,128)S(1)}, f32[5,32,125]{2,1,0:T(8,128)S(1)}, u32[]{:S(2)}, u32[]{:S(2)}) collective-permute-start(f32[5,32,125]{2,1,0:T(8,128)S(1)} %get-tuple-element.63), channel_id=1, source_target_pairs={{0,760},{8,16},{16,8},{24,32},{32,24},{40,48},{48,40},{56,64},{64,... | collective-permute-start | bytes 240008 | tf_op jit(solution)/shard_map/ppermute | solution.py:407

commit v6 on v5

--- a/solution.py
+++ b/solution.py
@@ -24,6 +24,9 @@
 PAIR1 = GROUP_ROWS + WIDE_FACES
 ROWS = GROUP_ROWS + 2 * WIDE_FACES
 LOCAL = 10
+HALF = GROUP_ROWS // 2
+TURN_A = False
+TURN_B = True
 
 F32 = jnp.float32
 BF16 = jnp.bfloat16
@@ -95,6 +98,10 @@
 def select_nt(onehot, values):
     hi, mid, lo = thirds(values)
     return dot_nt(onehot, hi) + dot_nt(onehot, mid) + dot_nt(onehot, lo)
+
+
+def turned(rows, turn):
+    return jnp.concatenate([rows[HALF:], rows[:HALF]], axis=0) if turn else rows
 
 
 def iota(shape, dim):
@@ -171,7 +178,7 @@
                     v, rows_at(first, count, stride), :
                 ]
     pieces = halves(trace_ref[...])
-    grp_ref[...] = sum(dot_nt(s_ref[:GROUP_ROWS], x) for x in pieces)
+    grp_ref[...] = turned(sum(dot_nt(s_ref[:GROUP_ROWS], x) for x in pieces), TURN_A)
     send = pltpu.make_async_copy(grp_ref, grp_hbm, sems.at[len(copies)])
     send.start()
     sent = sum(dot_nt(s_ref[GROUP_ROWS:], x) for x in pieces)
@@ -261,7 +268,7 @@
     grp_ref, pair0_ref, pair1_ref, base_ref, speed_ref, near_ref, trace_ref, pick_ref, metric_ref, weight_ref,
     send_hbm, send0_ref, send1_ref, sec_ref, donor_ref, mean_ref, came_ref, outer_ref, send_ref, sem,
 ):
-    got = jnp.concatenate([grp_ref[...], pair0_ref[...], pair1_ref[...]], axis=0)
+    got = jnp.concatenate([turned(grp_ref[...], TURN_A), pair0_ref[...], pair1_ref[...]], axis=0)
     slot = jnp.broadcast_to(got[:, NODES : NODES + 1], (ROWS, ELEM))
     lanes = iota((1, ELEM), 1).astype(F32) + 1.0
     stacked = jnp.concatenate(halves(got.T), axis=0)
@@ -294,7 +301,7 @@
         donor_ref[128 * v + NODES + 1 : 128 * v + 128, :] = jnp.zeros((2, ELEM), F32)
         mean_ref[v : v + 1, :] = mean
     pieces = halves(donor_ref[...])
-    send_ref[...] = sum(dot_nt(pick_ref[:GROUP_ROWS], x) for x in pieces)
+    send_ref[...] = turned(sum(dot_nt(pick_ref[:GROUP_ROWS], x) for x in pieces), TURN_B)
     send = pltpu.make_async_copy(send_ref, send_hbm, sem.at[0])
     send.start()
     sent = sum(dot_nt(pick_ref[GROUP_ROWS:], x) for x in pieces)
@@ -346,7 +353,7 @@
     grp_ref, pair0_ref, pair1_ref, sum_ref, still_ref, far_ref, move_ref, cell_ref,
     limited_ref, go0_ref, go1_ref,
 ):
-    got = jnp.concatenate([grp_ref[...], pair0_ref[...], pair1_ref[...]], axis=0)
+    got = jnp.concatenate([turned(grp_ref[...], TURN_B), pair0_ref[...], pair1_ref[...]], axis=0)
     hi, mid = halves(got)
     far = far_ref[...]
     total = sum_ref[...] + (dot_nn(far, hi) + dot_nn(far, mid))
@@ -409,9 +416,12 @@
     return got0, got1
 
 
-def exchange(blocks, pair0, pair1):
+def exchange(blocks, pair0, pair1, turn):
+    order = [[4, 5, 6, 7, 0, 1, 2, 3]] if turn else None
     lanes = blocks.shape[1]
-    got = lax.all_to_all(blocks.reshape(GROUP, GROUP_FACES, lanes), "grp", 0, 0)
+    got = lax.all_to_all(
+        blocks.reshape(GROUP, GROUP_FACES, lanes), "grp", 0, 0, axis_index_groups=order
+    )
     return (got.reshape(GROUP_ROWS, lanes), *swap(pair0, pair1))
 
 
@@ -441,7 +451,7 @@
     )
     blocks, pair0, pair1, trace, pick, start = results[:6]
     nbr_elem, nbr_face, metric, troubled, new_owner, weight = results[6:]
-    got, got0, got1 = exchange(blocks, pair0, pair1)
+    got, got0, got1 = exchange(blocks, pair0, pair1, TURN_A)
     base, speeds, near = call(
         local_kernel,
         [((VARS, NODES, ELEM), F32), ((FACES, 25, ELEM), F32), ((128, slots), F32)],
@@ -455,7 +465,7 @@
         [pltpu.VMEM((128, slots), F32), pltpu.VMEM((GROUP_ROWS, cols), F32), dma((1,))],
         (got, got0, got1, base, speeds, near, trace, pick, metric, weight), (), 1,
     )
-    got, got0, got1 = exchange(blocks, pair0, pair1)
+    got, got0, got1 = exchange(blocks, pair0, pair1, TURN_B)
     total, still, far, move, cell = call(
         inside_kernel,
         [((ELEM, cols), F32), ((ELEM, cols), F32), ((ELEM, ROWS), BF16), ((2 * MOVE_CAP, ELEM), BF16), ((ELEM, 256), F32)],

time: 63.1 us -> 63.8 us (1.011)
  starting transfers between devices: 50.2 us -> 51.4 us
where the time goes in v6:
time: 63.8 us; the launch traced here: 63.3 us
  starting transfers between devices  51.4 us (81%)
  Pallas kernels  7.47 us (12%)
  waiting for transfers between devices  4.36 us (7%)
    ppermute x3, starting transfers between devices, swap(): got1 = lax.ppermute(pair1, 'wide', second)  25.1 us
    all_to_all x2, starting transfers between devices, exchange(): lax.all_to_all(blocks.reshape(GROUP, GROUP_FACES, lanes), 'grp', 0, 0, ax...  20.5 us
    pallas_call x5, Pallas kernels, call(): pl.pallas_call(kernel, out_shape=[space(shape, dtype) for space, (shape,...  6.03 us
    ppermute x3, starting transfers between devices, swap(): got0 = lax.ppermute(pair0, 'wide', first)  5.74 us
    ppermute x3, waiting for transfers between devices, swap(): got1 = lax.ppermute(pair1, 'wide', second)  4.35 us
  transfers between devices with their start and end apart: 8, of which 3 were waited for; matrix products, arithmetic and copies ran while one was open for 0% of the time, Pallas kernels for 3%

profile of v6, /device:TPU:8, one launch (start us, length us, event | category | flops | bytes accessed | tf_op | source)
XLA Modules:
  0.0 63.3 jit_solution(5234947701482932440)
XLA Ops:
  0.0 2.5 %shard_map.82 = (f32[128,128]{1,0:T(8,128)}, f32[32,128]{1,0:T(8,128)S(1)}, f32[32,128]{1,0:T(8,128)S(1)}, f32[128,768]{1,0:T(8,128)S(1)}, bf16[192,128]{1,0:T(8...) custom-call(s32[6,128]{1,0:T(8,128)} %elem_hbm.1, ...), custom_call_target="tpu_custom_call" | custom-call | tf_op jit(solution)/shard_map/pallas_call | solution.py:399
  2.5 12.7 %all-to-all-start = ((f32[8,16,128]{2,1,0:T(8,128)}), f32[8,16,128]{2,1,0:T(8,128)S(1)}, u32[]{:S(2)}, u32[]{:S(2)}) async-start(f32[8,16,128]{2,1,0:T(8,128)} %bitcast.11), calls=%async_computation | async-start | bytes 131072 | tf_op jit(solution)/shard_map/all_to_all | solution.py:422
  15.2 1.9 %collective-permute-start = (f32[32,128]{1,0:T(8,128)S(1)}, f32[32,128]{1,0:T(8,128)S(1)}, u32[]{:S(2)}, u32[]{:S(2)}) collective-permute-start(f32[32,128]{1,0:T(8,128)S(1)} %get-tuple-element.36), channel_id=1, source_target_pairs={{0,8},{8,0},{16,24},{24,16},{32,40},{40,32},{48,56},{56,48},{64,72... | collective-permute-start | bytes 49160 | tf_op jit(solution)/shard_map/ppermute | solution.py:415
  17.1 11.7 %collective-permute-start.1 = (f32[32,128]{1,0:T(8,128)S(1)}, f32[32,128]{1,0:T(8,128)S(1)}, u32[]{:S(2)}, u32[]{:S(2)}) collective-permute-start(f32[32,128]{1,0:T(8,128)S(1)} %get-tuple-element.37), channel_id=1, source_target_pairs={{0,760},{8,16},{16,8},{24,32},{32,24},{40,48},{48,40},{56,64},{64,... | collective-permute-start | bytes 49160 | tf_op jit(solution)/shard_map/ppermute | solution.py:414
  28.8 0.7 %shard_map.83 = (f32[5,125,128]{2,1,0:T(8,128)S(1)}, f32[6,25,128]{2,1,0:T(8,128)S(1)}, f32[128,768]{1,0:T(8,128)S(1)}) custom-call(s32[6,128]{1,0:T(8,128)S(1)} %get-tuple-element.38.elem_ref, s32[6,128]{1,0:T(8,128)S(1)} %get-tuple-element.39.face_ref, f32[5,125,128]{2,1,0:T(8,128)S(1)} %get-tuple-element.40.start_ref, ...), custom_call_target="tpu_custom_call" | custom-call | tf_op jit(solution)/shard_map/pallas_call | solution.py:399
  29.5 0.0 collective-permute-done.pair0_ref
  29.5 0.7 %collective-permute-done.1.pair1_ref = f32[32,128]{1,0:T(8,128)S(1)} collective-permute-done((f32[32,128]{1,0:T(8,128)S(1)}, f32[32,128]{1,0:T(8,128)S(1)}, u32[]{:S(2)}, u32[]{:S(2)}) %collective-permute-start.1) | collective-permute-done | bytes 16416 | tf_op jit(solution)/shard_map/ppermute | solution.py:414
  30.3 0.0 all-to-all-done
  30.3 1.8 %shard_map.84 = (f32[128,640]{1,0:T(8,128)}, f32[32,640]{1,0:T(8,128)S(1)}, f32[32,640]{1,0:T(8,128)S(1)}, f32[5,125,128]{2,1,0:T(8,128)S(1)}, f32[640,128]{1,0:...) custom-call(f32[128,128]{1,0:T(8,128)S(1)} %bitcast.9, f32[32,128]{1,0:T(8,128)S(1)} %collective-permute-done.pair0_ref, ...), custom_call_target="tpu_custom_call" | custom-call | tf_op jit(solution)/shard_map/pallas_call | solution.py:399
  32.1 7.8 %all-to-all-start.1 = ((f32[8,16,640]{2,1,0:T(8,128)}), f32[8,16,640]{2,1,0:T(8,128)S(1)}, u32[]{:S(2)}, u32[]{:S(2)}) async-start(f32[8,16,640]{2,1,0:T(8,128)} %bitcast.10), calls=%async_computation.1 | async-start | bytes 655360 | tf_op jit(solution)/shard_map/all_to_all | solution.py:422
  39.9 1.9 %collective-permute-start.2 = (f32[32,640]{1,0:T(8,128)S(1)}, f32[32,640]{1,0:T(8,128)S(1)}, u32[]{:S(2)}, u32[]{:S(2)}) collective-permute-start(f32[32,640]{1,0:T(8,128)S(1)} %get-tuple-element.49), channel_id=1, source_target_pairs={{0,8},{8,0},{16,24},{24,16},{32,40},{40,32},{48,56},{56,48},{64,72... | collective-permute-start | bytes 245768 | tf_op jit(solution)/shard_map/ppermute | solution.py:415
  41.9 6.7 %collective-permute-start.3 = (f32[32,640]{1,0:T(8,128)S(1)}, f32[32,640]{1,0:T(8,128)S(1)}, u32[]{:S(2)}, u32[]{:S(2)}) collective-permute-start(f32[32,640]{1,0:T(8,128)S(1)} %get-tuple-element.50), channel_id=1, source_target_pairs={{0,760},{8,16},{16,8},{24,32},{32,24},{40,48},{48,40},{56,64},{64,... | collective-permute-start | bytes 245768 | tf_op jit(solution)/shard_map/ppermute | solution.py:414
  48.5 0.4 shard_map.85
  48.9 0.0 collective-permute-done.2.pair0_ref
  49.0 2.0 %collective-permute-done.3.pair1_ref = f32[32,640]{1,0:T(8,128)S(1)} collective-permute-done((f32[32,640]{1,0:T(8,128)S(1)}, f32[32,640]{1,0:T(8,128)S(1)}, u32[]{:S(2)}, u32[]{:S(2)}) %collective-permute-start.3) | collective-permute-done | bytes 81952 | tf_op jit(solution)/shard_map/ppermute | solution.py:414
  50.9 0.0 all-to-all-done.1
  50.9 0.7 %shard_map.86 = (f32[128,640]{1,0:T(8,128)S(1)}, f32[5,32,125]{2,1,0:T(8,128)S(1)}, f32[5,32,125]{2,1,0:T(8,128)S(1)}) custom-call(f32[128,640]{1,0:T(8,128)S(1)} %bitcast.8, f32[32,640]{1,0:T(8,128)S(1)} %collective-permute-done.2.pair0_ref, f32[32,640]{1,0:T(8,128)S(1)} %collective-permute-done.3.pair1_ref, f32[128,640]{1,0:T(8,128)S(1)} %get-tuple-element.57.sum_ref, ...), custom_call_target="tpu_custom_call" | custom-call | tf_op jit(solution)/shard_map/pallas_call | solution.py:399
  51.6 1.9 %collective-permute-start.4 = (f32[5,32,125]{2,1,0:T(8,128)S(1)}, f32[5,32,125]{2,1,0:T(8,128)S(1)}, u32[]{:S(2)}, u32[]{:S(2)}) collective-permute-start(f32[5,32,125]{2,1,0:T(8,128)S(1)} %get-tuple-element.62), channel_id=1, source_target_pairs={{0,8},{8,0},{16,24},{24,16},{32,40},{40,32},{48,56},{56,48},{64,72... | collective-permute-start | bytes 240008 | tf_op jit(solution)/shard_map/ppermute | solution.py:415
  53.5 6.7 %collective-permute-start.5 = (f32[5,32,125]{2,1,0:T(8,128)S(1)}, f32[5,32,125]{2,1,0:T(8,128)S(1)}, u32[]{:S(2)}, u32[]{:S(2)}) collective-permute-start(f32[5,32,125]{2,1,0:T(8,128)S(1)} %get-tuple-element.63), channel_id=1, source_target_pairs={{0,760},{8,16},{16,8},{24,32},{32,24},{40,48},{48,40},{56,64},{64,... | collective-permute-start | bytes 240008 | tf_op jit(solution)/shard_map/ppermute | solution.py:414
  60.2 0.8 %shard_map.87.kept_ref = f32[5,192,125]{2,1,0:T(8,128)} custom-call(f32[128,640]{1,0:T(8,128)S(1)} %get-tuple-element.64.limited_ref, f32[128,256]{1,0:T(8,128)S(1)} %get-tuple-element.61.cell_ref), custom_call_target="tpu_custom_call" | custom-call | tf_op jit(solution)/shard_map/pallas_call | solution.py:484
  61.0 0.0 collective-permute-done.4.in0_ref
  61.0 1.6 %collective-permute-done.5.in1_ref = f32[5,32,125]{2,1,0:T(8,128)S(1)} collective-permute-done((f32[5,32,125]{2,1,0:T(8,128)S(1)}, f32[5,32,125]{2,1,0:T(8,128)S(1)}, u32[]{:S(2)}, u32[]{:S(2)}) %collective-permute-start.5) | collective-permute-done | bytes 80032 | tf_op jit(solution)/shard_map/ppermute | solution.py:414
  62.6 0.7 %shard_map.88 = f32[5,192,125]{2,1,0:T(8,128)} custom-call(f32[5,32,125]{2,1,0:T(8,128)S(1)} %collective-permute-done.4.in0_ref, f32[5,32,125]{2,1,0:T(8,128)S(1)} %collective-permute-done.5.in1_ref, f32[5,192,125]{2,1,0:T(8,128)} %shard_map.87.kept_ref), custom_call_target="tpu_custom_call", output_to_operand_aliasing={{}: (2, {})} | custom-call | tf_op jit(solution)/shard_map/pallas_call | solution.py:493
Async XLA Ops:
  2.5 27.8 %all-to-all-start = ((f32[8,16,128]{2,1,0:T(8,128)}), f32[8,16,128]{2,1,0:T(8,128)S(1)}, u32[]{:S(2)}, u32[]{:S(2)}) async-start(f32[8,16,128]{2,1,0:T(8,128)} %bitcast.11), calls=%async_computation | async-start | bytes 131072 | tf_op jit(solution)/shard_map/all_to_all | solution.py:422
  15.2 14.4 %collective-permute-start = (f32[32,128]{1,0:T(8,128)S(1)}, f32[32,128]{1,0:T(8,128)S(1)}, u32[]{:S(2)}, u32[]{:S(2)}) collective-permute-start(f32[32,128]{1,0:T(8,128)S(1)} %get-tuple-element.36), channel_id=1, source_target_pairs={{0,8},{8,0},{16,24},{24,16},{32,40},{40,32},{48,56},{56,48},{64,72... | collective-permute-start | bytes 49160 | tf_op jit(solution)/shard_map/ppermute | solution.py:415
  17.1 13.2 %collective-permute-start.1 = (f32[32,128]{1,0:T(8,128)S(1)}, f32[32,128]{1,0:T(8,128)S(1)}, u32[]{:S(2)}, u32[]{:S(2)}) collective-permute-start(f32[32,128]{1,0:T(8,128)S(1)} %get-tuple-element.37), channel_id=1, source_target_pairs={{0,760},{8,16},{16,8},{24,32},{32,24},{40,48},{48,40},{56,64},{64,... | collective-permute-start | bytes 49160 | tf_op jit(solution)/shard_map/ppermute | solution.py:414
  32.1 18.8 %all-to-all-start.1 = ((f32[8,16,640]{2,1,0:T(8,128)}), f32[8,16,640]{2,1,0:T(8,128)S(1)}, u32[]{:S(2)}, u32[]{:S(2)}) async-start(f32[8,16,640]{2,1,0:T(8,128)} %bitcast.10), calls=%async_computation.1 | async-start | bytes 655360 | tf_op jit(solution)/shard_map/all_to_all | solution.py:422
  39.9 9.0 %collective-permute-start.2 = (f32[32,640]{1,0:T(8,128)S(1)}, f32[32,640]{1,0:T(8,128)S(1)}, u32[]{:S(2)}, u32[]{:S(2)}) collective-permute-start(f32[32,640]{1,0:T(8,128)S(1)} %get-tuple-element.49), channel_id=1, source_target_pairs={{0,8},{8,0},{16,24},{24,16},{32,40},{40,32},{48,56},{56,48},{64,72... | collective-permute-start | bytes 245768 | tf_op jit(solution)/shard_map/ppermute | solution.py:415
  41.9 9.1 %collective-permute-start.3 = (f32[32,640]{1,0:T(8,128)S(1)}, f32[32,640]{1,0:T(8,128)S(1)}, u32[]{:S(2)}, u32[]{:S(2)}) collective-permute-start(f32[32,640]{1,0:T(8,128)S(1)} %get-tuple-element.50), channel_id=1, source_target_pairs={{0,760},{8,16},{16,8},{24,32},{32,24},{40,48},{48,40},{56,64},{64,... | collective-permute-start | bytes 245768 | tf_op jit(solution)/shard_map/ppermute | solution.py:414
  51.6 9.4 %collective-permute-start.4 = (f32[5,32,125]{2,1,0:T(8,128)S(1)}, f32[5,32,125]{2,1,0:T(8,128)S(1)}, u32[]{:S(2)}, u32[]{:S(2)}) collective-permute-start(f32[5,32,125]{2,1,0:T(8,128)S(1)} %get-tuple-element.62), channel_id=1, source_target_pairs={{0,8},{8,0},{16,24},{24,16},{32,40},{40,32},{48,56},{56,48},{64,72... | collective-permute-start | bytes 240008 | tf_op jit(solution)/shard_map/ppermute | solution.py:415
  53.5 9.1 %collective-permute-start.5 = (f32[5,32,125]{2,1,0:T(8,128)S(1)}, f32[5,32,125]{2,1,0:T(8,128)S(1)}, u32[]{:S(2)}, u32[]{:S(2)}) collective-permute-start(f32[5,32,125]{2,1,0:T(8,128)S(1)} %get-tuple-element.63), channel_id=1, source_target_pairs={{0,760},{8,16},{16,8},{24,32},{32,24},{40,48},{48,40},{56,64},{64,... | collective-permute-start | bytes 240008 | tf_op jit(solution)/shard_map/ppermute | solution.py:414
